TPU v7x, 128 devices: a whole 4x4x4 slice. The times are simulated.
128 devices in a mesh: section: 4 (over x), vertex: 16 (over z, y), feat: 2 (over core).
Axes of the slice: x: 4, y: 4, z: 4, core: 2. Of those that a mesh axis runs over, the one named last changes fastest.
Arguments:
- features: bfloat16 [32768, 1024], P('vertex', 'feat'), may hold values from -6 to 6
- history: bfloat16 [4, 32768, 1024], P('section', 'vertex', 'feat'), may hold values from -6 to 6
- weights: bfloat16 [4, 1024, 1024], P('section', None, 'feat'), may hold values from -0.1875 to 0.1875
- tile_values: bfloat16 [3, 1024, 128, 128], P(None, 'vertex'), may hold values from -0.125 to 0.125
- tile_rows: int32 [3, 1024], P(None, 'vertex'), may hold values from 0 to 15, as said below
- tile_cols: int32 [3, 1024], P(None, 'vertex'), may hold values from 0 to 15
- tile_counts: int32 [3, 16], P(None, 'vertex'), may hold values from 1 to 64, as said below
- span_ids: int32 [3, 2048], P(None, 'vertex'), may hold values from 0 to 2047, as said below
Outputs:
- layer_out: bfloat16 [4, 3, 2048, 1024], P('section', None, 'vertex', 'feat')
- new_history: bfloat16 [4, 32768, 1024], P('section', 'vertex', 'feat')
Inputs may be any that keep to these rules, and one draw needn't show every extreme that they name: `tile_rows`: within one owner's list for one block the (row block, column block) pairs are distinct. `tile_counts`: in every block some owner has exactly 64 live tiles. `span_ids`: the 384 entries of one owner over all blocks are distinct.
All inputs are finite; a program needn't handle non-finite values.
Results may differ from a plain program's by a relative error of at most 0.018.
Values may be sent and summed in bfloat16 or wider, within the bound.
No kernel may reach another device: no remote copies, remote signals or barrier semaphores. Data moves between devices by JAX's collectives and lax.ppermute only.
A program may use at most 128 MiB of HBM per device.

v0:
```python
import math

import jax
import jax.numpy as jnp
from jax import lax
from jax.experimental import pallas as pl
from jax.experimental.pallas import tpu as pltpu
from jax.sharding import PartitionSpec as P

RESIDUAL_SHARE = 0.2
BETA_SCALE = 0.5
MIB = 1 << 20
ROW_CHUNK = 1024
KERNEL_VMEM = 58
IN_HBM = pl.BlockSpec(memory_space=pltpu.HBM)
IN_VMEM = pl.BlockSpec(memory_space=pltpu.VMEM)
IN_SMEM = pl.BlockSpec(memory_space=pltpu.SMEM)


def rotated(array, axis, by):
    devices = lax.axis_size(axis)
    return lax.ppermute(array, axis, [(i, (i + by) % devices) for i in range(devices)])


def after(array, earlier):
    return lax.optimization_barrier((array, earlier))[0]


def vmem_params(mib):
    return pltpu.CompilerParams(vmem_limit_bytes=mib * MIB)


def cost(flops, bytes_accessed):
    return pl.CostEstimate(flops=flops, transcendentals=0, bytes_accessed=bytes_accessed)


def rows_from(tiles_ref, slots_ref, span, first, count, col_blocks):
    lines = []
    for row in range(count):
        base = (first + row) * col_blocks
        lines.append(
            jnp.concatenate(
                [tiles_ref[span, slots_ref[span, base + col]] for col in range(col_blocks)], axis=1
            )
        )
    return jnp.concatenate(lines, axis=0)


def tile_copies(tiles_ref, held, sems):
    spans, slots = tiles_ref.shape[:2]
    return [
        pltpu.make_async_copy(
            tiles_ref.at[span], held.at[span, pl.ds(0, slots)], sems.at[span]
        )
        for span in range(spans)
    ]


def tile_scratch(tiles):
    spans, slots, side, _ = tiles.shape
    return [pltpu.VMEM((spans, slots + 1, side, side), jnp.bfloat16), pltpu.SemaphoreType.DMA((spans,))]


def first_partial(tiles, slots, hist_slices, feats, replaced, row_devices):
    spans, slot_count, side, _ = tiles.shape
    _, cols, width = hist_slices.shape
    col_blocks = cols // side
    row_blocks = slots.shape[1] // col_blocks
    step = ROW_CHUNK // side
    chunks = row_blocks // step

    def kernel(slots_ref, tiles_ref, hist_ref, feat_ref, mask_ref, out_ref, held, tile_sems, hist, hist_sem, table, sums, out_sems):
        hist_copy = pltpu.make_async_copy(hist_ref.at[0], hist, hist_sem)
        copies = tile_copies(tiles_ref, held, tile_sems)
        for copy in [hist_copy] + copies:
            copy.start()
        def sent(span, chunk):
            at = pl.ds(chunk * step, step)
            return pltpu.make_async_copy(
                sums.at[span, at], out_ref.at[at, span], out_sems.at[span, chunk]
            )

        hist_copy.wait()
        for span in range(spans):
            held[span, slot_count] = jnp.zeros((side, side), jnp.bfloat16)
            table[...] = jnp.where(mask_ref[span] > 0, feat_ref[...], hist[...])
            copies[span].wait()

            @pl.loop(0, chunks)
            def _(chunk):
                left = rows_from(held, slots_ref, span, chunk * step, step, col_blocks)
                part = jnp.dot(left, table[...], preferred_element_type=jnp.float32)
                sums[span, pl.ds(chunk * step, step)] = part.astype(jnp.bfloat16).reshape(
                    step, side, width
                )
                sent(span, chunk).start()

        for span in range(spans):
            for chunk in range(chunks):
                sent(span, chunk).wait()

    return pl.pallas_call(
        kernel,
        out_shape=jax.ShapeDtypeStruct((row_devices, spans, side, width), jnp.bfloat16),
        in_specs=[IN_SMEM, IN_HBM, IN_HBM, IN_VMEM, IN_VMEM],
        out_specs=IN_HBM,
        scratch_shapes=[
            *tile_scratch(tiles),
            pltpu.VMEM((cols, width), jnp.bfloat16),
            pltpu.SemaphoreType.DMA(()),
            pltpu.VMEM((cols, width), jnp.bfloat16),
            pltpu.VMEM((spans, row_devices, side, width), jnp.bfloat16),
            pltpu.SemaphoreType.DMA((spans, chunks)),
        ],
        compiler_params=vmem_params(KERNEL_VMEM),
        cost_estimate=cost(2 * spans * row_blocks * side * cols * width, 2 * tiles.size),
        name="first_partial",
    )(slots, tiles, hist_slices, feats, replaced)


def section_slices(array, parts):
    rows, cols = array.shape
    width = cols // parts
    step = rows // 4

    def kernel(in_ref, out_ref):
        for part in range(parts):
            out_ref[part] = in_ref[:, part * width : (part + 1) * width]

    return pl.pallas_call(
        kernel,
        out_shape=jax.ShapeDtypeStruct((parts, rows, width), array.dtype),
        grid=(rows // step,),
        in_specs=[pl.BlockSpec((step, cols), lambda i: (i, 0))],
        out_specs=pl.BlockSpec((parts, step, width), lambda i: (0, i, 0)),
        compiler_params=vmem_params(KERNEL_VMEM),
        cost_estimate=cost(0, 4 * rows * cols),
        name="section_slices",
    )(array)


def selection(ids, owned, width):
    spans, rows_local = ids.shape
    picks = spans * rows_local
    chunk = 512

    def kernel(ids_ref, select_ref, mask_ref):
        first = pl.program_id(0) * chunk
        vertex = first + lax.broadcasted_iota(jnp.int32, (chunk, picks), 0)
        hits = (vertex == ids_ref[...]).astype(jnp.float32)
        select_ref[...] = hits.astype(jnp.bfloat16)
        total = jnp.zeros((chunk, 1), jnp.float32)
        for span in range(spans):
            part = hits[:, span * rows_local : (span + 1) * rows_local]
            total = total + jnp.sum(part, axis=1, keepdims=True)
            mask_ref[span] = jnp.broadcast_to(total, (chunk, width)).astype(jnp.bfloat16)

    return pl.pallas_call(
        kernel,
        out_shape=(
            jax.ShapeDtypeStruct((owned, picks), jnp.bfloat16),
            jax.ShapeDtypeStruct((spans, owned, width), jnp.bfloat16),
        ),
        grid=(owned // chunk,),
        in_specs=[pl.BlockSpec((1, picks), lambda i: (0, 0))],
        out_specs=(
            pl.BlockSpec((chunk, picks), lambda i: (i, 0)),
            pl.BlockSpec((spans, chunk, width), lambda i: (0, i, 0)),
        ),
        compiler_params=vmem_params(16),
        cost_estimate=cost(owned * picks, 4 * owned * picks),
        name="selection",
    )(ids.reshape(1, picks))


def collect(arrived, initial):
    owners, spans, rows_local, width = arrived.shape

    groups = 4
    each = owners // groups

    def kernel(in_ref, init_ref, out_ref, held, sems, sums):
        copies = [
            pltpu.make_async_copy(
                in_ref.at[pl.ds(group * each, each)], held.at[pl.ds(group * each, each)], sems.at[group]
            )
            for group in range(groups)
        ]
        for copy in copies:
            copy.start()
        for group in range(groups):
            copies[group].wait()
            for span in range(spans):
                at = slice(span * rows_local, (span + 1) * rows_local)
                total = held[group * each, span].astype(jnp.float32)
                for owner in range(group * each + 1, (group + 1) * each):
                    total = total + held[owner, span].astype(jnp.float32)
                if group:
                    total = sums[at] + total
                if group < groups - 1:
                    sums[at] = total
                else:
                    out_ref[at] = (
                        (1.0 - RESIDUAL_SHARE) * total + RESIDUAL_SHARE * init_ref[at]
                    ).astype(jnp.bfloat16)

    return pl.pallas_call(
        kernel,
        out_shape=jax.ShapeDtypeStruct((spans * rows_local, width), jnp.bfloat16),
        in_specs=[IN_HBM, IN_VMEM],
        out_specs=IN_VMEM,
        scratch_shapes=[
            pltpu.VMEM(arrived.shape, jnp.bfloat16),
            pltpu.SemaphoreType.DMA((groups,)),
            pltpu.VMEM((spans * rows_local, width), jnp.float32),
        ],
        compiler_params=vmem_params(16),
        cost_estimate=cost(arrived.size, 2 * arrived.size),
        name="collect",
    )(arrived, initial)


def static_parts(tiles, slots, hist_slices, replaced, select, which):
    spans, slot_count, side, _ = tiles.shape
    layers, cols, width = hist_slices.shape
    col_blocks = cols // side
    row_blocks = slots.shape[1] // col_blocks
    rows = row_blocks * side
    with_columns = which[0] == 1
    rows_local = select.shape[1] // spans
    picks = select.shape[1] if with_columns else 0
    kinds = len(which)
    stored = kinds * width
    step = ROW_CHUNK // side
    chunks = row_blocks // step

    def kernel(slots_ref, tiles_ref, hist_ref, mask_ref, sel_ref, *refs):
        static_refs = refs[:kinds]
        column_refs = refs[kinds : kinds + (spans if with_columns else 0)]
        held, tile_sems, hist, hist_sems, right, sums, sums_sems, cols_held, cols_sems = refs[-9:]
        hist_copies = [
            pltpu.make_async_copy(hist_ref.at[layer], hist.at[index], hist_sems.at[index])
            for index, layer in enumerate(which)
        ]
        copies = tile_copies(tiles_ref, held, tile_sems)
        for copy in hist_copies + copies:
            copy.start()
        if with_columns:
            right[:, stored:] = sel_ref[...]
        for copy in hist_copies:
            copy.wait()
        def sent(span, chunk, used):
            at = pl.ds(pl.multiple_of(chunk * ROW_CHUNK, ROW_CHUNK), ROW_CHUNK)
            moves = [
                pltpu.make_async_copy(
                    sums.at[index, span, at],
                    static_refs[index].at[span, at],
                    sums_sems.at[index, span, chunk],
                )
                for index in range(kinds)
            ]
            if with_columns:
                moves.append(
                    pltpu.make_async_copy(
                        cols_held.at[span, at, pl.ds(0, used)],
                        column_refs[span].at[at],
                        cols_sems.at[span, chunk],
                    )
                )
            return moves

        for span in range(spans):
            held[span, slot_count] = jnp.zeros((side, side), jnp.bfloat16)
            for index in range(kinds):
                right[:, index * width : (index + 1) * width] = jnp.where(
                    mask_ref[span] > 0, jnp.zeros_like(hist[index]), hist[index]
                )
            used = (span + 1) * rows_local if with_columns else 0
            copies[span].wait()

            @pl.loop(0, chunks)
            def _(chunk):
                left = rows_from(held, slots_ref, span, chunk * step, step, col_blocks)
                part = jnp.dot(
                    left, right[:, : stored + used], preferred_element_type=jnp.float32
                )
                at = pl.ds(pl.multiple_of(chunk * ROW_CHUNK, ROW_CHUNK), ROW_CHUNK)
                for index in range(kinds):
                    sums[index, span, at] = part[:, index * width : (index + 1) * width]
                if with_columns:
                    cols_held[span, at, :used] = part[:, stored:].astype(jnp.bfloat16)
                for move in sent(span, chunk, used):
                    move.start()

        for span in range(spans):
            for chunk in range(chunks):
                for move in sent(span, chunk, (span + 1) * rows_local):
                    move.wait()

    out_shape = [jax.ShapeDtypeStruct((spans, rows, width), jnp.float32) for _ in which]
    if with_columns:
        out_shape += [
            jax.ShapeDtypeStruct((rows, (span + 1) * rows_local), jnp.bfloat16)
            for span in range(spans)
        ]
    return pl.pallas_call(
        kernel,
        out_shape=tuple(out_shape),
        in_specs=[IN_SMEM, IN_HBM, IN_HBM, IN_VMEM, IN_VMEM],
        out_specs=tuple([IN_HBM] * len(out_shape)),
        scratch_shapes=[
            *tile_scratch(tiles),
            pltpu.VMEM((kinds, cols, width), jnp.bfloat16),
            pltpu.SemaphoreType.DMA((kinds,)),
            pltpu.VMEM((cols, stored + picks), jnp.bfloat16),
            pltpu.VMEM((kinds, spans, rows, width), jnp.float32),
            pltpu.SemaphoreType.DMA((kinds, spans, chunks)),
            pltpu.VMEM((spans, rows, picks) if with_columns else (1, 16, 128), jnp.bfloat16),
            pltpu.SemaphoreType.DMA((spans, chunks)),
        ],
        compiler_params=vmem_params(KERNEL_VMEM),
        cost_estimate=cost(
            2 * spans * rows * cols * (stored + picks),
            2 * tiles.size + spans * (4 * rows * stored + 2 * rows * picks),
        ),
        name="static_parts",
    )(slots, tiles, hist_slices, replaced, select)


def fill_left(left, gath_ref, section, halves, parts, width):
    for half in range(halves):
        for part in range(parts):
            first = (half * parts + part) * width
            place = lax.rem(section - part + parts, parts)
            left[:, first : first + width] = gath_ref[half, place]


def layer_step(place, gathered, support, slices, static, columns, layer, beta, row_devices):
    halves, parts, picks, width = gathered.shape
    spans, rows, _ = static.shape
    rows_local = rows // row_devices
    depth = halves * parts * width
    step = ROW_CHUNK // rows_local
    chunks = row_devices // step

    def kernel(place_ref, gath_ref, sup_ref, static_ref, *refs):
        slice_refs, column_refs = refs[:parts], refs[parts : parts + spans]
        out_ref, left, left_sems, sup, sup_sem, right, right_sem, stat, stat_sems, cols_sems, sums, out_sems = refs[parts + spans : -spans]
        cols = refs[-spans:]
        section = place_ref[0]
        apart = lax.rem(section - layer + parts, parts)
        incoming = []
        for half in range(halves):
            for part in range(parts):
                first = (half * parts + part) * width
                incoming.append(
                    pltpu.make_async_copy(
                        gath_ref.at[half, lax.rem(section - part + parts, parts)],
                        left.at[:, first : first + width],
                        left_sems.at[half, part],
                    )
                )
        incoming.append(pltpu.make_async_copy(sup_ref, sup, sup_sem))
        for copy in incoming:
            copy.start()
        for by in range(parts):
            @pl.when(apart == by)
            def _():
                pltpu.make_async_copy(slice_refs[by], right, right_sem).start()

        later = []
        for span in range(spans):
            pair = (
                pltpu.make_async_copy(column_refs[span], cols[span], cols_sems.at[span]),
                pltpu.make_async_copy(static_ref.at[span], stat.at[span], stat_sems.at[span]),
            )
            for copy in pair:
                copy.start()
            later.append(pair)
        for copy in incoming:
            copy.wait()
        pltpu.make_async_copy(slice_refs[0], right, right_sem).wait()
        projected = jnp.dot(left[...], right[...], preferred_element_type=jnp.float32)
        fresh = jnp.maximum(
            (1.0 - beta) * sup[...].astype(jnp.float32) + beta * projected, 0.0
        ).astype(jnp.bfloat16)
        outgoing = []
        for span in range(spans):
            used = (span + 1) * rows_local
            for copy in later[span]:
                copy.wait()
            for chunk in range(chunks):
                first = chunk * step
                at = slice(chunk * ROW_CHUNK, (chunk + 1) * ROW_CHUNK)
                part = stat[span, at] + jnp.dot(
                    cols[span][at], fresh[:used], preferred_element_type=jnp.float32
                )
                sums[span, first : first + step] = part.astype(jnp.bfloat16).reshape(
                    step, rows_local, width
                )
                outgoing.append(
                    pltpu.make_async_copy(
                        sums.at[span, first : first + step],
                        out_ref.at[first : first + step, span],
                        out_sems.at[span, chunk],
                    )
                )
                outgoing[-1].start()
        for copy in outgoing:
            copy.wait()

    return pl.pallas_call(
        kernel,
        out_shape=jax.ShapeDtypeStruct((row_devices, spans, rows_local, width), jnp.bfloat16),
        in_specs=[IN_SMEM] + [IN_HBM] * (3 + parts + spans),
        out_specs=IN_HBM,
        scratch_shapes=[
            pltpu.VMEM((picks, depth), jnp.bfloat16),
            pltpu.SemaphoreType.DMA((halves, parts)),
            pltpu.VMEM((picks, width), jnp.bfloat16),
            pltpu.SemaphoreType.DMA(()),
            pltpu.VMEM((depth, width), jnp.bfloat16),
            pltpu.SemaphoreType.DMA(()),
            pltpu.VMEM(static.shape, jnp.float32),
            pltpu.SemaphoreType.DMA((spans,)),
            pltpu.SemaphoreType.DMA((spans,)),
            pltpu.VMEM((spans, row_devices, rows_local, width), jnp.bfloat16),
            pltpu.SemaphoreType.DMA((spans, chunks)),
            *[pltpu.VMEM(each.shape, jnp.bfloat16) for each in columns],
        ],
        compiler_params=vmem_params(KERNEL_VMEM),
        cost_estimate=cost(
            2 * picks * depth * width + 2 * spans * rows * width * picks,
            6 * spans * rows * width + 2 * spans * rows * picks,
        ),
        name="layer_step",
    )(place, gathered, support, static, *slices, *columns)


def whole_rows(place, betas, gathered, weight_cols, earlier, layer):
    halves, parts, picks, width = gathered.shape
    depth, half = weight_cols.shape

    def kernel(place_ref, betas_ref, gath_ref, w_ref, *refs):
        if layer:
            earlier_ref, out_ref, left, own = refs
        else:
            out_ref, left, own = refs
        section, feat = place_ref[0], place_ref[1]

        @pl.when(section == layer)
        def _():
            beta = betas_ref[layer]
            fill_left(left, gath_ref, section, halves, parts, width)
            for part in range(parts):
                own[:, part * width : (part + 1) * width] = gath_ref[
                    feat, lax.rem(section - part + parts, parts)
                ]
            projected = jnp.dot(left[...], w_ref[...], preferred_element_type=jnp.float32)
            out_ref[...] = jnp.maximum(
                (1.0 - beta) * own[...].astype(jnp.float32) + beta * projected, 0.0
            ).astype(jnp.bfloat16)

        @pl.when(section != layer)
        def _():
            out_ref[...] = earlier_ref[...] if layer else jnp.zeros_like(out_ref)

    operands = [gathered, weight_cols] + ([earlier] if layer else [])
    return pl.pallas_call(
        kernel,
        out_shape=jax.ShapeDtypeStruct((picks, half), jnp.bfloat16),
        in_specs=[pl.BlockSpec(memory_space=pltpu.SMEM)] * 2
        + [pl.BlockSpec(memory_space=pltpu.VMEM)] * len(operands),
        scratch_shapes=[
            pltpu.VMEM((picks, depth), jnp.bfloat16),
            pltpu.VMEM((picks, half), jnp.bfloat16),
        ],
        compiler_params=vmem_params(16),
        cost_estimate=cost(2 * picks * depth * half, 2 * (picks * depth + depth * half)),
        name="whole_rows",
    )(place, betas, *operands)


def replace_rows(stored, ids, fresh):
    owned, half = stored.shape
    picks = ids.shape[1]
    chunk = 512

    def kernel(stored_ref, ids_ref, fresh_ref, out_ref):
        first = pl.program_id(0) * chunk
        vertex = first + lax.broadcasted_iota(jnp.int32, (chunk, picks), 0)
        hits = (vertex == ids_ref[...]).astype(jnp.float32)
        placed = jnp.dot(
            hits.astype(jnp.bfloat16), fresh_ref[...], preferred_element_type=jnp.float32
        )
        found = jnp.sum(hits, axis=1, keepdims=True) > 0
        out_ref[...] = jnp.where(found, placed, stored_ref[...].astype(jnp.float32)).astype(
            jnp.bfloat16
        )

    return pl.pallas_call(
        kernel,
        out_shape=jax.ShapeDtypeStruct((owned, half), jnp.bfloat16),
        grid=(owned // chunk,),
        in_specs=[
            pl.BlockSpec((chunk, half), lambda i: (i, 0)),
            pl.BlockSpec((1, picks), lambda i: (0, 0)),
            pl.BlockSpec((picks, half), lambda i: (0, 0)),
        ],
        out_specs=pl.BlockSpec((chunk, half), lambda i: (i, 0)),
        compiler_params=vmem_params(24),
        cost_estimate=cost(2 * owned * picks * half, 4 * owned * half),
        name="replace_rows",
    )(stored, ids, fresh)


def shards(features, history, weights, tile_values, tile_rows, tile_cols, tile_counts, span_ids):
    spans, rows_local = span_ids.shape
    side = tile_values.shape[2]
    owned, half = features.shape
    layers = lax.axis_size("section")
    row_devices = lax.axis_size("vertex")
    section = lax.axis_index("section")
    width = half // layers
    picks = spans * rows_local
    depth = weights.shape[1]
    betas = [math.log(BETA_SCALE / (layer + 1) + 1.0) for layer in range(layers)]
    place = jnp.stack([section, lax.axis_index("feat")]).astype(jnp.int32)
    beta_table = jnp.array(betas, jnp.float32)

    stored = history[0]
    hist_slices = lax.all_to_all(section_slices(stored, layers), "section", 0, 0, tiled=True)

    select, replaced = selection(span_ids, owned, width)
    ids = span_ids.reshape(1, picks)
    feat_slice = lax.dynamic_slice_in_dim(features, section * width, width, 1)
    initial_half = jnp.take(features, ids[0], axis=0)
    initial = lax.dynamic_slice_in_dim(initial_half, section * width, width, 1).astype(jnp.float32)
    col_blocks = owned // side
    blocks = rows_local * row_devices // side * col_blocks
    slot_count = tile_rows.shape[1]
    listed = jnp.arange(slot_count)[None, :]
    key = jnp.where(listed < tile_counts, tile_rows * col_blocks + tile_cols, blocks)
    here = key[:, :, None] == jnp.arange(blocks)[None, None, :]
    slots = slot_count + jnp.sum(
        jnp.where(here, listed[:, :, None] - slot_count, 0), axis=1, dtype=jnp.int32
    )
    hist_slices, replaced, feat_slice, initial, slots, select = lax.optimization_barrier(
        (hist_slices, replaced, feat_slice, initial, slots, select)
    )
    partial = first_partial(tile_values, slots, hist_slices, feat_slice, replaced, row_devices)
    own_weights = after(weights[0], partial)
    statics_one, *columns = static_parts(
        tile_values, slots, after(hist_slices, partial), replaced, select, (1,)
    )
    statics = [statics_one]
    by_distance = [
        lax.dynamic_slice_in_dim(own_weights, (section + by) % layers * width, width, 1)
        for by in range(layers)
    ]
    weight_slices = [by_distance[0]] + [
        rotated(by_distance[by], "section", by) for by in range(1, layers)
    ]

    rows_kept = table = None
    for layer in range(layers):
        if layer == layers - 1:
            before = rotated(rows_kept, "section", 1)
            table = replace_rows(stored, ids, jnp.where(section == 0, initial_half, before))
        arrived = lax.all_to_all(partial, "vertex", 0, 0, tiled=True)
        if layer == 0:
            arrived, statics, columns, weight_slices = lax.optimization_barrier(
                (arrived, statics, columns, weight_slices)
            )
        if layer == 1:
            statics += static_parts(
                tile_values,
                slots,
                after(hist_slices, partial),
                replaced,
                select,
                tuple(range(2, layers)),
            )
            arrived, statics = lax.optimization_barrier((arrived, statics))
        if table is not None:
            arrived, table = lax.optimization_barrier((arrived, table))
        support = collect(arrived, initial)
        near = jnp.stack([support] + [rotated(support, "section", by) for by in range(1, layers)])
        gathered = lax.all_gather(near, "feat", axis=0)
        if layer < layers - 1:
            partial = layer_step(
                place,
                gathered,
                support,
                weight_slices,
                statics[layer],
                columns,
                layer,
                betas[layer],
                row_devices,
            )
        rows_kept = whole_rows(place, beta_table, gathered, own_weights, rows_kept, layer)
    return (rows_kept.reshape(1, spans, rows_local, half), table[None])


def solution(mesh):
    placed = (
        P("vertex", "feat"),
        P("section", "vertex", "feat"),
        P("section", None, "feat"),
        P(None, "vertex", None, None),
        P(None, "vertex"),
        P(None, "vertex"),
        P(None, "vertex"),
        P(None, "vertex"),
    )
    return jax.shard_map(
        shards,
        mesh=mesh,
        in_specs=placed,
        out_specs=(P("section", None, "vertex", "feat"), P("section", "vertex", "feat")),
        check_vma=False,
    )
```

profile of v0, /device:TPU:1, one launch (start us, length us, event | category | flops | bytes accessed | tf_op | source)
XLA Modules:
  0.0 240.8 jit_solution(7751473484847897944)
XLA Ops:
  0.6 4.0 %section_slices.1 = bf16[4,2048,128]{2,1,0:T(8,128)(2,1)} custom-call(bf16[2048,512]{1,0:T(8,128)(2,1)} %bitcast.46), custom_call_target="tpu_custom_call" | custom-call | bytes 4194304 | tf_op jit(solution)/shard_map/section_slices/pallas_call | solution.py:130
  4.7 5.0 %all-to-all-start = ((bf16[4,2048,128]{2,1,0:T(8,128)(2,1)}), bf16[4,2048,128]{2,1,0:T(8,128)(2,1)}, u32[]{:S(2)}, u32[]{:S(2)}) async-start(bf16[4,2048,128]{2,1,0:T(8,128)(2,1)} %section_slices.1), calls=%async_computation | async-start | bytes 4194304 | tf_op jit(solution)/shard_map/all_to_all | solution.py:532
  9.7 2.1 gather_fusion
  11.8 1.2 selection.1
  13.1 1.2 copy-done.6
  14.2 1.2 copy-done.12
  17.4 18.3 %all-to-all-done.hist_ref = bf16[4,2048,128]{2,1,0:T(8,128)(2,1)} async-done(((bf16[4,2048,128]{2,1,0:T(8,128)(2,1)}), bf16[4,2048,128]{2,1,0:T(8,128)(2,1)}, u32[]{:S(2)}, u32[]{:S(2)}) %all-to-all-start) | async-done | bytes 2097184 | tf_op jit(solution)/shard_map/all_to_all | solution.py:532
  35.6 12.8 %first_partial.1 = bf16[16,3,128,128]{3,2,1,0:T(8,128)(2,1)} custom-call(s32[3,256]{1,0:T(4,128)} %broadcast_add_fusion.slots_ref, bf16[3,64,128,128]{3,2,1,0:T(8,128)(2,1)} %tiles_ref.5, bf16[4,2048,128]{2,1,0:T(8,128)(2,1)} %all-to-all-done.hist_ref, bf16[2048,128]{1,0:T(8,128)(2,1)} %constant_dynamic-slice_fusion.4.feat_ref, bf16[3,2048,128]{2,1,0:T(8,128)(2,1)} %copy-done.6), custom_call_target="tpu_custom_call" | custom-call | flops 3221225472 | bytes 6291456 | tf_op jit(solution)/shard_map/first_partial/pallas_call | solution.py:102
  48.5 8.2 %all-to-all-start.1 = ((bf16[16,3,128,128]{3,2,1,0:T(8,128)(2,1)}), bf16[16,3,128,128]{3,2,1,0:T(8,128)(2,1)}, u32[]{:S(2)}, u32[]{:S(2)}) async-start(bf16[16,3,128,128]{3,2,1,0:T(8,128)(2,1)} %first_partial.1), calls=%async_computation.1 | async-start | bytes 3145728 | tf_op jit(solution)/shard_map/all_to_all | solution.py:570
  58.6 1.2 collective-permute-start.1
  59.8 17.8 %static_parts.2 = (f32[3,2048,128]{2,1,0:T(8,128)}, bf16[2048,128]{1,0:T(8,128)(2,1)}, bf16[2048,256]{1,0:T(8,128)(2,1)}, bf16[2048,384]{1,0:T(8,128)(2,1)}) custom-call(s32[3,256]{1,0:T(4,128)} %broadcast_add_fusion.slots_ref, bf16[3,64,128,128]{3,2,1,0:T(8,128)(2,1)} %tiles_ref.5, bf16[4,2048,128]{2,1,0:T(8,128)(2,1)} %all-to-all-done.hist_ref, ...), custom_call_target="tpu_custom_call" | custom-call | flops 12884901888 | bytes 14155776 | tf_op jit(solution)/shard_map/static_parts/pallas_call | solution.py:306
  77.6 1.5 collect.4.sup_ref
  79.1 2.7 %collective-permute-start.5 = (bf16[384,128]{1,0:T(8,128)(2,1)S(1)}, bf16[384,128]{1,0:T(8,128)(2,1)S(1)}, u32[]{:S(2)}, u32[]{:S(2)}) collective-permute-start(bf16[384,128]{1,0:T(8,128)(2,1)S(1)} %collect.4.sup_ref), channel_id=1, source_target_pairs={{0,96},{32,0},{64,32},{96,64},{1,97},{33,1},{65,33},{97,65},{2,98}... | collective-permute-start | bytes 294920 | tf_op jit(solution)/shard_map/ppermute | solution.py:22
  83.7 3.2 %collective-permute-done.4 = bf16[384,128]{1,0:T(8,128)(2,1)S(1)} collective-permute-done((bf16[384,128]{1,0:T(8,128)(2,1)S(1)}, bf16[384,128]{1,0:T(8,128)(2,1)S(1)}, u32[]{:S(2)}, u32[]{:S(2)}) %collective-permute-start.4) | collective-permute-done | bytes 98336 | tf_op jit(solution)/shard_map/ppermute | solution.py:22
  87.9 6.2 %all-gather = bf16[8,384,128]{2,1,0:T(8,128)(2,1)} all-gather(bf16[4,384,128]{2,1,0:T(8,128)(2,1)S(1)} %pad_maximum_fusion), channel_id=2, replica_groups=mesh['section'=4,'vertex'=16,'feat'=2] {'feat'}, dimensions={0}, use_global_device_ids=true | all-gather | bytes 1179648 | tf_op jit(solution)/shard_map/all_gather | solution.py:589
  94.2 6.1 %layer_step.3 = bf16[16,3,128,128]{3,2,1,0:T(8,128)(2,1)} custom-call(s32[2]{0:T(128)} %pad_add_fusion.place_ref, bf16[2,4,384,128]{3,2,1,0:T(8,128)(2,1)} %bitcast.48, bf16[384,128]{1,0:T(8,128)(2,1)} %copy-done.8, f32[3,2048,128]{2,1,0:T(8,128)} %get-tuple-element.48.static_ref, bf16[1024,128]{1,0:T(8,128)(2,1)} %get-tuple-element.49.refs_0_, ...), custom_call_target="tpu_custom_call" | custom-call | flops 704643072 | bytes 9437184 | tf_op jit(solution)/shard_map/layer_step/pallas_call | solution.py:412
  100.2 6.9 %all-to-all-start.2 = ((bf16[16,3,128,128]{3,2,1,0:T(8,128)(2,1)}), bf16[16,3,128,128]{3,2,1,0:T(8,128)(2,1)}, u32[]{:S(2)}, u32[]{:S(2)}) async-start(bf16[16,3,128,128]{3,2,1,0:T(8,128)(2,1)} %layer_step.3), calls=%async_computation.2 | async-start | bytes 3145728 | tf_op jit(solution)/shard_map/all_to_all | solution.py:570
  107.1 14.3 %static_parts.3 = (f32[3,2048,128]{2,1,0:T(8,128)}, f32[3,2048,128]{2,1,0:T(8,128)}) custom-call(s32[3,256]{1,0:T(4,128)} %broadcast_add_fusion.slots_ref, bf16[3,64,128,128]{3,2,1,0:T(8,128)(2,1)} %tiles_ref.5, bf16[4,2048,128]{2,1,0:T(8,128)(2,1)} %all-to-all-done.hist_ref, bf16[3,2048,128]{2,1,0:T(8,128)(2,1)} %copy-done.6, bf16[2048,384]{1,0:T(8,128)(2,1)} %copy-done.12), custom_call_target="tpu_custom_call" | custom-call | flops 6442450944 | bytes 12582912 | tf_op jit(solution)/shard_map/static_parts/pallas_call | solution.py:306
  121.4 9.8 %all-to-all-done.2.in_ref = bf16[16,3,128,128]{3,2,1,0:T(8,128)(2,1)} async-done(((bf16[16,3,128,128]{3,2,1,0:T(8,128)(2,1)}), bf16[16,3,128,128]{3,2,1,0:T(8,128)(2,1)}, u32[]{:S(2)}, u32[]{:S(2)}) %all-to-all-start.2) | async-done | bytes 1572896 | tf_op jit(solution)/shard_map/all_to_all | solution.py:570
  131.2 1.5 collect.5.sup_ref
  134.3 1.9 collective-permute-done.8
  136.2 1.7 collective-permute-done.7
  137.9 1.0 collective-permute-done.6
  139.0 5.7 %all-gather.1 = bf16[8,384,128]{2,1,0:T(8,128)(2,1)} all-gather(bf16[4,384,128]{2,1,0:T(8,128)(2,1)S(1)} %pad_maximum_fusion.1), channel_id=3, replica_groups=mesh['section'=4,'vertex'=16,'feat'=2] {'feat'}, dimensions={0}, use_global_device_ids=true | all-gather | bytes 1179648 | tf_op jit(solution)/shard_map/all_gather | solution.py:589
  144.7 6.1 %layer_step.4 = bf16[16,3,128,128]{3,2,1,0:T(8,128)(2,1)} custom-call(s32[2]{0:T(128)} %pad_add_fusion.place_ref, bf16[2,4,384,128]{3,2,1,0:T(8,128)(2,1)} %bitcast.50, bf16[384,128]{1,0:T(8,128)(2,1)} %copy-done.9, f32[3,2048,128]{2,1,0:T(8,128)} %get-tuple-element.60.static_ref, bf16[1024,128]{1,0:T(8,128)(2,1)} %get-tuple-element.49.refs_0_, ...), custom_call_target="tpu_custom_call" | custom-call | flops 704643072 | bytes 9437184 | tf_op jit(solution)/shard_map/layer_step/pallas_call | solution.py:412
  150.8 25.9 %all_to_all.25.in_ref = bf16[16,3,128,128]{3,2,1,0:T(8,128)(2,1)S(1)} all-to-all(bf16[16,3,128,128]{3,2,1,0:T(8,128)(2,1)} %layer_step.4), channel_id=1, replica_groups=mesh['section'=4,'vertex'=16,'feat'=2] {'vertex'}, dimensions={0} | all-to-all | bytes 3145728 | tf_op jit(solution)/shard_map/all_to_all | solution.py:570
  176.7 1.0 collect.6.sup_ref
  177.7 1.1 collective-permute-start.11
  179.5 1.8 collective-permute-done.11
  181.3 2.6 %collective-permute-done.10 = bf16[384,128]{1,0:T(8,128)(2,1)S(1)} collective-permute-done((bf16[384,128]{1,0:T(8,128)(2,1)S(1)}, bf16[384,128]{1,0:T(8,128)(2,1)S(1)}, u32[]{:S(2)}, u32[]{:S(2)}) %collective-permute-start.10) | collective-permute-done | bytes 98336 | tf_op jit(solution)/shard_map/ppermute | solution.py:22
  183.9 1.0 collective-permute-done.9
  184.9 5.3 %all-gather.2 = bf16[8,384,128]{2,1,0:T(8,128)(2,1)} all-gather(bf16[4,384,128]{2,1,0:T(8,128)(2,1)S(1)} %pad_maximum_fusion.2), channel_id=4, replica_groups=mesh['section'=4,'vertex'=16,'feat'=2] {'feat'}, dimensions={0}, use_global_device_ids=true | all-gather | bytes 1179648 | tf_op jit(solution)/shard_map/all_gather | solution.py:589
  190.2 6.1 %layer_step.5 = bf16[16,3,128,128]{3,2,1,0:T(8,128)(2,1)} custom-call(s32[2]{0:T(128)} %pad_add_fusion.place_ref, bf16[2,4,384,128]{3,2,1,0:T(8,128)(2,1)} %bitcast.52, bf16[384,128]{1,0:T(8,128)(2,1)} %copy-done.7, f32[3,2048,128]{2,1,0:T(8,128)} %get-tuple-element.61.static_ref, bf16[1024,128]{1,0:T(8,128)(2,1)} %get-tuple-element.49.refs_0_, ...), custom_call_target="tpu_custom_call" | custom-call | flops 704643072 | bytes 9437184 | tf_op jit(solution)/shard_map/layer_step/pallas_call | solution.py:412
  196.4 4.4 %all-to-all-start.4 = ((bf16[16,3,128,128]{3,2,1,0:T(8,128)(2,1)}), bf16[16,3,128,128]{3,2,1,0:T(8,128)(2,1)}, u32[]{:S(2)}, u32[]{:S(2)}) async-start(bf16[16,3,128,128]{3,2,1,0:T(8,128)(2,1)} %layer_step.5), calls=%async_computation.4 | async-start | bytes 3145728 | tf_op jit(solution)/shard_map/all_to_all | solution.py:570
  200.8 1.1 copy-done.3
  202.0 1.2 whole_rows.4.refs_0_
  203.8 1.3 whole_rows.6.refs_0_
  205.1 11.9 %collective-permute-done.12 = bf16[384,512]{1,0:T(8,128)(2,1)} collective-permute-done((bf16[384,512]{1,0:T(8,128)(2,1)}, bf16[384,512]{1,0:T(8,128)(2,1)}, u32[]{:S(2)}, u32[]{:S(2)}) %collective-permute-start.12) | collective-permute-done | bytes 393248 | tf_op jit(solution)/shard_map/ppermute | solution.py:22
  217.0 1.1 broadcast_select_fusion.1.fresh_ref
  218.1 1.6 copy-done.2
  219.7 2.9 %replace_rows.1 = bf16[2048,512]{1,0:T(8,128)(2,1)} custom-call(bf16[2048,512]{1,0:T(8,128)(2,1)S(1)} %bitcast.47, s32[1,384]{1,0:T(1,128)S(1)} %bitcast.60, bf16[384,512]{1,0:T(8,128)(2,1)S(1)} %broadcast_select_fusion.1.fresh_ref), custom_call_target="tpu_custom_call" | custom-call | flops 805306368 | bytes 4194304 | tf_op jit(solution)/shard_map/replace_rows/pallas_call | solution.py:501
  222.6 3.4 %all-to-all-done.4.in_ref = bf16[16,3,128,128]{3,2,1,0:T(8,128)(2,1)} async-done(((bf16[16,3,128,128]{3,2,1,0:T(8,128)(2,1)}), bf16[16,3,128,128]{3,2,1,0:T(8,128)(2,1)}, u32[]{:S(2)}, u32[]{:S(2)}) %all-to-all-start.4) | async-done | bytes 1572896 | tf_op jit(solution)/shard_map/all_to_all | solution.py:570
  226.0 1.5 collect.7
  229.0 2.0 collective-permute-done.15
  231.0 2.1 collective-permute-done.14
  233.1 1.5 collective-permute-done.13
  234.7 4.3 %all-gather.3 = bf16[8,384,128]{2,1,0:T(8,128)(2,1)S(1)} all-gather(bf16[4,384,128]{2,1,0:T(8,128)(2,1)S(1)} %pad_maximum_fusion.3), channel_id=5, replica_groups=mesh['section'=4,'vertex'=16,'feat'=2] {'feat'}, dimensions={0}, use_global_device_ids=true | all-gather | bytes 1179648 | tf_op jit(solution)/shard_map/all_gather | solution.py:589
  239.0 1.8 whole_rows.7
  (69 shorter events, 11.2 us)
Async XLA Ops:
  0.6 9.1 %copy-start = (bf16[2048,512]{1,0:T(8,128)(2,1)S(1)}, bf16[2048,512]{1,0:T(8,128)(2,1)}, u32[]{:S(2)}) copy-start(bf16[2048,512]{1,0:T(8,128)(2,1)} %param.9) | copy-start | bytes 6291460
  4.7 5.0 %copy-start.14 = (s32[3,128]{1,0:T(4,128)S(1)}, s32[3,128]{1,0:T(4,128)}, u32[]{:S(2)}) copy-start(s32[3,128]{1,0:T(4,128)} %param.16) | copy-start | bytes 4612
  4.7 30.9 %all-to-all-start = ((bf16[4,2048,128]{2,1,0:T(8,128)(2,1)}), bf16[4,2048,128]{2,1,0:T(8,128)(2,1)}, u32[]{:S(2)}, u32[]{:S(2)}) async-start(bf16[4,2048,128]{2,1,0:T(8,128)(2,1)} %section_slices.1), calls=%async_computation | async-start | bytes 4194304 | tf_op jit(solution)/shard_map/all_to_all | solution.py:532
  9.7 5.9 %copy-start.15 = (s32[3,64]{1,0:T(4,128)S(1)}, s32[3,64]{1,0:T(4,128)}, u32[]{:S(2)}) copy-start(s32[3,64]{1,0:T(4,128)} %param.14) | copy-start | bytes 2308
  9.7 5.9 %copy-start.16 = (s32[3,64]{1,0:T(4,128)S(1)}, s32[3,64]{1,0:T(4,128)}, u32[]{:S(2)}) copy-start(s32[3,64]{1,0:T(4,128)} %param.13) | copy-start | bytes 2308
  9.7 5.9 %copy-start.17 = (s32[3,1]{0,1:T(1,128)S(1)}, s32[3,1]{0,1:T(1,128)}, u32[]{:S(2)}) copy-start(s32[3,1]{0,1:T(1,128)} %param.15) | copy-start | bytes 40
  11.8 23.8 %copy-start.13 = (bf16[384,512]{1,0:T(8,128)(2,1)}, bf16[384,512]{1,0:T(8,128)(2,1)S(1)}, u32[]{:S(2)}) copy-start(bf16[384,512]{1,0:T(8,128)(2,1)S(1)} %gather_fusion) | copy-start | bytes 1179652
  13.1 1.2 copy-start.6
  14.2 1.2 copy-start.12
  48.5 8.3 %copy-start.1 = (bf16[1,1024,512]{2,1,0:T(8,128)(2,1)S(1)}, bf16[1,1024,512]{2,1,0:T(8,128)(2,1)}, u32[]{:S(2)}) copy-start(bf16[1,1024,512]{2,1,0:T(8,128)(2,1)} %param.11) | copy-start | bytes 3145732
  48.5 29.1 %all-to-all-start.1 = ((bf16[16,3,128,128]{3,2,1,0:T(8,128)(2,1)}), bf16[16,3,128,128]{3,2,1,0:T(8,128)(2,1)}, u32[]{:S(2)}, u32[]{:S(2)}) async-start(bf16[16,3,128,128]{3,2,1,0:T(8,128)(2,1)} %first_partial.1), calls=%async_computation.1 | async-start | bytes 3145728 | tf_op jit(solution)/shard_map/all_to_all | solution.py:570
  57.7 19.9 %collective-permute-start.2 = (bf16[1024,128]{1,0:T(8,128)(2,1)S(1)}, bf16[1024,128]{1,0:T(8,128)(2,1)}, u32[]{:S(2)}, u32[]{:S(2)}) collective-permute-start(bf16[1024,128]{1,0:T(8,128)(2,1)S(1)} %get-tuple-element.64), channel_id=1, source_target_pairs={{0,96},{32,0},{64,32},{96,64},{1,97},{33,1},{65,33},{97,65},{2,98}... | collective-permute-start | bytes 786440 | tf_op jit(solution)/shard_map/ppermute | solution.py:22
  58.6 19.0 %collective-permute-start.1 = (bf16[1024,128]{1,0:T(8,128)(2,1)S(1)}, bf16[1024,128]{1,0:T(8,128)(2,1)}, u32[]{:S(2)}, u32[]{:S(2)}) collective-permute-start(bf16[1024,128]{1,0:T(8,128)(2,1)S(1)} %get-tuple-element.65), channel_id=1, source_target_pairs={{0,64},{32,96},{64,0},{96,32},{1,65},{33,97},{65,1},{97,33},{2,66}... | collective-permute-start | bytes 786440 | tf_op jit(solution)/shard_map/ppermute | solution.py:22
  59.8 17.8 %collective-permute-start = (bf16[1024,128]{1,0:T(8,128)(2,1)S(1)}, bf16[1024,128]{1,0:T(8,128)(2,1)}, u32[]{:S(2)}, u32[]{:S(2)}) collective-permute-start(bf16[1024,128]{1,0:T(8,128)(2,1)S(1)} %get-tuple-element.66), channel_id=1, source_target_pairs={{0,32},{32,64},{64,96},{96,0},{1,33},{33,65},{65,97},{97,1},{2,34}... | collective-permute-start | bytes 786440 | tf_op jit(solution)/shard_map/ppermute | solution.py:22
  79.1 15.1 %copy-start.8 = (bf16[384,128]{1,0:T(8,128)(2,1)}, bf16[384,128]{1,0:T(8,128)(2,1)S(1)}, u32[]{:S(2)}) copy-start(bf16[384,128]{1,0:T(8,128)(2,1)S(1)} %collect.4.sup_ref) | copy-start | bytes 294916
  79.1 4.6 %collective-permute-start.5 = (bf16[384,128]{1,0:T(8,128)(2,1)S(1)}, bf16[384,128]{1,0:T(8,128)(2,1)S(1)}, u32[]{:S(2)}, u32[]{:S(2)}) collective-permute-start(bf16[384,128]{1,0:T(8,128)(2,1)S(1)} %collect.4.sup_ref), channel_id=1, source_target_pairs={{0,96},{32,0},{64,32},{96,64},{1,97},{33,1},{65,33},{97,65},{2,98}... | collective-permute-start | bytes 294920 | tf_op jit(solution)/shard_map/ppermute | solution.py:22
  81.8 5.1 %collective-permute-start.4 = (bf16[384,128]{1,0:T(8,128)(2,1)S(1)}, bf16[384,128]{1,0:T(8,128)(2,1)S(1)}, u32[]{:S(2)}, u32[]{:S(2)}) collective-permute-start(bf16[384,128]{1,0:T(8,128)(2,1)S(1)} %collect.4.sup_ref), channel_id=1, source_target_pairs={{0,64},{32,96},{64,0},{96,32},{1,65},{33,97},{65,1},{97,33},{2,66}... | collective-permute-start | bytes 294920 | tf_op jit(solution)/shard_map/ppermute | solution.py:22
  82.4 5.4 %collective-permute-start.3 = (bf16[384,128]{1,0:T(8,128)(2,1)S(1)}, bf16[384,128]{1,0:T(8,128)(2,1)S(1)}, u32[]{:S(2)}, u32[]{:S(2)}) collective-permute-start(bf16[384,128]{1,0:T(8,128)(2,1)S(1)} %collect.4.sup_ref), channel_id=1, source_target_pairs={{0,32},{32,64},{64,96},{96,0},{1,33},{33,65},{65,97},{97,1},{2,34}... | collective-permute-start | bytes 294920 | tf_op jit(solution)/shard_map/ppermute | solution.py:22
  100.2 30.9 %all-to-all-start.2 = ((bf16[16,3,128,128]{3,2,1,0:T(8,128)(2,1)}), bf16[16,3,128,128]{3,2,1,0:T(8,128)(2,1)}, u32[]{:S(2)}, u32[]{:S(2)}) async-start(bf16[16,3,128,128]{3,2,1,0:T(8,128)(2,1)} %layer_step.3), calls=%async_computation.2 | async-start | bytes 3145728 | tf_op jit(solution)/shard_map/all_to_all | solution.py:570
  132.6 12.0 %copy-start.9 = (bf16[384,128]{1,0:T(8,128)(2,1)}, bf16[384,128]{1,0:T(8,128)(2,1)S(1)}, u32[]{:S(2)}) copy-start(bf16[384,128]{1,0:T(8,128)(2,1)S(1)} %collect.5.sup_ref) | copy-start | bytes 294916
  132.7 3.5 %collective-permute-start.8 = (bf16[384,128]{1,0:T(8,128)(2,1)S(1)}, bf16[384,128]{1,0:T(8,128)(2,1)S(1)}, u32[]{:S(2)}, u32[]{:S(2)}) collective-permute-start(bf16[384,128]{1,0:T(8,128)(2,1)S(1)} %collect.5.sup_ref), channel_id=1, source_target_pairs={{0,96},{32,0},{64,32},{96,64},{1,97},{33,1},{65,33},{97,65},{2,98}... | collective-permute-start | bytes 294920 | tf_op jit(solution)/shard_map/ppermute | solution.py:22
  132.9 5.0 %collective-permute-start.7 = (bf16[384,128]{1,0:T(8,128)(2,1)S(1)}, bf16[384,128]{1,0:T(8,128)(2,1)S(1)}, u32[]{:S(2)}, u32[]{:S(2)}) collective-permute-start(bf16[384,128]{1,0:T(8,128)(2,1)S(1)} %collect.5.sup_ref), channel_id=1, source_target_pairs={{0,64},{32,96},{64,0},{96,32},{1,65},{33,97},{65,1},{97,33},{2,66}... | collective-permute-start | bytes 294920 | tf_op jit(solution)/shard_map/ppermute | solution.py:22
  133.6 5.4 %collective-permute-start.6 = (bf16[384,128]{1,0:T(8,128)(2,1)S(1)}, bf16[384,128]{1,0:T(8,128)(2,1)S(1)}, u32[]{:S(2)}, u32[]{:S(2)}) collective-permute-start(bf16[384,128]{1,0:T(8,128)(2,1)S(1)} %collect.5.sup_ref), channel_id=1, source_target_pairs={{0,32},{32,64},{64,96},{96,0},{1,33},{33,65},{65,97},{97,1},{2,34}... | collective-permute-start | bytes 294920 | tf_op jit(solution)/shard_map/ppermute | solution.py:22
  177.7 12.5 %copy-start.7 = (bf16[384,128]{1,0:T(8,128)(2,1)}, bf16[384,128]{1,0:T(8,128)(2,1)S(1)}, u32[]{:S(2)}) copy-start(bf16[384,128]{1,0:T(8,128)(2,1)S(1)} %collect.6.sup_ref) | copy-start | bytes 294916
  177.7 3.5 %collective-permute-start.11 = (bf16[384,128]{1,0:T(8,128)(2,1)S(1)}, bf16[384,128]{1,0:T(8,128)(2,1)S(1)}, u32[]{:S(2)}, u32[]{:S(2)}) collective-permute-start(bf16[384,128]{1,0:T(8,128)(2,1)S(1)} %collect.6.sup_ref), channel_id=1, source_target_pairs={{0,96},{32,0},{64,32},{96,64},{1,97},{33,1},{65,33},{97,65},{2,98}... | collective-permute-start | bytes 294920 | tf_op jit(solution)/shard_map/ppermute | solution.py:22
  178.9 5.0 %collective-permute-start.10 = (bf16[384,128]{1,0:T(8,128)(2,1)S(1)}, bf16[384,128]{1,0:T(8,128)(2,1)S(1)}, u32[]{:S(2)}, u32[]{:S(2)}) collective-permute-start(bf16[384,128]{1,0:T(8,128)(2,1)S(1)} %collect.6.sup_ref), channel_id=1, source_target_pairs={{0,64},{32,96},{64,0},{96,32},{1,65},{33,97},{65,1},{97,33},{2,66}... | collective-permute-start | bytes 294920 | tf_op jit(solution)/shard_map/ppermute | solution.py:22
  179.5 5.4 %collective-permute-start.9 = (bf16[384,128]{1,0:T(8,128)(2,1)S(1)}, bf16[384,128]{1,0:T(8,128)(2,1)S(1)}, u32[]{:S(2)}, u32[]{:S(2)}) collective-permute-start(bf16[384,128]{1,0:T(8,128)(2,1)S(1)} %collect.6.sup_ref), channel_id=1, source_target_pairs={{0,32},{32,64},{64,96},{96,0},{1,33},{33,65},{65,97},{97,1},{2,34}... | collective-permute-start | bytes 294920 | tf_op jit(solution)/shard_map/ppermute | solution.py:22
  196.4 4.4 %copy-start.10 = (s32[2]{0:T(128)S(1)}, s32[2]{0:T(128)}, u32[]{:S(2)}) copy-start(s32[2]{0:T(128)} %pad_add_fusion.place_ref) | copy-start | bytes 28
  196.4 4.4 %copy-start.11 = (f32[4]{0:T(128)S(1)}, f32[4]{0:T(128)}, u32[]{:S(2)}) copy-start(f32[4]{0:T(128)} %constant.71.clone.betas_ref) | copy-start | bytes 52
  196.4 29.6 %all-to-all-start.4 = ((bf16[16,3,128,128]{3,2,1,0:T(8,128)(2,1)}), bf16[16,3,128,128]{3,2,1,0:T(8,128)(2,1)}, u32[]{:S(2)}, u32[]{:S(2)}) async-start(bf16[16,3,128,128]{3,2,1,0:T(8,128)(2,1)} %layer_step.5), calls=%async_computation.4 | async-start | bytes 3145728 | tf_op jit(solution)/shard_map/all_to_all | solution.py:570
  200.8 1.1 copy-start.3
  202.0 1.2 copy-start.4
  202.0 1.8 copy-start.5
  205.1 11.9 %collective-permute-start.12 = (bf16[384,512]{1,0:T(8,128)(2,1)}, bf16[384,512]{1,0:T(8,128)(2,1)}, u32[]{:S(2)}, u32[]{:S(2)}) collective-permute-start(bf16[384,512]{1,0:T(8,128)(2,1)} %whole_rows.6.refs_0_), channel_id=1, source_target_pairs={{0,32},{32,64},{64,96},{96,0},{1,33},{33,65},{65,97},{97,1},{2,34}... | collective-permute-start | bytes 1179656 | tf_op jit(solution)/shard_map/ppermute | solution.py:22
  218.1 1.6 copy-start.2
  227.5 3.5 %collective-permute-start.15 = (bf16[384,128]{1,0:T(8,128)(2,1)S(1)}, bf16[384,128]{1,0:T(8,128)(2,1)S(1)}, u32[]{:S(2)}, u32[]{:S(2)}) collective-permute-start(bf16[384,128]{1,0:T(8,128)(2,1)S(1)} %collect.7), channel_id=1, source_target_pairs={{0,96},{32,0},{64,32},{96,64},{1,97},{33,1},{65,33},{97,65},{2,98}... | collective-permute-start | bytes 294920 | tf_op jit(solution)/shard_map/ppermute | solution.py:22
  228.0 5.0 %collective-permute-start.14 = (bf16[384,128]{1,0:T(8,128)(2,1)S(1)}, bf16[384,128]{1,0:T(8,128)(2,1)S(1)}, u32[]{:S(2)}, u32[]{:S(2)}) collective-permute-start(bf16[384,128]{1,0:T(8,128)(2,1)S(1)} %collect.7), channel_id=1, source_target_pairs={{0,64},{32,96},{64,0},{96,32},{1,65},{33,97},{65,1},{97,33},{2,66}... | collective-permute-start | bytes 294920 | tf_op jit(solution)/shard_map/ppermute | solution.py:22
  228.6 6.0 %collective-permute-start.13 = (bf16[384,128]{1,0:T(8,128)(2,1)S(1)}, bf16[384,128]{1,0:T(8,128)(2,1)S(1)}, u32[]{:S(2)}, u32[]{:S(2)}) collective-permute-start(bf16[384,128]{1,0:T(8,128)(2,1)S(1)} %collect.7), channel_id=1, source_target_pairs={{0,32},{32,64},{64,96},{96,0},{1,33},{33,65},{65,97},{97,1},{2,34}... | collective-permute-start | bytes 294920 | tf_op jit(solution)/shard_map/ppermute | solution.py:22
where the time goes:
time: 242 us; the launch traced here: 241 us
  Pallas kernels  81.6 us (34%)
  waiting for transfers between devices  63.1 us (26%)
  blocking collectives  47.4 us (20%)
  starting transfers between devices  35.5 us (15%)
  local copies, waits for them, and re-layouts  9.03 us (4%)
  other arithmetic  2.96 us (1%)
    pallas_call x2, Pallas kernels, static_parts(): pl.pallas_call(kernel, out_shape=tuple(out_shape), in_specs=[IN_SMEM, IN_...  32 us
    ppermute x16, waiting for transfers between devices, rotated(): lax.ppermute(array, axis, [(i, (i + by) % devices) for i in range(devices)])  31.7 us
    all_to_all x1, blocking collectives, shards(): arrived = lax.all_to_all(partial, 'vertex', 0, 0, tiled=True)  25.9 us
    all_gather x4, blocking collectives, shards(): gathered = lax.all_gather(near, 'feat', axis=0)  21.5 us
    all_to_all x3, starting transfers between devices, shards(): arrived = lax.all_to_all(partial, 'vertex', 0, 0, tiled=True)  19.5 us
    all_to_all x1, waiting for transfers between devices, shards(): lax.all_to_all(section_slices(stored, layers), 'section', 0, 0, tiled=True)  18.3 us
    pallas_call x3, Pallas kernels, layer_step(): pl.pallas_call(kernel, out_shape=jax.ShapeDtypeStruct((row_devices, spans...  18.3 us
    all_to_all x3, waiting for transfers between devices, shards(): arrived = lax.all_to_all(partial, 'vertex', 0, 0, tiled=True)  13.2 us
  transfers between devices with their start and end apart: 20, of which 15 were waited for; matrix products, arithmetic and copies ran while one was open for 3% of the time, Pallas kernels for 16%

commit v1 on v0

--- a/solution.py
+++ b/solution.py
@@ -46,6 +46,19 @@
     return jnp.concatenate(lines, axis=0)
 
 
+def multiply(tiles_ref, slots_ref, span, right, width, put):
+    side = tiles_ref.shape[-1]
+    col_blocks = right.shape[0] // side
+    row_blocks = slots_ref.shape[1] // col_blocks
+    step = ROW_CHUNK // side
+
+    @pl.loop(0, row_blocks, step=step)
+    def _(first):
+        left = rows_from(tiles_ref, slots_ref, span, first, step, col_blocks)
+        part = jnp.dot(left, right[:, :width], preferred_element_type=jnp.float32)
+        put(pl.ds(pl.multiple_of(first * side, side), ROW_CHUNK), part)
+
+
 def tile_copies(tiles_ref, held, sems):
     spans, slots = tiles_ref.shape[:2]
     return [
@@ -66,54 +79,62 @@
     _, cols, width = hist_slices.shape
     col_blocks = cols // side
     row_blocks = slots.shape[1] // col_blocks
-    step = ROW_CHUNK // side
-    chunks = row_blocks // step
-
-    def kernel(slots_ref, tiles_ref, hist_ref, feat_ref, mask_ref, out_ref, held, tile_sems, hist, hist_sem, table, sums, out_sems):
-        hist_copy = pltpu.make_async_copy(hist_ref.at[0], hist, hist_sem)
+
+    def kernel(slots_ref, tiles_ref, hist_ref, feat_ref, mask_ref, out_ref, static_ref, held, tile_sems, hist, hist_sem, table, sums, out_sems, static, static_sems):
+        hist_copy = pltpu.make_async_copy(hist_ref.at[pl.ds(0, 2)], hist, hist_sem)
         copies = tile_copies(tiles_ref, held, tile_sems)
         for copy in [hist_copy] + copies:
             copy.start()
-        def sent(span, chunk):
-            at = pl.ds(chunk * step, step)
-            return pltpu.make_async_copy(
-                sums.at[span, at], out_ref.at[at, span], out_sems.at[span, chunk]
-            )
-
         hist_copy.wait()
+        outgoing = []
         for span in range(spans):
             held[span, slot_count] = jnp.zeros((side, side), jnp.bfloat16)
-            table[...] = jnp.where(mask_ref[span] > 0, feat_ref[...], hist[...])
+            replaces = mask_ref[span] > 0
+            table[:, :width] = jnp.where(replaces, feat_ref[...], hist[0])
+            table[:, width:] = jnp.where(replaces, jnp.zeros_like(hist[1]), hist[1])
             copies[span].wait()
 
-            @pl.loop(0, chunks)
-            def _(chunk):
-                left = rows_from(held, slots_ref, span, chunk * step, step, col_blocks)
-                part = jnp.dot(left, table[...], preferred_element_type=jnp.float32)
-                sums[span, pl.ds(chunk * step, step)] = part.astype(jnp.bfloat16).reshape(
-                    step, side, width
-                )
-                sent(span, chunk).start()
-
-        for span in range(spans):
-            for chunk in range(chunks):
-                sent(span, chunk).wait()
-
-    return pl.pallas_call(
-        kernel,
-        out_shape=jax.ShapeDtypeStruct((row_devices, spans, side, width), jnp.bfloat16),
+            def put(at, part, span=span):
+                sums[span, at] = part[:, :width].astype(jnp.bfloat16)
+                static[span, at] = part[:, width:]
+
+            multiply(held, slots_ref, span, table, 2 * width, put)
+            outgoing.append(
+                pltpu.make_async_copy(static.at[span], static_ref.at[span], static_sems.at[span])
+            )
+            outgoing[-1].start()
+            for device in range(row_devices):
+                outgoing.append(
+                    pltpu.make_async_copy(
+                        sums.at[span, pl.ds(device * side, side)],
+                        out_ref.at[device, span],
+                        out_sems.at[span, device],
+                    )
+                )
+                outgoing[-1].start()
+        for copy in outgoing:
+            copy.wait()
+
+    return pl.pallas_call(
+        kernel,
+        out_shape=(
+            jax.ShapeDtypeStruct((row_devices, spans, side, width), jnp.bfloat16),
+            jax.ShapeDtypeStruct((spans, row_blocks * side, width), jnp.float32),
+        ),
         in_specs=[IN_SMEM, IN_HBM, IN_HBM, IN_VMEM, IN_VMEM],
-        out_specs=IN_HBM,
+        out_specs=(IN_HBM, IN_HBM),
         scratch_shapes=[
             *tile_scratch(tiles),
-            pltpu.VMEM((cols, width), jnp.bfloat16),
+            pltpu.VMEM((2, cols, width), jnp.bfloat16),
             pltpu.SemaphoreType.DMA(()),
-            pltpu.VMEM((cols, width), jnp.bfloat16),
-            pltpu.VMEM((spans, row_devices, side, width), jnp.bfloat16),
-            pltpu.SemaphoreType.DMA((spans, chunks)),
+            pltpu.VMEM((cols, 2 * width), jnp.bfloat16),
+            pltpu.VMEM((spans, row_blocks * side, width), jnp.bfloat16),
+            pltpu.SemaphoreType.DMA((spans, row_devices)),
+            pltpu.VMEM((spans, row_blocks * side, width), jnp.float32),
+            pltpu.SemaphoreType.DMA((spans,)),
         ],
         compiler_params=vmem_params(KERNEL_VMEM),
-        cost_estimate=cost(2 * spans * row_blocks * side * cols * width, 2 * tiles.size),
+        cost_estimate=cost(4 * spans * row_blocks * side * cols * width, 2 * tiles.size),
         name="first_partial",
     )(slots, tiles, hist_slices, feats, replaced)
 
@@ -121,18 +142,44 @@
 def section_slices(array, parts):
     rows, cols = array.shape
     width = cols // parts
-    step = rows // 4
-
-    def kernel(in_ref, out_ref):
-        for part in range(parts):
-            out_ref[part] = in_ref[:, part * width : (part + 1) * width]
+    groups = 2
+    each = rows // groups
+
+    def kernel(in_ref, out_ref, held, in_sems, out_sems):
+        moves = []
+        for group in range(groups):
+            at = pl.ds(group * each, each)
+            for part in range(parts):
+                moves.append(
+                    (
+                        pltpu.make_async_copy(
+                            in_ref.at[at, pl.ds(part * width, width)],
+                            held.at[part, at],
+                            in_sems.at[part, group],
+                        ),
+                        pltpu.make_async_copy(
+                            held.at[part, at], out_ref.at[part, at], out_sems.at[part, group]
+                        ),
+                    )
+                )
+        for first, _ in moves:
+            first.start()
+        for first, second in moves:
+            first.wait()
+            second.start()
+        for _, second in moves:
+            second.wait()
 
     return pl.pallas_call(
         kernel,
         out_shape=jax.ShapeDtypeStruct((parts, rows, width), array.dtype),
-        grid=(rows // step,),
-        in_specs=[pl.BlockSpec((step, cols), lambda i: (i, 0))],
-        out_specs=pl.BlockSpec((parts, step, width), lambda i: (0, i, 0)),
+        in_specs=[IN_HBM],
+        out_specs=IN_HBM,
+        scratch_shapes=[
+            pltpu.VMEM((parts, rows, width), array.dtype),
+            pltpu.SemaphoreType.DMA((parts, groups)),
+            pltpu.SemaphoreType.DMA((parts, groups)),
+        ],
         compiler_params=vmem_params(KERNEL_VMEM),
         cost_estimate=cost(0, 4 * rows * cols),
         name="section_slices",
@@ -220,111 +267,108 @@
     )(arrived, initial)
 
 
-def static_parts(tiles, slots, hist_slices, replaced, select, which):
+def replaced_columns(tiles, slots, select):
+    spans, slot_count, side, _ = tiles.shape
+    cols, picks = select.shape
+    rows = slots.shape[1] // (cols // side) * side
+    rows_local = picks // spans
+
+    def kernel(slots_ref, tiles_ref, sel_ref, *refs):
+        column_refs, (held, tile_sems, sends) = refs[:spans], refs[spans : spans + 3]
+        kept = refs[spans + 3 :]
+        copies = tile_copies(tiles_ref, held, tile_sems)
+        for copy in copies:
+            copy.start()
+        outgoing = []
+        for span in range(spans):
+            used = (span + 1) * rows_local
+            held[span, slot_count] = jnp.zeros((side, side), jnp.bfloat16)
+            copies[span].wait()
+
+            def put(at, part, span=span):
+                kept[span][at] = part.astype(jnp.bfloat16)
+
+            multiply(held, slots_ref, span, sel_ref, used, put)
+            outgoing.append(pltpu.make_async_copy(kept[span], column_refs[span], sends.at[span]))
+            outgoing[-1].start()
+        for copy in outgoing:
+            copy.wait()
+
+    shapes = [(rows, (span + 1) * rows_local) for span in range(spans)]
+    return pl.pallas_call(
+        kernel,
+        out_shape=tuple(jax.ShapeDtypeStruct(shape, jnp.bfloat16) for shape in shapes),
+        in_specs=[IN_SMEM, IN_HBM, IN_VMEM],
+        out_specs=(IN_HBM,) * spans,
+        scratch_shapes=[
+            *tile_scratch(tiles),
+            pltpu.SemaphoreType.DMA((spans,)),
+            *[pltpu.VMEM(shape, jnp.bfloat16) for shape in shapes],
+        ],
+        compiler_params=vmem_params(KERNEL_VMEM),
+        cost_estimate=cost(2 * spans * rows * cols * picks, 2 * tiles.size + 6 * rows * picks),
+        name="replaced_columns",
+    )(slots, tiles, select)
+
+
+def static_parts(tiles, slots, hist_slices, replaced):
     spans, slot_count, side, _ = tiles.shape
     layers, cols, width = hist_slices.shape
-    col_blocks = cols // side
-    row_blocks = slots.shape[1] // col_blocks
-    rows = row_blocks * side
-    with_columns = which[0] == 1
-    rows_local = select.shape[1] // spans
-    picks = select.shape[1] if with_columns else 0
-    kinds = len(which)
+    rows = slots.shape[1] // (cols // side) * side
+    kinds = layers - 2
     stored = kinds * width
-    step = ROW_CHUNK // side
-    chunks = row_blocks // step
-
-    def kernel(slots_ref, tiles_ref, hist_ref, mask_ref, sel_ref, *refs):
+
+    def kernel(slots_ref, tiles_ref, hist_ref, mask_ref, *refs):
         static_refs = refs[:kinds]
-        column_refs = refs[kinds : kinds + (spans if with_columns else 0)]
-        held, tile_sems, hist, hist_sems, right, sums, sums_sems, cols_held, cols_sems = refs[-9:]
-        hist_copies = [
-            pltpu.make_async_copy(hist_ref.at[layer], hist.at[index], hist_sems.at[index])
-            for index, layer in enumerate(which)
-        ]
+        held, tile_sems, hist, hist_sem, right, sums, sends = refs[kinds:]
+        hist_copy = pltpu.make_async_copy(hist_ref.at[pl.ds(2, kinds)], hist, hist_sem)
         copies = tile_copies(tiles_ref, held, tile_sems)
-        for copy in hist_copies + copies:
+        for copy in [hist_copy] + copies:
             copy.start()
-        if with_columns:
-            right[:, stored:] = sel_ref[...]
-        for copy in hist_copies:
-            copy.wait()
-        def sent(span, chunk, used):
-            at = pl.ds(pl.multiple_of(chunk * ROW_CHUNK, ROW_CHUNK), ROW_CHUNK)
-            moves = [
-                pltpu.make_async_copy(
-                    sums.at[index, span, at],
-                    static_refs[index].at[span, at],
-                    sums_sems.at[index, span, chunk],
-                )
-                for index in range(kinds)
-            ]
-            if with_columns:
-                moves.append(
-                    pltpu.make_async_copy(
-                        cols_held.at[span, at, pl.ds(0, used)],
-                        column_refs[span].at[at],
-                        cols_sems.at[span, chunk],
-                    )
-                )
-            return moves
-
+        hist_copy.wait()
+        outgoing = []
         for span in range(spans):
             held[span, slot_count] = jnp.zeros((side, side), jnp.bfloat16)
             for index in range(kinds):
                 right[:, index * width : (index + 1) * width] = jnp.where(
                     mask_ref[span] > 0, jnp.zeros_like(hist[index]), hist[index]
                 )
-            used = (span + 1) * rows_local if with_columns else 0
             copies[span].wait()
 
-            @pl.loop(0, chunks)
-            def _(chunk):
-                left = rows_from(held, slots_ref, span, chunk * step, step, col_blocks)
-                part = jnp.dot(
-                    left, right[:, : stored + used], preferred_element_type=jnp.float32
-                )
-                at = pl.ds(pl.multiple_of(chunk * ROW_CHUNK, ROW_CHUNK), ROW_CHUNK)
+            def put(at, part, span=span):
                 for index in range(kinds):
                     sums[index, span, at] = part[:, index * width : (index + 1) * width]
-                if with_columns:
-                    cols_held[span, at, :used] = part[:, stored:].astype(jnp.bfloat16)
-                for move in sent(span, chunk, used):
-                    move.start()
-
-        for span in range(spans):
-            for chunk in range(chunks):
-                for move in sent(span, chunk, (span + 1) * rows_local):
-                    move.wait()
-
-    out_shape = [jax.ShapeDtypeStruct((spans, rows, width), jnp.float32) for _ in which]
-    if with_columns:
-        out_shape += [
-            jax.ShapeDtypeStruct((rows, (span + 1) * rows_local), jnp.bfloat16)
-            for span in range(spans)
-        ]
-    return pl.pallas_call(
-        kernel,
-        out_shape=tuple(out_shape),
-        in_specs=[IN_SMEM, IN_HBM, IN_HBM, IN_VMEM, IN_VMEM],
-        out_specs=tuple([IN_HBM] * len(out_shape)),
+
+            multiply(held, slots_ref, span, right, stored, put)
+            for index in range(kinds):
+                outgoing.append(
+                    pltpu.make_async_copy(
+                        sums.at[index, span], static_refs[index].at[span], sends.at[index, span]
+                    )
+                )
+                outgoing[-1].start()
+        for copy in outgoing:
+            copy.wait()
+
+    return pl.pallas_call(
+        kernel,
+        out_shape=(jax.ShapeDtypeStruct((spans, rows, width), jnp.float32),) * kinds,
+        in_specs=[IN_SMEM, IN_HBM, IN_HBM, IN_VMEM],
+        out_specs=(IN_HBM,) * kinds,
         scratch_shapes=[
             *tile_scratch(tiles),
             pltpu.VMEM((kinds, cols, width), jnp.bfloat16),
-            pltpu.SemaphoreType.DMA((kinds,)),
-            pltpu.VMEM((cols, stored + picks), jnp.bfloat16),
+            pltpu.SemaphoreType.DMA(()),
+            pltpu.VMEM((cols, stored), jnp.bfloat16),
             pltpu.VMEM((kinds, spans, rows, width), jnp.float32),
-            pltpu.SemaphoreType.DMA((kinds, spans, chunks)),
-            pltpu.VMEM((spans, rows, picks) if with_columns else (1, 16, 128), jnp.bfloat16),
-            pltpu.SemaphoreType.DMA((spans, chunks)),
+            pltpu.SemaphoreType.DMA((kinds, spans)),
         ],
         compiler_params=vmem_params(KERNEL_VMEM),
         cost_estimate=cost(
-            2 * spans * rows * cols * (stored + picks),
-            2 * tiles.size + spans * (4 * rows * stored + 2 * rows * picks),
+            2 * spans * rows * cols * stored, 2 * tiles.size + spans * 4 * rows * stored
         ),
         name="static_parts",
-    )(slots, tiles, hist_slices, replaced, select)
+    )(slots, tiles, hist_slices, replaced)
 
 
 def fill_left(left, gath_ref, section, halves, parts, width):
@@ -545,15 +589,15 @@
     slots = slot_count + jnp.sum(
         jnp.where(here, listed[:, :, None] - slot_count, 0), axis=1, dtype=jnp.int32
     )
-    hist_slices, replaced, feat_slice, initial, slots, select = lax.optimization_barrier(
-        (hist_slices, replaced, feat_slice, initial, slots, select)
+    columns = replaced_columns(tile_values, slots, select)
+    hist_slices, replaced, feat_slice, initial, slots, columns = lax.optimization_barrier(
+        (hist_slices, replaced, feat_slice, initial, slots, columns)
     )
-    partial = first_partial(tile_values, slots, hist_slices, feat_slice, replaced, row_devices)
+    partial, static_one = first_partial(
+        tile_values, slots, hist_slices, feat_slice, replaced, row_devices
+    )
     own_weights = after(weights[0], partial)
-    statics_one, *columns = static_parts(
-        tile_values, slots, after(hist_slices, partial), replaced, select, (1,)
-    )
-    statics = [statics_one]
+    statics = [static_one, *static_parts(tile_values, slots, after(hist_slices, partial), replaced)]
     by_distance = [
         lax.dynamic_slice_in_dim(own_weights, (section + by) % layers * width, width, 1)
         for by in range(layers)
@@ -569,19 +613,9 @@
             table = replace_rows(stored, ids, jnp.where(section == 0, initial_half, before))
         arrived = lax.all_to_all(partial, "vertex", 0, 0, tiled=True)
         if layer == 0:
-            arrived, statics, columns, weight_slices = lax.optimization_barrier(
-                (arrived, statics, columns, weight_slices)
+            arrived, statics, weight_slices = lax.optimization_barrier(
+                (arrived, statics, weight_slices)
             )
-        if layer == 1:
-            statics += static_parts(
-                tile_values,
-                slots,
-                after(hist_slices, partial),
-                replaced,
-                select,
-                tuple(range(2, layers)),
-            )
-            arrived, statics = lax.optimization_barrier((arrived, statics))
         if table is not None:
             arrived, table = lax.optimization_barrier((arrived, table))
         support = collect(arrived, initial)

time: 242 us -> 235 us (0.971)
  waiting for transfers between devices: 63.1 us -> 35.7 us
  blocking collectives: 47.4 us -> 73.3 us
  Pallas kernels: 81.6 us -> 77.1 us
    all_to_all x1 -> x2, blocking collectives: 25.9 us -> 51.7 us  [shards(): arrived = lax.all_to_all(partial, 'vertex', 0, 0, tiled=True)]
    all_to_all x1, waiting for transfers between devices: 18.3 us -> 3.6 us  [shards(): lax.all_to_all(section_slices(stored, layers), 'section', 0, 0, tiled=True)]
    all_to_all x3 -> x2, starting transfers between devices: 19.5 us -> 12.7 us  [shards(): arrived = lax.all_to_all(partial, 'vertex', 0, 0, tiled=True)]
    all_to_all x3 -> x2, waiting for transfers between devices: 13.2 us -> 6.46 us  [shards(): arrived = lax.all_to_all(partial, 'vertex', 0, 0, tiled=True)]
    ppermute x16, waiting for transfers between devices: 31.7 us -> 25.6 us  [rotated(): lax.ppermute(array, axis, [(i, (i + by) % devices) for i in range(devices)])]
    ppermute x16, starting transfers between devices: 11 us -> 16.5 us  [rotated(): lax.ppermute(array, axis, [(i, (i + by) % devices) for i in range(devices)])]
    pallas_call x3, Pallas kernels: 44.9 us -> 42.4 us  [the longest x1 14.4 us: first_partial(): pl.pallas_call(kernel, out_shape=(jax.ShapeDtypeStruct((row_devices, span...]
  transfers between devices with their start and end apart: 20 -> 19, of which waited for: 15 -> 15; matrix products, arithmetic and copies ran while one was open for 3% -> 3% of each run, Pallas kernels for 16% -> 15%
where the time goes in v1:
time: 235 us; the launch traced here: 234 us
  Pallas kernels  77.1 us (33%)
  blocking collectives  73.3 us (31%)
  waiting for transfers between devices  35.7 us (15%)
  starting transfers between devices  34 us (14%)
  local copies, waits for them, and re-layouts  9.66 us (4%)
  other arithmetic  2.85 us (1%)
    all_to_all x2, blocking collectives, shards(): arrived = lax.all_to_all(partial, 'vertex', 0, 0, tiled=True)  51.7 us
    ppermute x16, waiting for transfers between devices, rotated(): lax.ppermute(array, axis, [(i, (i + by) % devices) for i in range(devices)])  25.6 us
    all_gather x4, blocking collectives, shards(): gathered = lax.all_gather(near, 'feat', axis=0)  21.6 us
    pallas_call x3, Pallas kernels, layer_step(): pl.pallas_call(kernel, out_shape=jax.ShapeDtypeStruct((row_devices, spans...  18.2 us
    ppermute x16, starting transfers between devices, rotated(): lax.ppermute(array, axis, [(i, (i + by) % devices) for i in range(devices)])  16.5 us
    pallas_call x1, Pallas kernels, first_partial(): pl.pallas_call(kernel, out_shape=(jax.ShapeDtypeStruct((row_devices, span...  14.4 us
    pallas_call x1, Pallas kernels, static_parts(): pl.pallas_call(kernel, out_shape=(jax.ShapeDtypeStruct((spans, rows, widt...  14 us
    pallas_call x1, Pallas kernels, replaced_columns(): pl.pallas_call(kernel, out_shape=tuple((jax.ShapeDtypeStruct(shape, jnp.b...  14 us
  transfers between devices with their start and end apart: 19, of which 15 were waited for; matrix products, arithmetic and copies ran while one was open for 3% of the time, Pallas kernels for 15%

profile of v1, /device:TPU:1, one launch (start us, length us, event | category | flops | bytes accessed | tf_op | source)
XLA Modules:
  0.0 233.8 jit_solution(1735814712016485701)
XLA Ops:
  0.6 2.6 %section_slices.1 = bf16[4,2048,128]{2,1,0:T(8,128)(2,1)} custom-call(bf16[2048,512]{1,0:T(8,128)(2,1)} %bitcast.46), custom_call_target="tpu_custom_call" | custom-call | bytes 4194304 | tf_op jit(solution)/shard_map/section_slices/pallas_call | solution.py:173
  3.2 4.9 %all-to-all-start = ((bf16[4,2048,128]{2,1,0:T(8,128)(2,1)}), bf16[4,2048,128]{2,1,0:T(8,128)(2,1)}, u32[]{:S(2)}, u32[]{:S(2)}) async-start(bf16[4,2048,128]{2,1,0:T(8,128)(2,1)} %section_slices.1), calls=%async_computation | async-start | bytes 4194304 | tf_op jit(solution)/shard_map/all_to_all | solution.py:576
  8.1 1.2 selection.1
  9.4 1.1 copy-done.11
  10.5 1.2 copy-done.12
  11.7 2.1 gather_fusion
  16.4 14.0 %replaced_columns.1 = (bf16[2048,128]{1,0:T(8,128)(2,1)}, bf16[2048,256]{1,0:T(8,128)(2,1)}, bf16[2048,384]{1,0:T(8,128)(2,1)}) custom-call(s32[3,256]{1,0:T(4,128)} %broadcast_add_fusion.slots_ref, bf16[3,64,128,128]{3,2,1,0:T(8,128)(2,1)} %tiles_ref.5, bf16[2048,384]{1,0:T(8,128)(2,1)} %copy-done.12), custom_call_target="tpu_custom_call" | custom-call | flops 9663676416 | bytes 11010048 | tf_op jit(solution)/shard_map/replaced_columns/pallas_call | solution.py:298
  30.4 3.6 %all-to-all-done.hist_ref = bf16[4,2048,128]{2,1,0:T(8,128)(2,1)} async-done(((bf16[4,2048,128]{2,1,0:T(8,128)(2,1)}), bf16[4,2048,128]{2,1,0:T(8,128)(2,1)}, u32[]{:S(2)}, u32[]{:S(2)}) %all-to-all-start) | async-done | bytes 2097184 | tf_op jit(solution)/shard_map/all_to_all | solution.py:576
  34.0 14.4 %first_partial.1 = (bf16[16,3,128,128]{3,2,1,0:T(8,128)(2,1)}, f32[3,2048,128]{2,1,0:T(8,128)}) custom-call(s32[3,256]{1,0:T(4,128)} %broadcast_add_fusion.slots_ref, bf16[3,64,128,128]{3,2,1,0:T(8,128)(2,1)} %tiles_ref.5, bf16[4,2048,128]{2,1,0:T(8,128)(2,1)} %all-to-all-done.hist_ref, bf16[2048,128]{1,0:T(8,128)(2,1)} %constant_dynamic-slice_fusion.4.feat_ref, ...), custom_call_target="tpu_custom_call" | custom-call | flops 6442450944 | bytes 6291456 | tf_op jit(solution)/shard_map/first_partial/pallas_call | solution.py:118
  48.4 8.3 %all-to-all-start.1 = ((bf16[16,3,128,128]{3,2,1,0:T(8,128)(2,1)}), bf16[16,3,128,128]{3,2,1,0:T(8,128)(2,1)}, u32[]{:S(2)}, u32[]{:S(2)}) async-start(bf16[16,3,128,128]{3,2,1,0:T(8,128)(2,1)} %get-tuple-element.40), calls=%async_computation.1 | async-start | bytes 3145728 | tf_op jit(solution)/shard_map/all_to_all | solution.py:614
  57.9 1.8 collective-permute-start.1
  60.3 14.0 %static_parts.1 = (f32[3,2048,128]{2,1,0:T(8,128)}, f32[3,2048,128]{2,1,0:T(8,128)}) custom-call(s32[3,256]{1,0:T(4,128)} %broadcast_add_fusion.slots_ref, bf16[3,64,128,128]{3,2,1,0:T(8,128)(2,1)} %tiles_ref.5, bf16[4,2048,128]{2,1,0:T(8,128)(2,1)} %all-to-all-done.hist_ref, bf16[3,2048,128]{2,1,0:T(8,128)(2,1)} %copy-done.11), custom_call_target="tpu_custom_call" | custom-call | flops 6442450944 | bytes 12582912 | tf_op jit(solution)/shard_map/static_parts/pallas_call | solution.py:353
  74.4 3.1 %all-to-all-done.1.in_ref = bf16[16,3,128,128]{3,2,1,0:T(8,128)(2,1)} async-done(((bf16[16,3,128,128]{3,2,1,0:T(8,128)(2,1)}), bf16[16,3,128,128]{3,2,1,0:T(8,128)(2,1)}, u32[]{:S(2)}, u32[]{:S(2)}) %all-to-all-start.1) | async-done | bytes 1572896 | tf_op jit(solution)/shard_map/all_to_all | solution.py:614
  77.5 1.5 collect.4.sup_ref
  79.3 1.8 collective-permute-start.4
  82.4 2.4 %collective-permute-done.3 = bf16[384,128]{1,0:T(8,128)(2,1)S(1)} collective-permute-done((bf16[384,128]{1,0:T(8,128)(2,1)S(1)}, bf16[384,128]{1,0:T(8,128)(2,1)S(1)}, u32[]{:S(2)}, u32[]{:S(2)}) %collective-permute-start.3) | collective-permute-done | bytes 98336 | tf_op jit(solution)/shard_map/ppermute | solution.py:22
  85.4 7.4 %all-gather = bf16[8,384,128]{2,1,0:T(8,128)(2,1)} all-gather(bf16[4,384,128]{2,1,0:T(8,128)(2,1)S(1)} %pad_maximum_fusion), channel_id=2, replica_groups=mesh['section'=4,'vertex'=16,'feat'=2] {'feat'}, dimensions={0}, use_global_device_ids=true | all-gather | bytes 1179648 | tf_op jit(solution)/shard_map/all_gather | solution.py:623
  92.9 6.1 %layer_step.3 = bf16[16,3,128,128]{3,2,1,0:T(8,128)(2,1)} custom-call(s32[2]{0:T(128)} %pad_add_fusion.place_ref, bf16[2,4,384,128]{3,2,1,0:T(8,128)(2,1)} %bitcast.48, bf16[384,128]{1,0:T(8,128)(2,1)} %copy-done.7, f32[3,2048,128]{2,1,0:T(8,128)} %get-tuple-element.48.static_ref, bf16[1024,128]{1,0:T(8,128)(2,1)} %get-tuple-element.49.refs_0_, ...), custom_call_target="tpu_custom_call" | custom-call | flops 704643072 | bytes 9437184 | tf_op jit(solution)/shard_map/layer_step/pallas_call | solution.py:456
  98.9 25.8 %all_to_all.25.in_ref = bf16[16,3,128,128]{3,2,1,0:T(8,128)(2,1)S(1)} all-to-all(bf16[16,3,128,128]{3,2,1,0:T(8,128)(2,1)} %layer_step.3), channel_id=1, replica_groups=mesh['section'=4,'vertex'=16,'feat'=2] {'vertex'}, dimensions={0} | all-to-all | bytes 3145728 | tf_op jit(solution)/shard_map/all_to_all | solution.py:614
  124.7 1.0 collect.5.sup_ref
  126.4 2.7 %collective-permute-start.7 = (bf16[384,128]{1,0:T(8,128)(2,1)S(1)}, bf16[384,128]{1,0:T(8,128)(2,1)S(1)}, u32[]{:S(2)}, u32[]{:S(2)}) collective-permute-start(bf16[384,128]{1,0:T(8,128)(2,1)S(1)} %collect.5.sup_ref), channel_id=1, source_target_pairs={{0,64},{32,96},{64,0},{96,32},{1,65},{33,97},{65,1},{97,33},{2,66}... | collective-permute-start | bytes 294920 | tf_op jit(solution)/shard_map/ppermute | solution.py:22
  129.0 1.4 collective-permute-done.6
  130.5 1.7 collective-permute-done.7
  133.0 5.2 %all-gather.1 = bf16[8,384,128]{2,1,0:T(8,128)(2,1)} all-gather(bf16[4,384,128]{2,1,0:T(8,128)(2,1)S(1)} %pad_maximum_fusion.1), channel_id=3, replica_groups=mesh['section'=4,'vertex'=16,'feat'=2] {'feat'}, dimensions={0}, use_global_device_ids=true | all-gather | bytes 1179648 | tf_op jit(solution)/shard_map/all_gather | solution.py:623
  138.2 6.1 %layer_step.4 = bf16[16,3,128,128]{3,2,1,0:T(8,128)(2,1)} custom-call(s32[2]{0:T(128)} %pad_add_fusion.place_ref, bf16[2,4,384,128]{3,2,1,0:T(8,128)(2,1)} %bitcast.50, bf16[384,128]{1,0:T(8,128)(2,1)} %copy-done.8, f32[3,2048,128]{2,1,0:T(8,128)} %get-tuple-element.56.static_ref, bf16[1024,128]{1,0:T(8,128)(2,1)} %get-tuple-element.49.refs_0_, ...), custom_call_target="tpu_custom_call" | custom-call | flops 704643072 | bytes 9437184 | tf_op jit(solution)/shard_map/layer_step/pallas_call | solution.py:456
  144.3 26.0 %all_to_all.26.in_ref = bf16[16,3,128,128]{3,2,1,0:T(8,128)(2,1)S(1)} all-to-all(bf16[16,3,128,128]{3,2,1,0:T(8,128)(2,1)} %layer_step.4), channel_id=1, replica_groups=mesh['section'=4,'vertex'=16,'feat'=2] {'vertex'}, dimensions={0} | all-to-all | bytes 3145728 | tf_op jit(solution)/shard_map/all_to_all | solution.py:614
  170.2 1.0 collect.6.sup_ref
  171.4 2.9 %collective-permute-start.10 = (bf16[384,128]{1,0:T(8,128)(2,1)S(1)}, bf16[384,128]{1,0:T(8,128)(2,1)S(1)}, u32[]{:S(2)}, u32[]{:S(2)}) collective-permute-start(bf16[384,128]{1,0:T(8,128)(2,1)S(1)} %collect.6.sup_ref), channel_id=1, source_target_pairs={{0,64},{32,96},{64,0},{96,32},{1,65},{33,97},{65,1},{97,33},{2,66}... | collective-permute-start | bytes 294920 | tf_op jit(solution)/shard_map/ppermute | solution.py:22
  174.7 1.4 collective-permute-done.9
  176.0 1.4 collective-permute-done.10
  178.1 5.0 %all-gather.2 = bf16[8,384,128]{2,1,0:T(8,128)(2,1)} all-gather(bf16[4,384,128]{2,1,0:T(8,128)(2,1)S(1)} %pad_maximum_fusion.2), channel_id=4, replica_groups=mesh['section'=4,'vertex'=16,'feat'=2] {'feat'}, dimensions={0}, use_global_device_ids=true | all-gather | bytes 1179648 | tf_op jit(solution)/shard_map/all_gather | solution.py:623
  183.1 6.1 %layer_step.5 = bf16[16,3,128,128]{3,2,1,0:T(8,128)(2,1)} custom-call(s32[2]{0:T(128)} %pad_add_fusion.place_ref, bf16[2,4,384,128]{3,2,1,0:T(8,128)(2,1)} %bitcast.52, bf16[384,128]{1,0:T(8,128)(2,1)} %copy-done.6, f32[3,2048,128]{2,1,0:T(8,128)} %get-tuple-element.57.static_ref, bf16[1024,128]{1,0:T(8,128)(2,1)} %get-tuple-element.49.refs_0_, ...), custom_call_target="tpu_custom_call" | custom-call | flops 704643072 | bytes 9437184 | tf_op jit(solution)/shard_map/layer_step/pallas_call | solution.py:456
  189.2 4.4 %all-to-all-start.4 = ((bf16[16,3,128,128]{3,2,1,0:T(8,128)(2,1)}), bf16[16,3,128,128]{3,2,1,0:T(8,128)(2,1)}, u32[]{:S(2)}, u32[]{:S(2)}) async-start(bf16[16,3,128,128]{3,2,1,0:T(8,128)(2,1)} %layer_step.5), calls=%async_computation.4 | async-start | bytes 3145728 | tf_op jit(solution)/shard_map/all_to_all | solution.py:614
  193.7 1.1 copy-done.3
  194.8 1.2 whole_rows.4.refs_0_
  196.6 1.3 whole_rows.6.refs_0_
  198.8 10.9 %collective-permute-done.12 = bf16[384,512]{1,0:T(8,128)(2,1)} collective-permute-done((bf16[384,512]{1,0:T(8,128)(2,1)}, bf16[384,512]{1,0:T(8,128)(2,1)}, u32[]{:S(2)}, u32[]{:S(2)}) %collective-permute-start.12) | collective-permute-done | bytes 393248 | tf_op jit(solution)/shard_map/ppermute | solution.py:22
  209.8 1.1 broadcast_select_fusion.1.fresh_ref
  210.9 1.6 copy-done.2
  212.5 2.9 %replace_rows.1 = bf16[2048,512]{1,0:T(8,128)(2,1)} custom-call(bf16[2048,512]{1,0:T(8,128)(2,1)S(1)} %bitcast.47, s32[1,384]{1,0:T(1,128)S(1)} %bitcast.60, bf16[384,512]{1,0:T(8,128)(2,1)S(1)} %broadcast_select_fusion.1.fresh_ref), custom_call_target="tpu_custom_call" | custom-call | flops 805306368 | bytes 4194304 | tf_op jit(solution)/shard_map/replace_rows/pallas_call | solution.py:545
  215.4 3.4 %all-to-all-done.4.in_ref = bf16[16,3,128,128]{3,2,1,0:T(8,128)(2,1)} async-done(((bf16[16,3,128,128]{3,2,1,0:T(8,128)(2,1)}), bf16[16,3,128,128]{3,2,1,0:T(8,128)(2,1)}, u32[]{:S(2)}, u32[]{:S(2)}) %all-to-all-start.4) | async-done | bytes 1572896 | tf_op jit(solution)/shard_map/all_to_all | solution.py:614
  218.8 1.5 collect.7
  220.7 2.9 %collective-permute-start.14 = (bf16[384,128]{1,0:T(8,128)(2,1)S(1)}, bf16[384,128]{1,0:T(8,128)(2,1)S(1)}, u32[]{:S(2)}, u32[]{:S(2)}) collective-permute-start(bf16[384,128]{1,0:T(8,128)(2,1)S(1)} %collect.7), channel_id=1, source_target_pairs={{0,64},{32,96},{64,0},{96,32},{1,65},{33,97},{65,1},{97,33},{2,66}... | collective-permute-start | bytes 294920 | tf_op jit(solution)/shard_map/ppermute | solution.py:22
  223.6 1.4 collective-permute-done.13
  225.0 2.0 collective-permute-done.14
  227.0 1.0 collective-permute-done.15
  228.1 3.9 %all-gather.3 = bf16[8,384,128]{2,1,0:T(8,128)(2,1)S(1)} all-gather(bf16[4,384,128]{2,1,0:T(8,128)(2,1)S(1)} %pad_maximum_fusion.3), channel_id=5, replica_groups=mesh['section'=4,'vertex'=16,'feat'=2] {'feat'}, dimensions={0}, use_global_device_ids=true | all-gather | bytes 1179648 | tf_op jit(solution)/shard_map/all_gather | solution.py:623
  232.0 1.8 whole_rows.7
  (68 shorter events, 11.4 us)
Async XLA Ops:
  0.6 11.1 %copy-start = (bf16[2048,512]{1,0:T(8,128)(2,1)S(1)}, bf16[2048,512]{1,0:T(8,128)(2,1)}, u32[]{:S(2)}) copy-start(bf16[2048,512]{1,0:T(8,128)(2,1)} %param.9) | copy-start | bytes 6291460
  3.2 4.9 %copy-start.14 = (s32[3,128]{1,0:T(4,128)S(1)}, s32[3,128]{1,0:T(4,128)}, u32[]{:S(2)}) copy-start(s32[3,128]{1,0:T(4,128)} %param.16) | copy-start | bytes 4612
  3.2 30.7 %all-to-all-start = ((bf16[4,2048,128]{2,1,0:T(8,128)(2,1)}), bf16[4,2048,128]{2,1,0:T(8,128)(2,1)}, u32[]{:S(2)}, u32[]{:S(2)}) async-start(bf16[4,2048,128]{2,1,0:T(8,128)(2,1)} %section_slices.1), calls=%async_computation | async-start | bytes 4194304 | tf_op jit(solution)/shard_map/all_to_all | solution.py:576
  9.4 1.1 copy-start.11
  10.5 1.2 copy-start.12
  11.7 3.0 %copy-start.15 = (s32[3,64]{1,0:T(4,128)S(1)}, s32[3,64]{1,0:T(4,128)}, u32[]{:S(2)}) copy-start(s32[3,64]{1,0:T(4,128)} %param.14) | copy-start | bytes 2308
  11.7 3.0 %copy-start.16 = (s32[3,64]{1,0:T(4,128)S(1)}, s32[3,64]{1,0:T(4,128)}, u32[]{:S(2)}) copy-start(s32[3,64]{1,0:T(4,128)} %param.13) | copy-start | bytes 2308
  11.7 3.0 %copy-start.17 = (s32[3,1]{0,1:T(1,128)S(1)}, s32[3,1]{0,1:T(1,128)}, u32[]{:S(2)}) copy-start(s32[3,1]{0,1:T(1,128)} %param.15) | copy-start | bytes 40
  13.8 0.7 copy-start.13
  48.4 8.4 %copy-start.1 = (bf16[1,1024,512]{2,1,0:T(8,128)(2,1)S(1)}, bf16[1,1024,512]{2,1,0:T(8,128)(2,1)}, u32[]{:S(2)}) copy-start(bf16[1,1024,512]{2,1,0:T(8,128)(2,1)} %param.11) | copy-start | bytes 3145732
  48.4 29.1 %all-to-all-start.1 = ((bf16[16,3,128,128]{3,2,1,0:T(8,128)(2,1)}), bf16[16,3,128,128]{3,2,1,0:T(8,128)(2,1)}, u32[]{:S(2)}, u32[]{:S(2)}) async-start(bf16[16,3,128,128]{3,2,1,0:T(8,128)(2,1)} %get-tuple-element.40), calls=%async_computation.1 | async-start | bytes 3145728 | tf_op jit(solution)/shard_map/all_to_all | solution.py:614
  57.6 16.7 %collective-permute-start = (bf16[1024,128]{1,0:T(8,128)(2,1)S(1)}, bf16[1024,128]{1,0:T(8,128)(2,1)}, u32[]{:S(2)}, u32[]{:S(2)}) collective-permute-start(bf16[1024,128]{1,0:T(8,128)(2,1)S(1)} %get-tuple-element.62), channel_id=1, source_target_pairs={{0,32},{32,64},{64,96},{96,0},{1,33},{33,65},{65,97},{97,1},{2,34}... | collective-permute-start | bytes 786440 | tf_op jit(solution)/shard_map/ppermute | solution.py:22
  57.9 16.5 %collective-permute-start.1 = (bf16[1024,128]{1,0:T(8,128)(2,1)S(1)}, bf16[1024,128]{1,0:T(8,128)(2,1)}, u32[]{:S(2)}, u32[]{:S(2)}) collective-permute-start(bf16[1024,128]{1,0:T(8,128)(2,1)S(1)} %get-tuple-element.61), channel_id=1, source_target_pairs={{0,64},{32,96},{64,0},{96,32},{1,65},{33,97},{65,1},{97,33},{2,66}... | collective-permute-start | bytes 786440 | tf_op jit(solution)/shard_map/ppermute | solution.py:22
  59.7 14.7 %collective-permute-start.2 = (bf16[1024,128]{1,0:T(8,128)(2,1)S(1)}, bf16[1024,128]{1,0:T(8,128)(2,1)}, u32[]{:S(2)}, u32[]{:S(2)}) collective-permute-start(bf16[1024,128]{1,0:T(8,128)(2,1)S(1)} %get-tuple-element.60), channel_id=1, source_target_pairs={{0,96},{32,0},{64,32},{96,64},{1,97},{33,1},{65,33},{97,65},{2,98}... | collective-permute-start | bytes 786440 | tf_op jit(solution)/shard_map/ppermute | solution.py:22
  79.0 13.9 %copy-start.7 = (bf16[384,128]{1,0:T(8,128)(2,1)}, bf16[384,128]{1,0:T(8,128)(2,1)S(1)}, u32[]{:S(2)}) copy-start(bf16[384,128]{1,0:T(8,128)(2,1)S(1)} %collect.4.sup_ref) | copy-start | bytes 294916
  79.0 5.8 %collective-permute-start.3 = (bf16[384,128]{1,0:T(8,128)(2,1)S(1)}, bf16[384,128]{1,0:T(8,128)(2,1)S(1)}, u32[]{:S(2)}, u32[]{:S(2)}) collective-permute-start(bf16[384,128]{1,0:T(8,128)(2,1)S(1)} %collect.4.sup_ref), channel_id=1, source_target_pairs={{0,32},{32,64},{64,96},{96,0},{1,33},{33,65},{65,97},{97,1},{2,34}... | collective-permute-start | bytes 294920 | tf_op jit(solution)/shard_map/ppermute | solution.py:22
  79.3 5.5 %collective-permute-start.4 = (bf16[384,128]{1,0:T(8,128)(2,1)S(1)}, bf16[384,128]{1,0:T(8,128)(2,1)S(1)}, u32[]{:S(2)}, u32[]{:S(2)}) collective-permute-start(bf16[384,128]{1,0:T(8,128)(2,1)S(1)} %collect.4.sup_ref), channel_id=1, source_target_pairs={{0,64},{32,96},{64,0},{96,32},{1,65},{33,97},{65,1},{97,33},{2,66}... | collective-permute-start | bytes 294920 | tf_op jit(solution)/shard_map/ppermute | solution.py:22
  81.1 4.3 %collective-permute-start.5 = (bf16[384,128]{1,0:T(8,128)(2,1)S(1)}, bf16[384,128]{1,0:T(8,128)(2,1)S(1)}, u32[]{:S(2)}, u32[]{:S(2)}) collective-permute-start(bf16[384,128]{1,0:T(8,128)(2,1)S(1)} %collect.4.sup_ref), channel_id=1, source_target_pairs={{0,96},{32,0},{64,32},{96,64},{1,97},{33,1},{65,33},{97,65},{2,98}... | collective-permute-start | bytes 294920 | tf_op jit(solution)/shard_map/ppermute | solution.py:22
  125.7 12.5 %copy-start.8 = (bf16[384,128]{1,0:T(8,128)(2,1)}, bf16[384,128]{1,0:T(8,128)(2,1)S(1)}, u32[]{:S(2)}) copy-start(bf16[384,128]{1,0:T(8,128)(2,1)S(1)} %collect.5.sup_ref) | copy-start | bytes 294916
  125.7 4.7 %collective-permute-start.6 = (bf16[384,128]{1,0:T(8,128)(2,1)S(1)}, bf16[384,128]{1,0:T(8,128)(2,1)S(1)}, u32[]{:S(2)}, u32[]{:S(2)}) collective-permute-start(bf16[384,128]{1,0:T(8,128)(2,1)S(1)} %collect.5.sup_ref), channel_id=1, source_target_pairs={{0,32},{32,64},{64,96},{96,0},{1,33},{33,65},{65,97},{97,1},{2,34}... | collective-permute-start | bytes 294920 | tf_op jit(solution)/shard_map/ppermute | solution.py:22
  126.4 5.8 %collective-permute-start.7 = (bf16[384,128]{1,0:T(8,128)(2,1)S(1)}, bf16[384,128]{1,0:T(8,128)(2,1)S(1)}, u32[]{:S(2)}, u32[]{:S(2)}) collective-permute-start(bf16[384,128]{1,0:T(8,128)(2,1)S(1)} %collect.5.sup_ref), channel_id=1, source_target_pairs={{0,64},{32,96},{64,0},{96,32},{1,65},{33,97},{65,1},{97,33},{2,66}... | collective-permute-start | bytes 294920 | tf_op jit(solution)/shard_map/ppermute | solution.py:22
  129.0 3.9 %collective-permute-start.8 = (bf16[384,128]{1,0:T(8,128)(2,1)S(1)}, bf16[384,128]{1,0:T(8,128)(2,1)S(1)}, u32[]{:S(2)}, u32[]{:S(2)}) collective-permute-start(bf16[384,128]{1,0:T(8,128)(2,1)S(1)} %collect.5.sup_ref), channel_id=1, source_target_pairs={{0,96},{32,0},{64,32},{96,64},{1,97},{33,1},{65,33},{97,65},{2,98}... | collective-permute-start | bytes 294920 | tf_op jit(solution)/shard_map/ppermute | solution.py:22
  171.3 11.8 %copy-start.6 = (bf16[384,128]{1,0:T(8,128)(2,1)}, bf16[384,128]{1,0:T(8,128)(2,1)S(1)}, u32[]{:S(2)}) copy-start(bf16[384,128]{1,0:T(8,128)(2,1)S(1)} %collect.6.sup_ref) | copy-start | bytes 294916
  171.3 4.7 %collective-permute-start.9 = (bf16[384,128]{1,0:T(8,128)(2,1)S(1)}, bf16[384,128]{1,0:T(8,128)(2,1)S(1)}, u32[]{:S(2)}, u32[]{:S(2)}) collective-permute-start(bf16[384,128]{1,0:T(8,128)(2,1)S(1)} %collect.6.sup_ref), channel_id=1, source_target_pairs={{0,32},{32,64},{64,96},{96,0},{1,33},{33,65},{65,97},{97,1},{2,34}... | collective-permute-start | bytes 294920 | tf_op jit(solution)/shard_map/ppermute | solution.py:22
  171.4 6.0 %collective-permute-start.10 = (bf16[384,128]{1,0:T(8,128)(2,1)S(1)}, bf16[384,128]{1,0:T(8,128)(2,1)S(1)}, u32[]{:S(2)}, u32[]{:S(2)}) collective-permute-start(bf16[384,128]{1,0:T(8,128)(2,1)S(1)} %collect.6.sup_ref), channel_id=1, source_target_pairs={{0,64},{32,96},{64,0},{96,32},{1,65},{33,97},{65,1},{97,33},{2,66}... | collective-permute-start | bytes 294920 | tf_op jit(solution)/shard_map/ppermute | solution.py:22
  174.2 3.8 %collective-permute-start.11 = (bf16[384,128]{1,0:T(8,128)(2,1)S(1)}, bf16[384,128]{1,0:T(8,128)(2,1)S(1)}, u32[]{:S(2)}, u32[]{:S(2)}) collective-permute-start(bf16[384,128]{1,0:T(8,128)(2,1)S(1)} %collect.6.sup_ref), channel_id=1, source_target_pairs={{0,96},{32,0},{64,32},{96,64},{1,97},{33,1},{65,33},{97,65},{2,98}... | collective-permute-start | bytes 294920 | tf_op jit(solution)/shard_map/ppermute | solution.py:22
  189.2 4.4 %copy-start.9 = (s32[2]{0:T(128)S(1)}, s32[2]{0:T(128)}, u32[]{:S(2)}) copy-start(s32[2]{0:T(128)} %pad_add_fusion.place_ref) | copy-start | bytes 28
  189.2 4.4 %copy-start.10 = (f32[4]{0:T(128)S(1)}, f32[4]{0:T(128)}, u32[]{:S(2)}) copy-start(f32[4]{0:T(128)} %constant.71.clone.betas_ref) | copy-start | bytes 52
  189.2 29.6 %all-to-all-start.4 = ((bf16[16,3,128,128]{3,2,1,0:T(8,128)(2,1)}), bf16[16,3,128,128]{3,2,1,0:T(8,128)(2,1)}, u32[]{:S(2)}, u32[]{:S(2)}) async-start(bf16[16,3,128,128]{3,2,1,0:T(8,128)(2,1)} %layer_step.5), calls=%async_computation.4 | async-start | bytes 3145728 | tf_op jit(solution)/shard_map/all_to_all | solution.py:614
  193.7 1.1 copy-start.3
  194.8 1.2 copy-start.4
  194.8 1.8 copy-start.5
  197.9 11.9 %collective-permute-start.12 = (bf16[384,512]{1,0:T(8,128)(2,1)}, bf16[384,512]{1,0:T(8,128)(2,1)}, u32[]{:S(2)}, u32[]{:S(2)}) collective-permute-start(bf16[384,512]{1,0:T(8,128)(2,1)} %whole_rows.6.refs_0_), channel_id=1, source_target_pairs={{0,32},{32,64},{64,96},{96,0},{1,33},{33,65},{65,97},{97,1},{2,34}... | collective-permute-start | bytes 1179656 | tf_op jit(solution)/shard_map/ppermute | solution.py:22
  210.9 1.6 copy-start.2
  220.2 4.7 %collective-permute-start.13 = (bf16[384,128]{1,0:T(8,128)(2,1)S(1)}, bf16[384,128]{1,0:T(8,128)(2,1)S(1)}, u32[]{:S(2)}, u32[]{:S(2)}) collective-permute-start(bf16[384,128]{1,0:T(8,128)(2,1)S(1)} %collect.7), channel_id=1, source_target_pairs={{0,32},{32,64},{64,96},{96,0},{1,33},{33,65},{65,97},{97,1},{2,34}... | collective-permute-start | bytes 294920 | tf_op jit(solution)/shard_map/ppermute | solution.py:22
  220.7 6.3 %collective-permute-start.14 = (bf16[384,128]{1,0:T(8,128)(2,1)S(1)}, bf16[384,128]{1,0:T(8,128)(2,1)S(1)}, u32[]{:S(2)}, u32[]{:S(2)}) collective-permute-start(bf16[384,128]{1,0:T(8,128)(2,1)S(1)} %collect.7), channel_id=1, source_target_pairs={{0,64},{32,96},{64,0},{96,32},{1,65},{33,97},{65,1},{97,33},{2,66}... | collective-permute-start | bytes 294920 | tf_op jit(solution)/shard_map/ppermute | solution.py:22
  223.6 4.4 %collective-permute-start.15 = (bf16[384,128]{1,0:T(8,128)(2,1)S(1)}, bf16[384,128]{1,0:T(8,128)(2,1)S(1)}, u32[]{:S(2)}, u32[]{:S(2)}) collective-permute-start(bf16[384,128]{1,0:T(8,128)(2,1)S(1)} %collect.7), channel_id=1, source_target_pairs={{0,96},{32,0},{64,32},{96,64},{1,97},{33,1},{65,33},{97,65},{2,98}... | collective-permute-start | bytes 294920 | tf_op jit(solution)/shard_map/ppermute | solution.py:22

commit v2 on v1

--- a/solution.py
+++ b/solution.py
@@ -46,17 +46,22 @@
     return jnp.concatenate(lines, axis=0)
 
 
-def multiply(tiles_ref, slots_ref, span, right, width, put):
+def multiply(tiles_ref, slots_ref, span, right, width, put, unrolled=False):
     side = tiles_ref.shape[-1]
     col_blocks = right.shape[0] // side
     row_blocks = slots_ref.shape[1] // col_blocks
     step = ROW_CHUNK // side
 
-    @pl.loop(0, row_blocks, step=step)
-    def _(first):
+    def chunk(first):
         left = rows_from(tiles_ref, slots_ref, span, first, step, col_blocks)
         part = jnp.dot(left, right[:, :width], preferred_element_type=jnp.float32)
         put(pl.ds(pl.multiple_of(first * side, side), ROW_CHUNK), part)
+
+    if unrolled:
+        for first in range(0, row_blocks, step):
+            chunk(first)
+    else:
+        pl.loop(0, row_blocks, step=step)(chunk)
 
 
 def tile_copies(tiles_ref, held, sems):
@@ -98,7 +103,7 @@
                 sums[span, at] = part[:, :width].astype(jnp.bfloat16)
                 static[span, at] = part[:, width:]
 
-            multiply(held, slots_ref, span, table, 2 * width, put)
+            multiply(held, slots_ref, span, table, 2 * width, put, unrolled=True)
             outgoing.append(
                 pltpu.make_async_copy(static.at[span], static_ref.at[span], static_sems.at[span])
             )
@@ -379,13 +384,16 @@
             left[:, first : first + width] = gath_ref[half, place]
 
 
-def layer_step(place, gathered, support, slices, static, columns, layer, beta, row_devices):
+def layer_step(place, gathered, support, slices, static, columns, layer, beta, row_devices, resident):
     halves, parts, picks, width = gathered.shape
     spans, rows, _ = static.shape
     rows_local = rows // row_devices
     depth = halves * parts * width
     step = ROW_CHUNK // rows_local
     chunks = row_devices // step
+
+    heavy = IN_VMEM if resident else IN_HBM
+    small = (1, 16, 128)
 
     def kernel(place_ref, gath_ref, sup_ref, static_ref, *refs):
         slice_refs, column_refs = refs[:parts], refs[parts : parts + spans]
@@ -412,15 +420,18 @@
             def _():
                 pltpu.make_async_copy(slice_refs[by], right, right_sem).start()
 
-        later = []
-        for span in range(spans):
-            pair = (
-                pltpu.make_async_copy(column_refs[span], cols[span], cols_sems.at[span]),
-                pltpu.make_async_copy(static_ref.at[span], stat.at[span], stat_sems.at[span]),
-            )
-            for copy in pair:
-                copy.start()
-            later.append(pair)
+        later = [()] * spans
+        if resident:
+            cols, stat = column_refs, static_ref
+        else:
+            for span in range(spans):
+                later[span] = (
+                    pltpu.make_async_copy(column_refs[span], cols[span], cols_sems.at[span]),
+                    pltpu.make_async_copy(static_ref.at[span], stat.at[span], stat_sems.at[span]),
+                )
+                for copy in later[span]:
+                    copy.start()
+
         for copy in incoming:
             copy.wait()
         pltpu.make_async_copy(slice_refs[0], right, right_sem).wait()
@@ -456,7 +467,7 @@
     return pl.pallas_call(
         kernel,
         out_shape=jax.ShapeDtypeStruct((row_devices, spans, rows_local, width), jnp.bfloat16),
-        in_specs=[IN_SMEM] + [IN_HBM] * (3 + parts + spans),
+        in_specs=[IN_SMEM, IN_HBM, IN_HBM, heavy] + [IN_HBM] * parts + [heavy] * spans,
         out_specs=IN_HBM,
         scratch_shapes=[
             pltpu.VMEM((picks, depth), jnp.bfloat16),
@@ -465,14 +476,14 @@
             pltpu.SemaphoreType.DMA(()),
             pltpu.VMEM((depth, width), jnp.bfloat16),
             pltpu.SemaphoreType.DMA(()),
-            pltpu.VMEM(static.shape, jnp.float32),
+            pltpu.VMEM(small if resident else static.shape, jnp.float32),
             pltpu.SemaphoreType.DMA((spans,)),
             pltpu.SemaphoreType.DMA((spans,)),
             pltpu.VMEM((spans, row_devices, rows_local, width), jnp.bfloat16),
             pltpu.SemaphoreType.DMA((spans, chunks)),
-            *[pltpu.VMEM(each.shape, jnp.bfloat16) for each in columns],
-        ],
-        compiler_params=vmem_params(KERNEL_VMEM),
+            *[pltpu.VMEM(small if resident else each.shape, jnp.bfloat16) for each in columns],
+        ],
+        compiler_params=vmem_params(16 if resident else KERNEL_VMEM),
         cost_estimate=cost(
             2 * picks * depth * width + 2 * spans * rows * width * picks,
             6 * spans * rows * width + 2 * spans * rows * picks,
@@ -632,6 +643,7 @@
                 layer,
                 betas[layer],
                 row_devices,
+                layer > 0,
             )
         rows_kept = whole_rows(place, beta_table, gathered, own_weights, rows_kept, layer)
     return (rows_kept.reshape(1, spans, rows_local, half), table[None])

time: 235 us -> 233 us (level)
  Pallas kernels: 77.1 us -> 73.7 us
    pallas_call x3, Pallas kernels: 18.2 us -> 15.7 us  [layer_step(): pl.pallas_call(kernel, out_shape=jax.ShapeDtypeStruct((row_devices, spans...]
    unnamed x37 -> x51, local copies, waits for them, and re-layouts: 5.85 us -> 7.88 us
where the time goes in v2:
time: 233 us; the launch traced here: 232 us
  Pallas kernels  73.7 us (32%)
  blocking collectives  72.4 us (31%)
  waiting for transfers between devices  35.7 us (15%)
  starting transfers between devices  34.1 us (15%)
  local copies, waits for them, and re-layouts  11.7 us (5%)
  other arithmetic  2.84 us (1%)
    all_to_all x2, blocking collectives, shards(): arrived = lax.all_to_all(partial, 'vertex', 0, 0, tiled=True)  50.7 us
    ppermute x16, waiting for transfers between devices, rotated(): lax.ppermute(array, axis, [(i, (i + by) % devices) for i in range(devices)])  25.7 us
    all_gather x4, blocking collectives, shards(): gathered = lax.all_gather(near, 'feat', axis=0)  21.8 us
    ppermute x16, starting transfers between devices, rotated(): lax.ppermute(array, axis, [(i, (i + by) % devices) for i in range(devices)])  16.4 us
    pallas_call x3, Pallas kernels, layer_step(): pl.pallas_call(kernel, out_shape=jax.ShapeDtypeStruct((row_devices, spans...  15.7 us
    pallas_call x1, Pallas kernels, static_parts(): pl.pallas_call(kernel, out_shape=(jax.ShapeDtypeStruct((spans, rows, widt...  14 us
    pallas_call x1, Pallas kernels, replaced_columns(): pl.pallas_call(kernel, out_shape=tuple((jax.ShapeDtypeStruct(shape, jnp.b...  14 us
    pallas_call x1, Pallas kernels, first_partial(): pl.pallas_call(kernel, out_shape=(jax.ShapeDtypeStruct((row_devices, span...  13.4 us
  transfers between devices with their start and end apart: 19, of which 15 were waited for; matrix products, arithmetic and copies ran while one was open for 3% of the time, Pallas kernels for 15%

profile of v2, /device:TPU:1, one launch (start us, length us, event | category | flops | bytes accessed | tf_op | source)
XLA Modules:
  0.0 231.7 jit_solution(1496834811197664181)
XLA Ops:
  0.6 2.6 %section_slices.1 = bf16[4,2048,128]{2,1,0:T(8,128)(2,1)} custom-call(bf16[2048,512]{1,0:T(8,128)(2,1)} %bitcast.46), custom_call_target="tpu_custom_call" | custom-call | bytes 4194304 | tf_op jit(solution)/shard_map/section_slices/pallas_call | solution.py:178
  3.2 4.9 %all-to-all-start = ((bf16[4,2048,128]{2,1,0:T(8,128)(2,1)}), bf16[4,2048,128]{2,1,0:T(8,128)(2,1)}, u32[]{:S(2)}, u32[]{:S(2)}) async-start(bf16[4,2048,128]{2,1,0:T(8,128)(2,1)} %section_slices.1), calls=%async_computation | async-start | bytes 4194304 | tf_op jit(solution)/shard_map/all_to_all | solution.py:587
  8.1 1.2 selection.1
  9.4 1.1 copy-done.18
  10.5 1.2 copy-done.19
  11.7 2.1 gather_fusion
  16.4 14.0 %replaced_columns.1 = (bf16[2048,128]{1,0:T(8,128)(2,1)}, bf16[2048,256]{1,0:T(8,128)(2,1)}, bf16[2048,384]{1,0:T(8,128)(2,1)}) custom-call(s32[3,256]{1,0:T(4,128)} %broadcast_add_fusion.slots_ref, bf16[3,64,128,128]{3,2,1,0:T(8,128)(2,1)} %tiles_ref.5, bf16[2048,384]{1,0:T(8,128)(2,1)} %copy-done.19), custom_call_target="tpu_custom_call" | custom-call | flops 9663676416 | bytes 11010048 | tf_op jit(solution)/shard_map/replaced_columns/pallas_call | solution.py:303
  30.4 3.5 %all-to-all-done.hist_ref = bf16[4,2048,128]{2,1,0:T(8,128)(2,1)} async-done(((bf16[4,2048,128]{2,1,0:T(8,128)(2,1)}), bf16[4,2048,128]{2,1,0:T(8,128)(2,1)}, u32[]{:S(2)}, u32[]{:S(2)}) %all-to-all-start) | async-done | bytes 2097184 | tf_op jit(solution)/shard_map/all_to_all | solution.py:587
  33.9 13.4 %first_partial.1 = (bf16[16,3,128,128]{3,2,1,0:T(8,128)(2,1)}, f32[3,2048,128]{2,1,0:T(8,128)}) custom-call(s32[3,256]{1,0:T(4,128)} %broadcast_add_fusion.slots_ref, bf16[3,64,128,128]{3,2,1,0:T(8,128)(2,1)} %tiles_ref.5, bf16[4,2048,128]{2,1,0:T(8,128)(2,1)} %all-to-all-done.hist_ref, bf16[2048,128]{1,0:T(8,128)(2,1)} %constant_dynamic-slice_fusion.4.feat_ref, ...), custom_call_target="tpu_custom_call" | custom-call | flops 6442450944 | bytes 6291456 | tf_op jit(solution)/shard_map/first_partial/pallas_call | solution.py:123
  47.4 8.4 %all-to-all-start.1 = ((bf16[16,3,128,128]{3,2,1,0:T(8,128)(2,1)}), bf16[16,3,128,128]{3,2,1,0:T(8,128)(2,1)}, u32[]{:S(2)}, u32[]{:S(2)}) async-start(bf16[16,3,128,128]{3,2,1,0:T(8,128)(2,1)} %get-tuple-element.40), calls=%async_computation.1 | async-start | bytes 3145728 | tf_op jit(solution)/shard_map/all_to_all | solution.py:625
  57.0 1.8 collective-permute-start.1
  59.4 14.0 %static_parts.1 = (f32[3,2048,128]{2,1,0:T(8,128)}, f32[3,2048,128]{2,1,0:T(8,128)}) custom-call(s32[3,256]{1,0:T(4,128)} %broadcast_add_fusion.slots_ref, bf16[3,64,128,128]{3,2,1,0:T(8,128)(2,1)} %tiles_ref.5, bf16[4,2048,128]{2,1,0:T(8,128)(2,1)} %all-to-all-done.hist_ref, bf16[3,2048,128]{2,1,0:T(8,128)(2,1)} %copy-done.18), custom_call_target="tpu_custom_call" | custom-call | flops 6442450944 | bytes 12582912 | tf_op jit(solution)/shard_map/static_parts/pallas_call | solution.py:358
  73.5 3.1 %all-to-all-done.1.in_ref = bf16[16,3,128,128]{3,2,1,0:T(8,128)(2,1)} async-done(((bf16[16,3,128,128]{3,2,1,0:T(8,128)(2,1)}), bf16[16,3,128,128]{3,2,1,0:T(8,128)(2,1)}, u32[]{:S(2)}, u32[]{:S(2)}) %all-to-all-start.1) | async-done | bytes 1572896 | tf_op jit(solution)/shard_map/all_to_all | solution.py:625
  76.5 1.5 collect.4.sup_ref
  78.4 1.8 collective-permute-start.4
  81.4 2.4 %collective-permute-done.3 = bf16[384,128]{1,0:T(8,128)(2,1)S(1)} collective-permute-done((bf16[384,128]{1,0:T(8,128)(2,1)S(1)}, bf16[384,128]{1,0:T(8,128)(2,1)S(1)}, u32[]{:S(2)}, u32[]{:S(2)}) %collective-permute-start.3) | collective-permute-done | bytes 98336 | tf_op jit(solution)/shard_map/ppermute | solution.py:22
  84.5 7.4 %all-gather = bf16[8,384,128]{2,1,0:T(8,128)(2,1)} all-gather(bf16[4,384,128]{2,1,0:T(8,128)(2,1)S(1)} %pad_maximum_fusion), channel_id=2, replica_groups=mesh['section'=4,'vertex'=16,'feat'=2] {'feat'}, dimensions={0}, use_global_device_ids=true | all-gather | bytes 1179648 | tf_op jit(solution)/shard_map/all_gather | solution.py:634
  91.9 6.1 %layer_step.3 = bf16[16,3,128,128]{3,2,1,0:T(8,128)(2,1)} custom-call(s32[2]{0:T(128)} %pad_add_fusion.place_ref, bf16[2,4,384,128]{3,2,1,0:T(8,128)(2,1)} %bitcast.48, bf16[384,128]{1,0:T(8,128)(2,1)} %copy-done.15, f32[3,2048,128]{2,1,0:T(8,128)} %get-tuple-element.48.static_ref, bf16[1024,128]{1,0:T(8,128)(2,1)} %get-tuple-element.49.refs_0_, ...), custom_call_target="tpu_custom_call" | custom-call | flops 704643072 | bytes 9437184 | tf_op jit(solution)/shard_map/layer_step/pallas_call | solution.py:467
  98.0 26.1 %all_to_all.25.in_ref = bf16[16,3,128,128]{3,2,1,0:T(8,128)(2,1)S(1)} all-to-all(bf16[16,3,128,128]{3,2,1,0:T(8,128)(2,1)} %layer_step.3), channel_id=1, replica_groups=mesh['section'=4,'vertex'=16,'feat'=2] {'vertex'}, dimensions={0} | all-to-all | bytes 3145728 | tf_op jit(solution)/shard_map/all_to_all | solution.py:625
  124.0 1.0 collect.5.sup_ref
  125.7 2.7 %collective-permute-start.7 = (bf16[384,128]{1,0:T(8,128)(2,1)S(1)}, bf16[384,128]{1,0:T(8,128)(2,1)S(1)}, u32[]{:S(2)}, u32[]{:S(2)}) collective-permute-start(bf16[384,128]{1,0:T(8,128)(2,1)S(1)} %collect.5.sup_ref), channel_id=1, source_target_pairs={{0,64},{32,96},{64,0},{96,32},{1,65},{33,97},{65,1},{97,33},{2,66}... | collective-permute-start | bytes 294920 | tf_op jit(solution)/shard_map/ppermute | solution.py:22
  128.4 1.4 collective-permute-done.6
  129.8 1.7 collective-permute-done.7
  132.3 5.0 %all-gather.1 = bf16[8,384,128]{2,1,0:T(8,128)(2,1)S(1)} all-gather(bf16[4,384,128]{2,1,0:T(8,128)(2,1)S(1)} %pad_maximum_fusion.1), channel_id=3, replica_groups=mesh['section'=4,'vertex'=16,'feat'=2] {'feat'}, dimensions={0}, use_global_device_ids=true | all-gather | bytes 1179648 | tf_op jit(solution)/shard_map/all_gather | solution.py:634
  137.4 4.8 %layer_step.4 = bf16[16,3,128,128]{3,2,1,0:T(8,128)(2,1)S(1)} custom-call(s32[2]{0:T(128)S(1)} %copy-done.16, bf16[2,4,384,128]{3,2,1,0:T(8,128)(2,1)S(1)} %bitcast.50, bf16[384,128]{1,0:T(8,128)(2,1)S(1)} %collect.5.sup_ref, f32[3,2048,128]{2,1,0:T(8,128)S(1)} %copy-done.14, bf16[1024,128]{1,0:T(8,128)(2,1)S(1)} %copy-done.12, ...), custom_call_target="tpu_custom_call" | custom-call | flops 704643072 | bytes 9437184 | tf_op jit(solution)/shard_map/layer_step/pallas_call | solution.py:467
  142.3 24.6 %all_to_all.26.in_ref = bf16[16,3,128,128]{3,2,1,0:T(8,128)(2,1)S(1)} all-to-all(bf16[16,3,128,128]{3,2,1,0:T(8,128)(2,1)S(1)} %layer_step.4), channel_id=1, replica_groups=mesh['section'=4,'vertex'=16,'feat'=2] {'vertex'}, dimensions={0} | all-to-all | bytes 3145728 | tf_op jit(solution)/shard_map/all_to_all | solution.py:625
  166.9 1.0 collect.6.sup_ref
  168.2 3.0 %collective-permute-start.10 = (bf16[384,128]{1,0:T(8,128)(2,1)S(1)}, bf16[384,128]{1,0:T(8,128)(2,1)S(1)}, u32[]{:S(2)}, u32[]{:S(2)}) collective-permute-start(bf16[384,128]{1,0:T(8,128)(2,1)S(1)} %collect.6.sup_ref), channel_id=1, source_target_pairs={{0,64},{32,96},{64,0},{96,32},{1,65},{33,97},{65,1},{97,33},{2,66}... | collective-permute-start | bytes 294920 | tf_op jit(solution)/shard_map/ppermute | solution.py:22
  171.5 1.4 collective-permute-done.9
  172.9 1.4 collective-permute-done.10
  175.0 5.2 %all-gather.2 = bf16[8,384,128]{2,1,0:T(8,128)(2,1)S(1)} all-gather(bf16[4,384,128]{2,1,0:T(8,128)(2,1)S(1)} %pad_maximum_fusion.2), channel_id=4, replica_groups=mesh['section'=4,'vertex'=16,'feat'=2] {'feat'}, dimensions={0}, use_global_device_ids=true | all-gather | bytes 1179648 | tf_op jit(solution)/shard_map/all_gather | solution.py:634
  180.2 4.8 %layer_step.5 = bf16[16,3,128,128]{3,2,1,0:T(8,128)(2,1)S(1)} custom-call(s32[2]{0:T(128)S(1)} %copy-done.16, bf16[2,4,384,128]{3,2,1,0:T(8,128)(2,1)S(1)} %bitcast.52, bf16[384,128]{1,0:T(8,128)(2,1)S(1)} %collect.6.sup_ref, f32[3,2048,128]{2,1,0:T(8,128)S(1)} %copy-done.13, bf16[1024,128]{1,0:T(8,128)(2,1)S(1)} %copy-done.12, ...), custom_call_target="tpu_custom_call" | custom-call | flops 704643072 | bytes 9437184 | tf_op jit(solution)/shard_map/layer_step/pallas_call | solution.py:467
  185.9 1.2 copy-done.10
  187.1 4.5 %all-to-all-start.4 = ((bf16[16,3,128,128]{3,2,1,0:T(8,128)(2,1)}), bf16[16,3,128,128]{3,2,1,0:T(8,128)(2,1)}, u32[]{:S(2)}, u32[]{:S(2)}) async-start(bf16[16,3,128,128]{3,2,1,0:T(8,128)(2,1)} %copy-done.10), calls=%async_computation.4 | async-start | bytes 3145728 | tf_op jit(solution)/shard_map/all_to_all | solution.py:625
  191.7 1.1 copy-done.5
  192.8 1.2 whole_rows.4.refs_0_
  194.6 1.3 whole_rows.6.refs_0_
  196.7 11.1 %collective-permute-done.12 = bf16[384,512]{1,0:T(8,128)(2,1)} collective-permute-done((bf16[384,512]{1,0:T(8,128)(2,1)}, bf16[384,512]{1,0:T(8,128)(2,1)}, u32[]{:S(2)}, u32[]{:S(2)}) %collective-permute-start.12) | collective-permute-done | bytes 393248 | tf_op jit(solution)/shard_map/ppermute | solution.py:22
  207.8 1.1 broadcast_select_fusion.1.fresh_ref
  208.9 1.6 copy-done.4
  210.5 2.9 %replace_rows.1 = bf16[2048,512]{1,0:T(8,128)(2,1)} custom-call(bf16[2048,512]{1,0:T(8,128)(2,1)S(1)} %bitcast.47, s32[1,384]{1,0:T(1,128)S(1)} %bitcast.60, bf16[384,512]{1,0:T(8,128)(2,1)S(1)} %broadcast_select_fusion.1.fresh_ref), custom_call_target="tpu_custom_call" | custom-call | flops 805306368 | bytes 4194304 | tf_op jit(solution)/shard_map/replace_rows/pallas_call | solution.py:556
  213.4 3.4 %all-to-all-done.4.in_ref = bf16[16,3,128,128]{3,2,1,0:T(8,128)(2,1)} async-done(((bf16[16,3,128,128]{3,2,1,0:T(8,128)(2,1)}), bf16[16,3,128,128]{3,2,1,0:T(8,128)(2,1)}, u32[]{:S(2)}, u32[]{:S(2)}) %all-to-all-start.4) | async-done | bytes 1572896 | tf_op jit(solution)/shard_map/all_to_all | solution.py:625
  216.8 1.5 collect.7
  218.6 2.9 %collective-permute-start.14 = (bf16[384,128]{1,0:T(8,128)(2,1)S(1)}, bf16[384,128]{1,0:T(8,128)(2,1)S(1)}, u32[]{:S(2)}, u32[]{:S(2)}) collective-permute-start(bf16[384,128]{1,0:T(8,128)(2,1)S(1)} %collect.7), channel_id=1, source_target_pairs={{0,64},{32,96},{64,0},{96,32},{1,65},{33,97},{65,1},{97,33},{2,66}... | collective-permute-start | bytes 294920 | tf_op jit(solution)/shard_map/ppermute | solution.py:22
  221.5 1.6 collective-permute-done.13
  223.0 1.9 collective-permute-done.14
  225.8 4.1 %all-gather.3 = bf16[8,384,128]{2,1,0:T(8,128)(2,1)S(1)} all-gather(bf16[4,384,128]{2,1,0:T(8,128)(2,1)S(1)} %pad_maximum_fusion.3), channel_id=5, replica_groups=mesh['section'=4,'vertex'=16,'feat'=2] {'feat'}, dimensions={0}, use_global_device_ids=true | all-gather | bytes 1179648 | tf_op jit(solution)/shard_map/all_gather | solution.py:634
  229.9 1.8 whole_rows.7
  (82 shorter events, 13.0 us)
Async XLA Ops:
  0.6 11.1 %copy-start = (bf16[2048,512]{1,0:T(8,128)(2,1)S(1)}, bf16[2048,512]{1,0:T(8,128)(2,1)}, u32[]{:S(2)}) copy-start(bf16[2048,512]{1,0:T(8,128)(2,1)} %param.9) | copy-start | bytes 6291460
  3.2 4.9 %copy-start.21 = (s32[3,128]{1,0:T(4,128)S(1)}, s32[3,128]{1,0:T(4,128)}, u32[]{:S(2)}) copy-start(s32[3,128]{1,0:T(4,128)} %param.16) | copy-start | bytes 4612
  3.2 30.7 %all-to-all-start = ((bf16[4,2048,128]{2,1,0:T(8,128)(2,1)}), bf16[4,2048,128]{2,1,0:T(8,128)(2,1)}, u32[]{:S(2)}, u32[]{:S(2)}) async-start(bf16[4,2048,128]{2,1,0:T(8,128)(2,1)} %section_slices.1), calls=%async_computation | async-start | bytes 4194304 | tf_op jit(solution)/shard_map/all_to_all | solution.py:587
  9.4 1.1 copy-start.18
  10.5 1.2 copy-start.19
  11.7 3.0 %copy-start.22 = (s32[3,64]{1,0:T(4,128)S(1)}, s32[3,64]{1,0:T(4,128)}, u32[]{:S(2)}) copy-start(s32[3,64]{1,0:T(4,128)} %param.14) | copy-start | bytes 2308
  11.7 3.0 %copy-start.23 = (s32[3,64]{1,0:T(4,128)S(1)}, s32[3,64]{1,0:T(4,128)}, u32[]{:S(2)}) copy-start(s32[3,64]{1,0:T(4,128)} %param.13) | copy-start | bytes 2308
  11.7 3.0 %copy-start.24 = (s32[3,1]{0,1:T(1,128)S(1)}, s32[3,1]{0,1:T(1,128)}, u32[]{:S(2)}) copy-start(s32[3,1]{0,1:T(1,128)} %param.15) | copy-start | bytes 40
  13.8 0.7 copy-start.20
  47.4 8.4 %copy-start.1 = (bf16[1,1024,512]{2,1,0:T(8,128)(2,1)S(1)}, bf16[1,1024,512]{2,1,0:T(8,128)(2,1)}, u32[]{:S(2)}) copy-start(bf16[1,1024,512]{2,1,0:T(8,128)(2,1)} %param.11) | copy-start | bytes 3145732
  47.4 29.1 %all-to-all-start.1 = ((bf16[16,3,128,128]{3,2,1,0:T(8,128)(2,1)}), bf16[16,3,128,128]{3,2,1,0:T(8,128)(2,1)}, u32[]{:S(2)}, u32[]{:S(2)}) async-start(bf16[16,3,128,128]{3,2,1,0:T(8,128)(2,1)} %get-tuple-element.40), calls=%async_computation.1 | async-start | bytes 3145728 | tf_op jit(solution)/shard_map/all_to_all | solution.py:625
  56.7 16.7 %collective-permute-start = (bf16[1024,128]{1,0:T(8,128)(2,1)S(1)}, bf16[1024,128]{1,0:T(8,128)(2,1)}, u32[]{:S(2)}, u32[]{:S(2)}) collective-permute-start(bf16[1024,128]{1,0:T(8,128)(2,1)S(1)} %get-tuple-element.62), channel_id=1, source_target_pairs={{0,32},{32,64},{64,96},{96,0},{1,33},{33,65},{65,97},{97,1},{2,34}... | collective-permute-start | bytes 786440 | tf_op jit(solution)/shard_map/ppermute | solution.py:22
  57.0 16.4 %collective-permute-start.1 = (bf16[1024,128]{1,0:T(8,128)(2,1)S(1)}, bf16[1024,128]{1,0:T(8,128)(2,1)}, u32[]{:S(2)}, u32[]{:S(2)}) collective-permute-start(bf16[1024,128]{1,0:T(8,128)(2,1)S(1)} %get-tuple-element.61), channel_id=1, source_target_pairs={{0,64},{32,96},{64,0},{96,32},{1,65},{33,97},{65,1},{97,33},{2,66}... | collective-permute-start | bytes 786440 | tf_op jit(solution)/shard_map/ppermute | solution.py:22
  58.8 14.7 %collective-permute-start.2 = (bf16[1024,128]{1,0:T(8,128)(2,1)S(1)}, bf16[1024,128]{1,0:T(8,128)(2,1)}, u32[]{:S(2)}, u32[]{:S(2)}) collective-permute-start(bf16[1024,128]{1,0:T(8,128)(2,1)S(1)} %get-tuple-element.60), channel_id=1, source_target_pairs={{0,96},{32,0},{64,32},{96,64},{1,97},{33,1},{65,33},{97,65},{2,98}... | collective-permute-start | bytes 786440 | tf_op jit(solution)/shard_map/ppermute | solution.py:22
  78.0 13.9 %copy-start.15 = (bf16[384,128]{1,0:T(8,128)(2,1)}, bf16[384,128]{1,0:T(8,128)(2,1)S(1)}, u32[]{:S(2)}) copy-start(bf16[384,128]{1,0:T(8,128)(2,1)S(1)} %collect.4.sup_ref) | copy-start | bytes 294916
  78.0 5.8 %collective-permute-start.3 = (bf16[384,128]{1,0:T(8,128)(2,1)S(1)}, bf16[384,128]{1,0:T(8,128)(2,1)S(1)}, u32[]{:S(2)}, u32[]{:S(2)}) collective-permute-start(bf16[384,128]{1,0:T(8,128)(2,1)S(1)} %collect.4.sup_ref), channel_id=1, source_target_pairs={{0,32},{32,64},{64,96},{96,0},{1,33},{33,65},{65,97},{97,1},{2,34}... | collective-permute-start | bytes 294920 | tf_op jit(solution)/shard_map/ppermute | solution.py:22
  78.4 5.4 %collective-permute-start.4 = (bf16[384,128]{1,0:T(8,128)(2,1)S(1)}, bf16[384,128]{1,0:T(8,128)(2,1)S(1)}, u32[]{:S(2)}, u32[]{:S(2)}) collective-permute-start(bf16[384,128]{1,0:T(8,128)(2,1)S(1)} %collect.4.sup_ref), channel_id=1, source_target_pairs={{0,64},{32,96},{64,0},{96,32},{1,65},{33,97},{65,1},{97,33},{2,66}... | collective-permute-start | bytes 294920 | tf_op jit(solution)/shard_map/ppermute | solution.py:22
  80.2 4.3 %collective-permute-start.5 = (bf16[384,128]{1,0:T(8,128)(2,1)S(1)}, bf16[384,128]{1,0:T(8,128)(2,1)S(1)}, u32[]{:S(2)}, u32[]{:S(2)}) collective-permute-start(bf16[384,128]{1,0:T(8,128)(2,1)S(1)} %collect.4.sup_ref), channel_id=1, source_target_pairs={{0,96},{32,0},{64,32},{96,64},{1,97},{33,1},{65,33},{97,65},{2,98}... | collective-permute-start | bytes 294920 | tf_op jit(solution)/shard_map/ppermute | solution.py:22
  98.0 39.4 %copy-start.14 = (f32[3,2048,128]{2,1,0:T(8,128)S(1)}, f32[3,2048,128]{2,1,0:T(8,128)}, u32[]{:S(2)}) copy-start(f32[3,2048,128]{2,1,0:T(8,128)} %get-tuple-element.56.static_ref) | copy-start | bytes 9437188
  124.0 13.4 %copy-start.2 = (bf16[2048,384]{1,0:T(8,128)(2,1)S(1)}, bf16[2048,384]{1,0:T(8,128)(2,1)}, u32[]{:S(2)}) copy-start(bf16[2048,384]{1,0:T(8,128)(2,1)} %get-tuple-element.55.refs_6_) | copy-start | bytes 4718596
  124.0 13.4 %copy-start.3 = (bf16[2048,256]{1,0:T(8,128)(2,1)S(1)}, bf16[2048,256]{1,0:T(8,128)(2,1)}, u32[]{:S(2)}) copy-start(bf16[2048,256]{1,0:T(8,128)(2,1)} %get-tuple-element.54.refs_5_) | copy-start | bytes 3145732
  124.0 13.4 %copy-start.11 = (bf16[2048,128]{1,0:T(8,128)(2,1)S(1)}, bf16[2048,128]{1,0:T(8,128)(2,1)}, u32[]{:S(2)}) copy-start(bf16[2048,128]{1,0:T(8,128)(2,1)} %get-tuple-element.53.refs_4_) | copy-start | bytes 1572868
  124.0 13.4 %copy-start.12 = (bf16[1024,128]{1,0:T(8,128)(2,1)S(1)}, bf16[1024,128]{1,0:T(8,128)(2,1)}, u32[]{:S(2)}) copy-start(bf16[1024,128]{1,0:T(8,128)(2,1)} %get-tuple-element.49.refs_0_) | copy-start | bytes 786436
  124.0 13.4 %copy-start.16 = (s32[2]{0:T(128)S(1)}, s32[2]{0:T(128)}, u32[]{:S(2)}) copy-start(s32[2]{0:T(128)} %pad_add_fusion.place_ref) | copy-start | bytes 28
  125.1 4.7 %collective-permute-start.6 = (bf16[384,128]{1,0:T(8,128)(2,1)S(1)}, bf16[384,128]{1,0:T(8,128)(2,1)S(1)}, u32[]{:S(2)}, u32[]{:S(2)}) collective-permute-start(bf16[384,128]{1,0:T(8,128)(2,1)S(1)} %collect.5.sup_ref), channel_id=1, source_target_pairs={{0,32},{32,64},{64,96},{96,0},{1,33},{33,65},{65,97},{97,1},{2,34}... | collective-permute-start | bytes 294920 | tf_op jit(solution)/shard_map/ppermute | solution.py:22
  125.7 5.8 %collective-permute-start.7 = (bf16[384,128]{1,0:T(8,128)(2,1)S(1)}, bf16[384,128]{1,0:T(8,128)(2,1)S(1)}, u32[]{:S(2)}, u32[]{:S(2)}) collective-permute-start(bf16[384,128]{1,0:T(8,128)(2,1)S(1)} %collect.5.sup_ref), channel_id=1, source_target_pairs={{0,64},{32,96},{64,0},{96,32},{1,65},{33,97},{65,1},{97,33},{2,66}... | collective-permute-start | bytes 294920 | tf_op jit(solution)/shard_map/ppermute | solution.py:22
  128.4 3.9 %collective-permute-start.8 = (bf16[384,128]{1,0:T(8,128)(2,1)S(1)}, bf16[384,128]{1,0:T(8,128)(2,1)S(1)}, u32[]{:S(2)}, u32[]{:S(2)}) collective-permute-start(bf16[384,128]{1,0:T(8,128)(2,1)S(1)} %collect.5.sup_ref), channel_id=1, source_target_pairs={{0,96},{32,0},{64,32},{96,64},{1,97},{33,1},{65,33},{97,65},{2,98}... | collective-permute-start | bytes 294920 | tf_op jit(solution)/shard_map/ppermute | solution.py:22
  137.4 4.9 %copy-start.6 = (bf16[8,384,128]{2,1,0:T(8,128)(2,1)}, bf16[8,384,128]{2,1,0:T(8,128)(2,1)S(1)}, u32[]{:S(2)}) copy-start(bf16[8,384,128]{2,1,0:T(8,128)(2,1)S(1)} %all-gather.1) | copy-start | bytes 2359300
  166.9 13.3 %copy-start.13 = (f32[3,2048,128]{2,1,0:T(8,128)S(1)}, f32[3,2048,128]{2,1,0:T(8,128)}, u32[]{:S(2)}) copy-start(f32[3,2048,128]{2,1,0:T(8,128)} %get-tuple-element.57.static_ref) | copy-start | bytes 9437188
  167.9 5.0 %collective-permute-start.9 = (bf16[384,128]{1,0:T(8,128)(2,1)S(1)}, bf16[384,128]{1,0:T(8,128)(2,1)S(1)}, u32[]{:S(2)}, u32[]{:S(2)}) collective-permute-start(bf16[384,128]{1,0:T(8,128)(2,1)S(1)} %collect.6.sup_ref), channel_id=1, source_target_pairs={{0,32},{32,64},{64,96},{96,0},{1,33},{33,65},{65,97},{97,1},{2,34}... | collective-permute-start | bytes 294920 | tf_op jit(solution)/shard_map/ppermute | solution.py:22
  168.2 6.1 %collective-permute-start.10 = (bf16[384,128]{1,0:T(8,128)(2,1)S(1)}, bf16[384,128]{1,0:T(8,128)(2,1)S(1)}, u32[]{:S(2)}, u32[]{:S(2)}) collective-permute-start(bf16[384,128]{1,0:T(8,128)(2,1)S(1)} %collect.6.sup_ref), channel_id=1, source_target_pairs={{0,64},{32,96},{64,0},{96,32},{1,65},{33,97},{65,1},{97,33},{2,66}... | collective-permute-start | bytes 294920 | tf_op jit(solution)/shard_map/ppermute | solution.py:22
  171.2 3.8 %collective-permute-start.11 = (bf16[384,128]{1,0:T(8,128)(2,1)S(1)}, bf16[384,128]{1,0:T(8,128)(2,1)S(1)}, u32[]{:S(2)}, u32[]{:S(2)}) collective-permute-start(bf16[384,128]{1,0:T(8,128)(2,1)S(1)} %collect.6.sup_ref), channel_id=1, source_target_pairs={{0,96},{32,0},{64,32},{96,64},{1,97},{33,1},{65,33},{97,65},{2,98}... | collective-permute-start | bytes 294920 | tf_op jit(solution)/shard_map/ppermute | solution.py:22
  185.1 0.9 copy-start.8
  185.9 1.2 copy-start.10
  187.1 4.5 %copy-start.17 = (f32[4]{0:T(128)S(1)}, f32[4]{0:T(128)}, u32[]{:S(2)}) copy-start(f32[4]{0:T(128)} %constant.71.clone.betas_ref) | copy-start | bytes 52
  187.1 29.7 %all-to-all-start.4 = ((bf16[16,3,128,128]{3,2,1,0:T(8,128)(2,1)}), bf16[16,3,128,128]{3,2,1,0:T(8,128)(2,1)}, u32[]{:S(2)}, u32[]{:S(2)}) async-start(bf16[16,3,128,128]{3,2,1,0:T(8,128)(2,1)} %copy-done.10), calls=%async_computation.4 | async-start | bytes 3145728 | tf_op jit(solution)/shard_map/all_to_all | solution.py:625
  191.7 1.1 copy-start.5
  192.8 1.2 copy-start.7
  192.8 1.8 copy-start.9
  195.9 11.9 %collective-permute-start.12 = (bf16[384,512]{1,0:T(8,128)(2,1)}, bf16[384,512]{1,0:T(8,128)(2,1)}, u32[]{:S(2)}, u32[]{:S(2)}) collective-permute-start(bf16[384,512]{1,0:T(8,128)(2,1)} %whole_rows.6.refs_0_), channel_id=1, source_target_pairs={{0,32},{32,64},{64,96},{96,0},{1,33},{33,65},{65,97},{97,1},{2,34}... | collective-permute-start | bytes 1179656 | tf_op jit(solution)/shard_map/ppermute | solution.py:22
  208.9 1.6 copy-start.4
  218.3 4.7 %collective-permute-start.13 = (bf16[384,128]{1,0:T(8,128)(2,1)S(1)}, bf16[384,128]{1,0:T(8,128)(2,1)S(1)}, u32[]{:S(2)}, u32[]{:S(2)}) collective-permute-start(bf16[384,128]{1,0:T(8,128)(2,1)S(1)} %collect.7), channel_id=1, source_target_pairs={{0,32},{32,64},{64,96},{96,0},{1,33},{33,65},{65,97},{97,1},{2,34}... | collective-permute-start | bytes 294920 | tf_op jit(solution)/shard_map/ppermute | solution.py:22
  218.6 6.3 %collective-permute-start.14 = (bf16[384,128]{1,0:T(8,128)(2,1)S(1)}, bf16[384,128]{1,0:T(8,128)(2,1)S(1)}, u32[]{:S(2)}, u32[]{:S(2)}) collective-permute-start(bf16[384,128]{1,0:T(8,128)(2,1)S(1)} %collect.7), channel_id=1, source_target_pairs={{0,64},{32,96},{64,0},{96,32},{1,65},{33,97},{65,1},{97,33},{2,66}... | collective-permute-start | bytes 294920 | tf_op jit(solution)/shard_map/ppermute | solution.py:22
  221.5 4.3 %collective-permute-start.15 = (bf16[384,128]{1,0:T(8,128)(2,1)S(1)}, bf16[384,128]{1,0:T(8,128)(2,1)S(1)}, u32[]{:S(2)}, u32[]{:S(2)}) collective-permute-start(bf16[384,128]{1,0:T(8,128)(2,1)S(1)} %collect.7), channel_id=1, source_target_pairs={{0,96},{32,0},{64,32},{96,64},{1,97},{33,1},{65,33},{97,65},{2,98}... | collective-permute-start | bytes 294920 | tf_op jit(solution)/shard_map/ppermute | solution.py:22

commit v3 on v2

--- a/solution.py
+++ b/solution.py
@@ -497,10 +497,7 @@
     depth, half = weight_cols.shape
 
     def kernel(place_ref, betas_ref, gath_ref, w_ref, *refs):
-        if layer:
-            earlier_ref, out_ref, left, own = refs
-        else:
-            out_ref, left, own = refs
+        earlier_ref, out_ref, left, own = refs
         section, feat = place_ref[0], place_ref[1]
 
         @pl.when(section == layer)
@@ -518,9 +515,9 @@
 
         @pl.when(section != layer)
         def _():
-            out_ref[...] = earlier_ref[...] if layer else jnp.zeros_like(out_ref)
-
-    operands = [gathered, weight_cols] + ([earlier] if layer else [])
+            out_ref[...] = earlier_ref[...]
+
+    operands = [gathered, weight_cols, earlier]
     return pl.pallas_call(
         kernel,
         out_shape=jax.ShapeDtypeStruct((picks, half), jnp.bfloat16),
@@ -563,7 +560,7 @@
             pl.BlockSpec((picks, half), lambda i: (0, 0)),
         ],
         out_specs=pl.BlockSpec((chunk, half), lambda i: (i, 0)),
-        compiler_params=vmem_params(24),
+        compiler_params=vmem_params(KERNEL_VMEM),
         cost_estimate=cost(2 * owned * picks * half, 4 * owned * half),
         name="replace_rows",
     )(stored, ids, fresh)
@@ -617,11 +614,11 @@
         rotated(by_distance[by], "section", by) for by in range(1, layers)
     ]
 
-    rows_kept = table = None
+    rows_kept, table = initial_half, None
     for layer in range(layers):
         if layer == layers - 1:
             before = rotated(rows_kept, "section", 1)
-            table = replace_rows(stored, ids, jnp.where(section == 0, initial_half, before))
+            table = replace_rows(stored, ids, before)
         arrived = lax.all_to_all(partial, "vertex", 0, 0, tiled=True)
         if layer == 0:
             arrived, statics, weight_slices = lax.optimization_barrier(

time: 233 us -> 232 us (level)
    unnamed x51 -> x59, local copies, waits for them, and re-layouts: 7.88 us -> 8.05 us
  transfers between devices with their start and end apart: 19 -> 19, of which waited for: 15 -> 15; matrix products, arithmetic and copies ran while one was open for 3% -> 2% of each run, Pallas kernels for 15% -> 16%
where the time goes in v3:
time: 232 us; the launch traced here: 231 us
  Pallas kernels  74.1 us (32%)
  blocking collectives  72.3 us (31%)
  waiting for transfers between devices  35.5 us (15%)
  starting transfers between devices  34.3 us (15%)
  local copies, waits for them, and re-layouts  11.9 us (5%)
    all_to_all x2, blocking collectives, shards(): arrived = lax.all_to_all(partial, 'vertex', 0, 0, tiled=True)  50.6 us
    ppermute x16, waiting for transfers between devices, rotated(): lax.ppermute(array, axis, [(i, (i + by) % devices) for i in range(devices)])  24.7 us
    all_gather x4, blocking collectives, shards(): gathered = lax.all_gather(near, 'feat', axis=0)  21.7 us
    ppermute x16, starting transfers between devices, rotated(): lax.ppermute(array, axis, [(i, (i + by) % devices) for i in range(devices)])  16.6 us
    pallas_call x3, Pallas kernels, layer_step(): pl.pallas_call(kernel, out_shape=jax.ShapeDtypeStruct((row_devices, spans...  15.7 us
    pallas_call x1, Pallas kernels, static_parts(): pl.pallas_call(kernel, out_shape=(jax.ShapeDtypeStruct((spans, rows, widt...  14 us
    pallas_call x1, Pallas kernels, replaced_columns(): pl.pallas_call(kernel, out_shape=tuple((jax.ShapeDtypeStruct(shape, jnp.b...  13.9 us
    pallas_call x1, Pallas kernels, first_partial(): pl.pallas_call(kernel, out_shape=(jax.ShapeDtypeStruct((row_devices, span...  13.3 us
  transfers between devices with their start and end apart: 19, of which 15 were waited for; matrix products, arithmetic and copies ran while one was open for 2% of the time, Pallas kernels for 16%

profile of v3, /device:TPU:1, one launch (start us, length us, event | category | flops | bytes accessed | tf_op | source)
XLA Modules:
  0.0 231.1 jit_solution(6257153483521600752)
XLA Ops:
  0.6 2.6 %section_slices.1 = bf16[4,2048,128]{2,1,0:T(8,128)(2,1)} custom-call(bf16[2048,512]{1,0:T(8,128)(2,1)} %bitcast.59), custom_call_target="tpu_custom_call" | custom-call | bytes 4194304 | tf_op jit(solution)/shard_map/section_slices/pallas_call | solution.py:178
  3.2 4.9 %all-to-all-start = ((bf16[4,2048,128]{2,1,0:T(8,128)(2,1)}), bf16[4,2048,128]{2,1,0:T(8,128)(2,1)}, u32[]{:S(2)}, u32[]{:S(2)}) async-start(bf16[4,2048,128]{2,1,0:T(8,128)(2,1)} %section_slices.1), calls=%async_computation | async-start | bytes 4194304 | tf_op jit(solution)/shard_map/all_to_all | solution.py:584
  8.1 1.2 selection.1
  9.4 1.1 copy-done.22
  10.5 1.2 copy-done.23
  11.7 2.1 gather_fusion
  14.8 0.9 constant_dynamic-slice_fusion.4.feat_ref
  15.7 13.9 %replaced_columns.1 = (bf16[2048,128]{1,0:T(8,128)(2,1)}, bf16[2048,256]{1,0:T(8,128)(2,1)}, bf16[2048,384]{1,0:T(8,128)(2,1)}) custom-call(s32[3,256]{1,0:T(4,128)} %broadcast_add_fusion.slots_ref, bf16[3,64,128,128]{3,2,1,0:T(8,128)(2,1)} %tiles_ref.5, bf16[2048,384]{1,0:T(8,128)(2,1)} %copy-done.23), custom_call_target="tpu_custom_call" | custom-call | flops 9663676416 | bytes 11010048 | tf_op jit(solution)/shard_map/replaced_columns/pallas_call | solution.py:303
  29.7 4.2 %all-to-all-done.hist_ref = bf16[4,2048,128]{2,1,0:T(8,128)(2,1)} async-done(((bf16[4,2048,128]{2,1,0:T(8,128)(2,1)}), bf16[4,2048,128]{2,1,0:T(8,128)(2,1)}, u32[]{:S(2)}, u32[]{:S(2)}) %all-to-all-start) | async-done | bytes 2097184 | tf_op jit(solution)/shard_map/all_to_all | solution.py:584
  33.9 13.3 %first_partial.1 = (bf16[16,3,128,128]{3,2,1,0:T(8,128)(2,1)}, f32[3,2048,128]{2,1,0:T(8,128)}) custom-call(s32[3,256]{1,0:T(4,128)} %broadcast_add_fusion.slots_ref, bf16[3,64,128,128]{3,2,1,0:T(8,128)(2,1)} %tiles_ref.5, bf16[4,2048,128]{2,1,0:T(8,128)(2,1)} %all-to-all-done.hist_ref, bf16[2048,128]{1,0:T(8,128)(2,1)} %constant_dynamic-slice_fusion.4.feat_ref, ...), custom_call_target="tpu_custom_call" | custom-call | flops 6442450944 | bytes 6291456 | tf_op jit(solution)/shard_map/first_partial/pallas_call | solution.py:123
  47.2 8.4 %all-to-all-start.1 = ((bf16[16,3,128,128]{3,2,1,0:T(8,128)(2,1)}), bf16[16,3,128,128]{3,2,1,0:T(8,128)(2,1)}, u32[]{:S(2)}, u32[]{:S(2)}) async-start(bf16[16,3,128,128]{3,2,1,0:T(8,128)(2,1)} %get-tuple-element.40), calls=%async_computation.1 | async-start | bytes 3145728 | tf_op jit(solution)/shard_map/all_to_all | solution.py:622
  55.7 0.9 constant_dynamic-slice_fusion
  56.9 1.8 collective-permute-start.1
  59.3 14.0 %static_parts.1 = (f32[3,2048,128]{2,1,0:T(8,128)}, f32[3,2048,128]{2,1,0:T(8,128)}) custom-call(s32[3,256]{1,0:T(4,128)} %broadcast_add_fusion.slots_ref, bf16[3,64,128,128]{3,2,1,0:T(8,128)(2,1)} %tiles_ref.5, bf16[4,2048,128]{2,1,0:T(8,128)(2,1)} %all-to-all-done.hist_ref, bf16[3,2048,128]{2,1,0:T(8,128)(2,1)} %copy-done.22), custom_call_target="tpu_custom_call" | custom-call | flops 6442450944 | bytes 12582912 | tf_op jit(solution)/shard_map/static_parts/pallas_call | solution.py:358
  73.3 3.1 %all-to-all-done.1.in_ref = bf16[16,3,128,128]{3,2,1,0:T(8,128)(2,1)} async-done(((bf16[16,3,128,128]{3,2,1,0:T(8,128)(2,1)}), bf16[16,3,128,128]{3,2,1,0:T(8,128)(2,1)}, u32[]{:S(2)}, u32[]{:S(2)}) %all-to-all-start.1) | async-done | bytes 1572896 | tf_op jit(solution)/shard_map/all_to_all | solution.py:622
  76.4 1.5 collect.4.sup_ref
  78.2 1.8 collective-permute-start.4
  81.4 2.3 %collective-permute-done.3 = bf16[384,128]{1,0:T(8,128)(2,1)S(1)} collective-permute-done((bf16[384,128]{1,0:T(8,128)(2,1)S(1)}, bf16[384,128]{1,0:T(8,128)(2,1)S(1)}, u32[]{:S(2)}, u32[]{:S(2)}) %collective-permute-start.3) | collective-permute-done | bytes 98336 | tf_op jit(solution)/shard_map/ppermute | solution.py:22
  84.4 7.4 %all-gather = bf16[8,384,128]{2,1,0:T(8,128)(2,1)} all-gather(bf16[4,384,128]{2,1,0:T(8,128)(2,1)S(1)} %pad_maximum_fusion), channel_id=2, replica_groups=mesh['section'=4,'vertex'=16,'feat'=2] {'feat'}, dimensions={0}, use_global_device_ids=true | all-gather | bytes 1179648 | tf_op jit(solution)/shard_map/all_gather | solution.py:631
  91.8 6.1 %layer_step.3 = bf16[16,3,128,128]{3,2,1,0:T(8,128)(2,1)} custom-call(s32[2]{0:T(128)} %pad_add_fusion.place_ref, bf16[2,4,384,128]{3,2,1,0:T(8,128)(2,1)} %bitcast.46, bf16[384,128]{1,0:T(8,128)(2,1)} %copy-done.18, f32[3,2048,128]{2,1,0:T(8,128)} %get-tuple-element.48.static_ref, bf16[1024,128]{1,0:T(8,128)(2,1)} %get-tuple-element.49.refs_0_, ...), custom_call_target="tpu_custom_call" | custom-call | flops 704643072 | bytes 9437184 | tf_op jit(solution)/shard_map/layer_step/pallas_call | solution.py:467
  97.9 26.0 %all_to_all.25.in_ref = bf16[16,3,128,128]{3,2,1,0:T(8,128)(2,1)S(1)} all-to-all(bf16[16,3,128,128]{3,2,1,0:T(8,128)(2,1)} %layer_step.3), channel_id=1, replica_groups=mesh['section'=4,'vertex'=16,'feat'=2] {'vertex'}, dimensions={0} | all-to-all | bytes 3145728 | tf_op jit(solution)/shard_map/all_to_all | solution.py:622
  123.9 1.0 collect.5.sup_ref
  125.6 2.7 %collective-permute-start.7 = (bf16[384,128]{1,0:T(8,128)(2,1)S(1)}, bf16[384,128]{1,0:T(8,128)(2,1)S(1)}, u32[]{:S(2)}, u32[]{:S(2)}) collective-permute-start(bf16[384,128]{1,0:T(8,128)(2,1)S(1)} %collect.5.sup_ref), channel_id=1, source_target_pairs={{0,64},{32,96},{64,0},{96,32},{1,65},{33,97},{65,1},{97,33},{2,66}... | collective-permute-start | bytes 294920 | tf_op jit(solution)/shard_map/ppermute | solution.py:22
  128.3 1.4 collective-permute-done.6
  129.7 1.7 collective-permute-done.7
  132.3 5.0 %all-gather.1 = bf16[8,384,128]{2,1,0:T(8,128)(2,1)S(1)} all-gather(bf16[4,384,128]{2,1,0:T(8,128)(2,1)S(1)} %pad_maximum_fusion.1), channel_id=3, replica_groups=mesh['section'=4,'vertex'=16,'feat'=2] {'feat'}, dimensions={0}, use_global_device_ids=true | all-gather | bytes 1179648 | tf_op jit(solution)/shard_map/all_gather | solution.py:631
  137.3 4.8 %layer_step.4 = bf16[16,3,128,128]{3,2,1,0:T(8,128)(2,1)S(1)} custom-call(s32[2]{0:T(128)S(1)} %copy-done.19, bf16[2,4,384,128]{3,2,1,0:T(8,128)(2,1)S(1)} %bitcast.48, bf16[384,128]{1,0:T(8,128)(2,1)S(1)} %collect.5.sup_ref, f32[3,2048,128]{2,1,0:T(8,128)S(1)} %copy-done.13, bf16[1024,128]{1,0:T(8,128)(2,1)S(1)} %copy-done.11, ...), custom_call_target="tpu_custom_call" | custom-call | flops 704643072 | bytes 9437184 | tf_op jit(solution)/shard_map/layer_step/pallas_call | solution.py:467
  142.2 24.6 %all_to_all.26.in_ref = bf16[16,3,128,128]{3,2,1,0:T(8,128)(2,1)S(1)} all-to-all(bf16[16,3,128,128]{3,2,1,0:T(8,128)(2,1)S(1)} %layer_step.4), channel_id=1, replica_groups=mesh['section'=4,'vertex'=16,'feat'=2] {'vertex'}, dimensions={0} | all-to-all | bytes 3145728 | tf_op jit(solution)/shard_map/all_to_all | solution.py:622
  166.8 1.0 collect.6.sup_ref
  168.1 3.0 %collective-permute-start.10 = (bf16[384,128]{1,0:T(8,128)(2,1)S(1)}, bf16[384,128]{1,0:T(8,128)(2,1)S(1)}, u32[]{:S(2)}, u32[]{:S(2)}) collective-permute-start(bf16[384,128]{1,0:T(8,128)(2,1)S(1)} %collect.6.sup_ref), channel_id=1, source_target_pairs={{0,64},{32,96},{64,0},{96,32},{1,65},{33,97},{65,1},{97,33},{2,66}... | collective-permute-start | bytes 294920 | tf_op jit(solution)/shard_map/ppermute | solution.py:22
  171.4 1.4 collective-permute-done.9
  172.8 1.4 collective-permute-done.10
  174.9 5.2 %all-gather.2 = bf16[8,384,128]{2,1,0:T(8,128)(2,1)S(1)} all-gather(bf16[4,384,128]{2,1,0:T(8,128)(2,1)S(1)} %pad_maximum_fusion.2), channel_id=4, replica_groups=mesh['section'=4,'vertex'=16,'feat'=2] {'feat'}, dimensions={0}, use_global_device_ids=true | all-gather | bytes 1179648 | tf_op jit(solution)/shard_map/all_gather | solution.py:631
  180.1 4.8 %layer_step.5 = bf16[16,3,128,128]{3,2,1,0:T(8,128)(2,1)S(1)} custom-call(s32[2]{0:T(128)S(1)} %copy-done.19, bf16[2,4,384,128]{3,2,1,0:T(8,128)(2,1)S(1)} %bitcast.50, bf16[384,128]{1,0:T(8,128)(2,1)S(1)} %collect.6.sup_ref, f32[3,2048,128]{2,1,0:T(8,128)S(1)} %copy-done.12, bf16[1024,128]{1,0:T(8,128)(2,1)S(1)} %copy-done.11, ...), custom_call_target="tpu_custom_call" | custom-call | flops 704643072 | bytes 9437184 | tf_op jit(solution)/shard_map/layer_step/pallas_call | solution.py:467
  185.8 1.1 copy-done.9
  186.9 4.5 %all-to-all-start.4 = ((bf16[16,3,128,128]{3,2,1,0:T(8,128)(2,1)}), bf16[16,3,128,128]{3,2,1,0:T(8,128)(2,1)}, u32[]{:S(2)}, u32[]{:S(2)}) async-start(bf16[16,3,128,128]{3,2,1,0:T(8,128)(2,1)} %copy-done.9), calls=%async_computation.4 | async-start | bytes 3145728 | tf_op jit(solution)/shard_map/all_to_all | solution.py:622
  191.5 1.1 copy-done.4
  192.6 1.0 copy-done.15
  193.6 1.2 whole_rows.4.refs_0_
  197.6 10.1 %collective-permute-done.12.fresh_ref = bf16[384,512]{1,0:T(8,128)(2,1)S(1)} collective-permute-done((bf16[384,512]{1,0:T(8,128)(2,1)S(1)}, bf16[384,512]{1,0:T(8,128)(2,1)S(1)}, u32[]{:S(2)}, u32[]{:S(2)}) %collective-permute-start.12) | collective-permute-done | bytes 393248 | tf_op jit(solution)/shard_map/ppermute | solution.py:22
  208.5 4.7 %replace_rows.1 = bf16[2048,512]{1,0:T(8,128)(2,1)} custom-call(bf16[2048,512]{1,0:T(8,128)(2,1)} %bitcast.60, s32[1,384]{1,0:T(1,128)} %bitcast.58, bf16[384,512]{1,0:T(8,128)(2,1)} %copy-done.24), custom_call_target="tpu_custom_call" | custom-call | flops 805306368 | bytes 4194304 | tf_op jit(solution)/shard_map/replace_rows/pallas_call | solution.py:553
  213.2 3.5 %all-to-all-done.4.in_ref = bf16[16,3,128,128]{3,2,1,0:T(8,128)(2,1)} async-done(((bf16[16,3,128,128]{3,2,1,0:T(8,128)(2,1)}), bf16[16,3,128,128]{3,2,1,0:T(8,128)(2,1)}, u32[]{:S(2)}, u32[]{:S(2)}) %all-to-all-start.4) | async-done | bytes 1572896 | tf_op jit(solution)/shard_map/all_to_all | solution.py:622
  216.6 1.5 collect.7
  218.5 2.9 %collective-permute-start.14 = (bf16[384,128]{1,0:T(8,128)(2,1)S(1)}, bf16[384,128]{1,0:T(8,128)(2,1)S(1)}, u32[]{:S(2)}, u32[]{:S(2)}) collective-permute-start(bf16[384,128]{1,0:T(8,128)(2,1)S(1)} %collect.7), channel_id=1, source_target_pairs={{0,64},{32,96},{64,0},{96,32},{1,65},{33,97},{65,1},{97,33},{2,66}... | collective-permute-start | bytes 294920 | tf_op jit(solution)/shard_map/ppermute | solution.py:22
  221.4 1.5 collective-permute-done.13
  222.9 1.9 collective-permute-done.14
  225.7 4.1 %all-gather.3 = bf16[8,384,128]{2,1,0:T(8,128)(2,1)S(1)} all-gather(bf16[4,384,128]{2,1,0:T(8,128)(2,1)S(1)} %pad_maximum_fusion.3), channel_id=5, replica_groups=mesh['section'=4,'vertex'=16,'feat'=2] {'feat'}, dimensions={0}, use_global_device_ids=true | all-gather | bytes 1179648 | tf_op jit(solution)/shard_map/all_gather | solution.py:631
  229.8 1.3 whole_rows.7
  (89 shorter events, 12.9 us)
Async XLA Ops:
  0.6 11.1 %copy-start = (bf16[2048,512]{1,0:T(8,128)(2,1)S(1)}, bf16[2048,512]{1,0:T(8,128)(2,1)}, u32[]{:S(2)}) copy-start(bf16[2048,512]{1,0:T(8,128)(2,1)} %param.9) | copy-start | bytes 6291460
  3.2 4.9 %copy-start.25 = (s32[3,128]{1,0:T(4,128)S(1)}, s32[3,128]{1,0:T(4,128)}, u32[]{:S(2)}) copy-start(s32[3,128]{1,0:T(4,128)} %param.16) | copy-start | bytes 4612
  3.2 30.7 %all-to-all-start = ((bf16[4,2048,128]{2,1,0:T(8,128)(2,1)}), bf16[4,2048,128]{2,1,0:T(8,128)(2,1)}, u32[]{:S(2)}, u32[]{:S(2)}) async-start(bf16[4,2048,128]{2,1,0:T(8,128)(2,1)} %section_slices.1), calls=%async_computation | async-start | bytes 4194304 | tf_op jit(solution)/shard_map/all_to_all | solution.py:584
  8.1 5.8 %copy-start.21 = (s32[1,1,3,128]{3,1,2,0:T(1,128)}, s32[1,1,3,128]{3,1,2,0:T(1,128)S(1)}, u32[]{:S(2)}) copy-start(s32[1,1,3,128]{3,1,2,0:T(1,128)S(1)} %copy.15) | copy-start | bytes 4612
  9.4 1.1 copy-start.22
  10.5 1.2 copy-start.23
  11.7 2.3 copy-start.26
  11.7 2.3 copy-start.27
  11.7 2.3 copy-start.28
  13.9 15.7 %copy-start.14 = (bf16[384,512]{1,0:T(8,128)(2,1)}, bf16[384,512]{1,0:T(8,128)(2,1)S(1)}, u32[]{:S(2)}) copy-start(bf16[384,512]{1,0:T(8,128)(2,1)S(1)} %broadcast_select_fusion.refs_0_) | copy-start | bytes 1179652
  47.2 8.5 %copy-start.1 = (bf16[1,1024,512]{2,1,0:T(8,128)(2,1)S(1)}, bf16[1,1024,512]{2,1,0:T(8,128)(2,1)}, u32[]{:S(2)}) copy-start(bf16[1,1024,512]{2,1,0:T(8,128)(2,1)} %param.11) | copy-start | bytes 3145732
  47.2 29.2 %all-to-all-start.1 = ((bf16[16,3,128,128]{3,2,1,0:T(8,128)(2,1)}), bf16[16,3,128,128]{3,2,1,0:T(8,128)(2,1)}, u32[]{:S(2)}, u32[]{:S(2)}) async-start(bf16[16,3,128,128]{3,2,1,0:T(8,128)(2,1)} %get-tuple-element.40), calls=%async_computation.1 | async-start | bytes 3145728 | tf_op jit(solution)/shard_map/all_to_all | solution.py:622
  56.6 16.7 %collective-permute-start = (bf16[1024,128]{1,0:T(8,128)(2,1)S(1)}, bf16[1024,128]{1,0:T(8,128)(2,1)}, u32[]{:S(2)}, u32[]{:S(2)}) collective-permute-start(bf16[1024,128]{1,0:T(8,128)(2,1)S(1)} %get-tuple-element.62), channel_id=1, source_target_pairs={{0,32},{32,64},{64,96},{96,0},{1,33},{33,65},{65,97},{97,1},{2,34}... | collective-permute-start | bytes 786440 | tf_op jit(solution)/shard_map/ppermute | solution.py:22
  56.9 16.4 %collective-permute-start.1 = (bf16[1024,128]{1,0:T(8,128)(2,1)S(1)}, bf16[1024,128]{1,0:T(8,128)(2,1)}, u32[]{:S(2)}, u32[]{:S(2)}) collective-permute-start(bf16[1024,128]{1,0:T(8,128)(2,1)S(1)} %get-tuple-element.61), channel_id=1, source_target_pairs={{0,64},{32,96},{64,0},{96,32},{1,65},{33,97},{65,1},{97,33},{2,66}... | collective-permute-start | bytes 786440 | tf_op jit(solution)/shard_map/ppermute | solution.py:22
  58.7 14.6 %collective-permute-start.2 = (bf16[1024,128]{1,0:T(8,128)(2,1)S(1)}, bf16[1024,128]{1,0:T(8,128)(2,1)}, u32[]{:S(2)}, u32[]{:S(2)}) collective-permute-start(bf16[1024,128]{1,0:T(8,128)(2,1)S(1)} %get-tuple-element.60), channel_id=1, source_target_pairs={{0,96},{32,0},{64,32},{96,64},{1,97},{33,1},{65,33},{97,65},{2,98}... | collective-permute-start | bytes 786440 | tf_op jit(solution)/shard_map/ppermute | solution.py:22
  77.9 13.9 %copy-start.18 = (bf16[384,128]{1,0:T(8,128)(2,1)}, bf16[384,128]{1,0:T(8,128)(2,1)S(1)}, u32[]{:S(2)}) copy-start(bf16[384,128]{1,0:T(8,128)(2,1)S(1)} %collect.4.sup_ref) | copy-start | bytes 294916
  77.9 5.8 %collective-permute-start.3 = (bf16[384,128]{1,0:T(8,128)(2,1)S(1)}, bf16[384,128]{1,0:T(8,128)(2,1)S(1)}, u32[]{:S(2)}, u32[]{:S(2)}) collective-permute-start(bf16[384,128]{1,0:T(8,128)(2,1)S(1)} %collect.4.sup_ref), channel_id=1, source_target_pairs={{0,32},{32,64},{64,96},{96,0},{1,33},{33,65},{65,97},{97,1},{2,34}... | collective-permute-start | bytes 294920 | tf_op jit(solution)/shard_map/ppermute | solution.py:22
  78.2 5.5 %collective-permute-start.4 = (bf16[384,128]{1,0:T(8,128)(2,1)S(1)}, bf16[384,128]{1,0:T(8,128)(2,1)S(1)}, u32[]{:S(2)}, u32[]{:S(2)}) collective-permute-start(bf16[384,128]{1,0:T(8,128)(2,1)S(1)} %collect.4.sup_ref), channel_id=1, source_target_pairs={{0,64},{32,96},{64,0},{96,32},{1,65},{33,97},{65,1},{97,33},{2,66}... | collective-permute-start | bytes 294920 | tf_op jit(solution)/shard_map/ppermute | solution.py:22
  80.0 4.3 %collective-permute-start.5 = (bf16[384,128]{1,0:T(8,128)(2,1)S(1)}, bf16[384,128]{1,0:T(8,128)(2,1)S(1)}, u32[]{:S(2)}, u32[]{:S(2)}) collective-permute-start(bf16[384,128]{1,0:T(8,128)(2,1)S(1)} %collect.4.sup_ref), channel_id=1, source_target_pairs={{0,96},{32,0},{64,32},{96,64},{1,97},{33,1},{65,33},{97,65},{2,98}... | collective-permute-start | bytes 294920 | tf_op jit(solution)/shard_map/ppermute | solution.py:22
  97.8 39.4 %copy-start.13 = (f32[3,2048,128]{2,1,0:T(8,128)S(1)}, f32[3,2048,128]{2,1,0:T(8,128)}, u32[]{:S(2)}) copy-start(f32[3,2048,128]{2,1,0:T(8,128)} %get-tuple-element.56.static_ref) | copy-start | bytes 9437188
  123.9 13.4 %copy-start.2 = (bf16[2048,384]{1,0:T(8,128)(2,1)S(1)}, bf16[2048,384]{1,0:T(8,128)(2,1)}, u32[]{:S(2)}) copy-start(bf16[2048,384]{1,0:T(8,128)(2,1)} %get-tuple-element.55.refs_6_) | copy-start | bytes 4718596
  123.9 13.4 %copy-start.3 = (bf16[2048,256]{1,0:T(8,128)(2,1)S(1)}, bf16[2048,256]{1,0:T(8,128)(2,1)}, u32[]{:S(2)}) copy-start(bf16[2048,256]{1,0:T(8,128)(2,1)} %get-tuple-element.54.refs_5_) | copy-start | bytes 3145732
  123.9 13.4 %copy-start.10 = (bf16[2048,128]{1,0:T(8,128)(2,1)S(1)}, bf16[2048,128]{1,0:T(8,128)(2,1)}, u32[]{:S(2)}) copy-start(bf16[2048,128]{1,0:T(8,128)(2,1)} %get-tuple-element.53.refs_4_) | copy-start | bytes 1572868
  123.9 13.4 %copy-start.11 = (bf16[1024,128]{1,0:T(8,128)(2,1)S(1)}, bf16[1024,128]{1,0:T(8,128)(2,1)}, u32[]{:S(2)}) copy-start(bf16[1024,128]{1,0:T(8,128)(2,1)} %get-tuple-element.49.refs_0_) | copy-start | bytes 786436
  123.9 13.4 %copy-start.19 = (s32[2]{0:T(128)S(1)}, s32[2]{0:T(128)}, u32[]{:S(2)}) copy-start(s32[2]{0:T(128)} %pad_add_fusion.place_ref) | copy-start | bytes 28
  124.9 4.7 %collective-permute-start.6 = (bf16[384,128]{1,0:T(8,128)(2,1)S(1)}, bf16[384,128]{1,0:T(8,128)(2,1)S(1)}, u32[]{:S(2)}, u32[]{:S(2)}) collective-permute-start(bf16[384,128]{1,0:T(8,128)(2,1)S(1)} %collect.5.sup_ref), channel_id=1, source_target_pairs={{0,32},{32,64},{64,96},{96,0},{1,33},{33,65},{65,97},{97,1},{2,34}... | collective-permute-start | bytes 294920 | tf_op jit(solution)/shard_map/ppermute | solution.py:22
  125.6 5.8 %collective-permute-start.7 = (bf16[384,128]{1,0:T(8,128)(2,1)S(1)}, bf16[384,128]{1,0:T(8,128)(2,1)S(1)}, u32[]{:S(2)}, u32[]{:S(2)}) collective-permute-start(bf16[384,128]{1,0:T(8,128)(2,1)S(1)} %collect.5.sup_ref), channel_id=1, source_target_pairs={{0,64},{32,96},{64,0},{96,32},{1,65},{33,97},{65,1},{97,33},{2,66}... | collective-permute-start | bytes 294920 | tf_op jit(solution)/shard_map/ppermute | solution.py:22
  128.3 3.9 %collective-permute-start.8 = (bf16[384,128]{1,0:T(8,128)(2,1)S(1)}, bf16[384,128]{1,0:T(8,128)(2,1)S(1)}, u32[]{:S(2)}, u32[]{:S(2)}) collective-permute-start(bf16[384,128]{1,0:T(8,128)(2,1)S(1)} %collect.5.sup_ref), channel_id=1, source_target_pairs={{0,96},{32,0},{64,32},{96,64},{1,97},{33,1},{65,33},{97,65},{2,98}... | collective-permute-start | bytes 294920 | tf_op jit(solution)/shard_map/ppermute | solution.py:22
  137.3 4.9 %copy-start.5 = (bf16[8,384,128]{2,1,0:T(8,128)(2,1)}, bf16[8,384,128]{2,1,0:T(8,128)(2,1)S(1)}, u32[]{:S(2)}) copy-start(bf16[8,384,128]{2,1,0:T(8,128)(2,1)S(1)} %all-gather.1) | copy-start | bytes 2359300
  166.8 13.3 %copy-start.12 = (f32[3,2048,128]{2,1,0:T(8,128)S(1)}, f32[3,2048,128]{2,1,0:T(8,128)}, u32[]{:S(2)}) copy-start(f32[3,2048,128]{2,1,0:T(8,128)} %get-tuple-element.57.static_ref) | copy-start | bytes 9437188
  167.8 5.0 %collective-permute-start.9 = (bf16[384,128]{1,0:T(8,128)(2,1)S(1)}, bf16[384,128]{1,0:T(8,128)(2,1)S(1)}, u32[]{:S(2)}, u32[]{:S(2)}) collective-permute-start(bf16[384,128]{1,0:T(8,128)(2,1)S(1)} %collect.6.sup_ref), channel_id=1, source_target_pairs={{0,32},{32,64},{64,96},{96,0},{1,33},{33,65},{65,97},{97,1},{2,34}... | collective-permute-start | bytes 294920 | tf_op jit(solution)/shard_map/ppermute | solution.py:22
  168.1 6.0 %collective-permute-start.10 = (bf16[384,128]{1,0:T(8,128)(2,1)S(1)}, bf16[384,128]{1,0:T(8,128)(2,1)S(1)}, u32[]{:S(2)}, u32[]{:S(2)}) collective-permute-start(bf16[384,128]{1,0:T(8,128)(2,1)S(1)} %collect.6.sup_ref), channel_id=1, source_target_pairs={{0,64},{32,96},{64,0},{96,32},{1,65},{33,97},{65,1},{97,33},{2,66}... | collective-permute-start | bytes 294920 | tf_op jit(solution)/shard_map/ppermute | solution.py:22
  171.1 3.8 %collective-permute-start.11 = (bf16[384,128]{1,0:T(8,128)(2,1)S(1)}, bf16[384,128]{1,0:T(8,128)(2,1)S(1)}, u32[]{:S(2)}, u32[]{:S(2)}) collective-permute-start(bf16[384,128]{1,0:T(8,128)(2,1)S(1)} %collect.6.sup_ref), channel_id=1, source_target_pairs={{0,96},{32,0},{64,32},{96,64},{1,97},{33,1},{65,33},{97,65},{2,98}... | collective-permute-start | bytes 294920 | tf_op jit(solution)/shard_map/ppermute | solution.py:22
  184.9 0.9 copy-start.7
  185.8 1.1 copy-start.9
  186.9 4.6 %copy-start.20 = (f32[4]{0:T(128)S(1)}, f32[4]{0:T(128)}, u32[]{:S(2)}) copy-start(f32[4]{0:T(128)} %constant.71.clone.betas_ref) | copy-start | bytes 52
  186.9 29.7 %all-to-all-start.4 = ((bf16[16,3,128,128]{3,2,1,0:T(8,128)(2,1)}), bf16[16,3,128,128]{3,2,1,0:T(8,128)(2,1)}, u32[]{:S(2)}, u32[]{:S(2)}) async-start(bf16[16,3,128,128]{3,2,1,0:T(8,128)(2,1)} %copy-done.9), calls=%async_computation.4 | async-start | bytes 3145728 | tf_op jit(solution)/shard_map/all_to_all | solution.py:622
  191.5 1.1 copy-start.4
  192.6 1.0 copy-start.15
  193.6 1.2 copy-start.6
  193.6 1.8 copy-start.8
  196.0 11.7 %collective-permute-start.12 = (bf16[384,512]{1,0:T(8,128)(2,1)S(1)}, bf16[384,512]{1,0:T(8,128)(2,1)S(1)}, u32[]{:S(2)}, u32[]{:S(2)}) collective-permute-start(bf16[384,512]{1,0:T(8,128)(2,1)S(1)} %whole_rows.6.refs_0_), channel_id=1, source_target_pairs={{0,32},{32,64},{64,96},{96,0},{1,33},{33,65},{65,97},{97,1},{2,34}... | collective-permute-start | bytes 1179656 | tf_op jit(solution)/shard_map/ppermute | solution.py:22
  196.9 0.7 copy-start.16
  207.7 0.7 copy-start.24
  216.6 13.2 %copy-start.17 = (bf16[384,512]{1,0:T(8,128)(2,1)S(1)}, bf16[384,512]{1,0:T(8,128)(2,1)}, u32[]{:S(2)}) copy-start(bf16[384,512]{1,0:T(8,128)(2,1)} %copy-done.16) | copy-start | bytes 1179652
  218.1 4.7 %collective-permute-start.13 = (bf16[384,128]{1,0:T(8,128)(2,1)S(1)}, bf16[384,128]{1,0:T(8,128)(2,1)S(1)}, u32[]{:S(2)}, u32[]{:S(2)}) collective-permute-start(bf16[384,128]{1,0:T(8,128)(2,1)S(1)} %collect.7), channel_id=1, source_target_pairs={{0,32},{32,64},{64,96},{96,0},{1,33},{33,65},{65,97},{97,1},{2,34}... | collective-permute-start | bytes 294920 | tf_op jit(solution)/shard_map/ppermute | solution.py:22
  218.5 6.3 %collective-permute-start.14 = (bf16[384,128]{1,0:T(8,128)(2,1)S(1)}, bf16[384,128]{1,0:T(8,128)(2,1)S(1)}, u32[]{:S(2)}, u32[]{:S(2)}) collective-permute-start(bf16[384,128]{1,0:T(8,128)(2,1)S(1)} %collect.7), channel_id=1, source_target_pairs={{0,64},{32,96},{64,0},{96,32},{1,65},{33,97},{65,1},{97,33},{2,66}... | collective-permute-start | bytes 294920 | tf_op jit(solution)/shard_map/ppermute | solution.py:22
  221.4 4.3 %collective-permute-start.15 = (bf16[384,128]{1,0:T(8,128)(2,1)S(1)}, bf16[384,128]{1,0:T(8,128)(2,1)S(1)}, u32[]{:S(2)}, u32[]{:S(2)}) collective-permute-start(bf16[384,128]{1,0:T(8,128)(2,1)S(1)} %collect.7), channel_id=1, source_target_pairs={{0,96},{32,0},{64,32},{96,64},{1,97},{33,1},{65,33},{97,65},{2,98}... | collective-permute-start | bytes 294920 | tf_op jit(solution)/shard_map/ppermute | solution.py:22

commit v4 on v3

--- a/solution.py
+++ b/solution.py
@@ -640,7 +640,7 @@
                 layer,
                 betas[layer],
                 row_devices,
-                layer > 0,
+                True,
             )
         rows_kept = whole_rows(place, beta_table, gathered, own_weights, rows_kept, layer)
     return (rows_kept.reshape(1, spans, rows_local, half), table[None])

time: 232 us -> 233 us (level)
  local copies, waits for them, and re-layouts: 11.9 us -> 18 us
  Pallas kernels: 74.1 us -> 70.3 us
    unnamed x59 -> x71, local copies, waits for them, and re-layouts: 8.05 us -> 14.2 us
    pallas_call x3, Pallas kernels: 15.7 us -> 11.8 us  [layer_step(): pl.pallas_call(kernel, out_shape=jax.ShapeDtypeStruct((row_devices, spans...]
where the time goes in v4:
time: 233 us
  blocking collectives  71.7 us (31%)
  Pallas kernels  70.3 us (30%)
  starting transfers between devices  36.4 us (16%)
  waiting for transfers between devices  33.7 us (14%)
  local copies, waits for them, and re-layouts  18 us (8%)
    all_to_all x2, blocking collectives, shards(): arrived = lax.all_to_all(partial, 'vertex', 0, 0, tiled=True)  51 us
    ppermute x16, waiting for transfers between devices, rotated(): lax.ppermute(array, axis, [(i, (i + by) % devices) for i in range(devices)])  25 us
    all_gather x4, blocking collectives, shards(): gathered = lax.all_gather(near, 'feat', axis=0)  20.7 us
    ppermute x16, starting transfers between devices, rotated(): lax.ppermute(array, axis, [(i, (i + by) % devices) for i in range(devices)])  18.6 us
    unnamed x71, local copies, waits for them, and re-layouts  14.2 us
    pallas_call x1, Pallas kernels, static_parts(): pl.pallas_call(kernel, out_shape=(jax.ShapeDtypeStruct((spans, rows, widt...  14 us
    pallas_call x1, Pallas kernels, replaced_columns(): pl.pallas_call(kernel, out_shape=tuple((jax.ShapeDtypeStruct(shape, jnp.b...  13.9 us
    pallas_call x1, Pallas kernels, first_partial(): pl.pallas_call(kernel, out_shape=(jax.ShapeDtypeStruct((row_devices, span...  13.3 us
  transfers between devices with their start and end apart: 19, of which 15 were waited for; matrix products, arithmetic and copies ran while one was open for 2% of the time, Pallas kernels for 16%

profile of v4, /device:TPU:1, one launch (start us, length us, event | category | flops | bytes accessed | tf_op | source)
XLA Modules:
  0.0 232.5 jit_solution(629210395982659213)
XLA Ops:
  0.6 2.6 %section_slices.1 = bf16[4,2048,128]{2,1,0:T(8,128)(2,1)} custom-call(bf16[2048,512]{1,0:T(8,128)(2,1)} %bitcast.59), custom_call_target="tpu_custom_call" | custom-call | bytes 4194304 | tf_op jit(solution)/shard_map/section_slices/pallas_call | solution.py:178
  3.2 4.9 %all-to-all-start = ((bf16[4,2048,128]{2,1,0:T(8,128)(2,1)}), bf16[4,2048,128]{2,1,0:T(8,128)(2,1)}, u32[]{:S(2)}, u32[]{:S(2)}) async-start(bf16[4,2048,128]{2,1,0:T(8,128)(2,1)} %section_slices.1), calls=%async_computation | async-start | bytes 4194304 | tf_op jit(solution)/shard_map/all_to_all | solution.py:584
  8.1 1.2 selection.1
  9.4 1.1 copy-done.28
  10.5 1.2 copy-done.29
  11.7 2.1 gather_fusion
  15.7 13.9 %replaced_columns.1 = (bf16[2048,128]{1,0:T(8,128)(2,1)}, bf16[2048,256]{1,0:T(8,128)(2,1)}, bf16[2048,384]{1,0:T(8,128)(2,1)}) custom-call(s32[3,256]{1,0:T(4,128)} %broadcast_add_fusion.slots_ref, bf16[3,64,128,128]{3,2,1,0:T(8,128)(2,1)} %tiles_ref.5, bf16[2048,384]{1,0:T(8,128)(2,1)} %copy-done.29), custom_call_target="tpu_custom_call" | custom-call | flops 9663676416 | bytes 11010048 | tf_op jit(solution)/shard_map/replaced_columns/pallas_call | solution.py:303
  29.6 4.2 %all-to-all-done.hist_ref = bf16[4,2048,128]{2,1,0:T(8,128)(2,1)} async-done(((bf16[4,2048,128]{2,1,0:T(8,128)(2,1)}), bf16[4,2048,128]{2,1,0:T(8,128)(2,1)}, u32[]{:S(2)}, u32[]{:S(2)}) %all-to-all-start) | async-done | bytes 2097184 | tf_op jit(solution)/shard_map/all_to_all | solution.py:584
  33.9 13.3 %first_partial.1 = (bf16[16,3,128,128]{3,2,1,0:T(8,128)(2,1)}, f32[3,2048,128]{2,1,0:T(8,128)}) custom-call(s32[3,256]{1,0:T(4,128)} %broadcast_add_fusion.slots_ref, bf16[3,64,128,128]{3,2,1,0:T(8,128)(2,1)} %tiles_ref.5, bf16[4,2048,128]{2,1,0:T(8,128)(2,1)} %all-to-all-done.hist_ref, bf16[2048,128]{1,0:T(8,128)(2,1)} %constant_dynamic-slice_fusion.4.feat_ref, ...), custom_call_target="tpu_custom_call" | custom-call | flops 6442450944 | bytes 6291456 | tf_op jit(solution)/shard_map/first_partial/pallas_call | solution.py:123
  47.2 8.4 %all-to-all-start.1 = ((bf16[16,3,128,128]{3,2,1,0:T(8,128)(2,1)}), bf16[16,3,128,128]{3,2,1,0:T(8,128)(2,1)}, u32[]{:S(2)}, u32[]{:S(2)}) async-start(bf16[16,3,128,128]{3,2,1,0:T(8,128)(2,1)} %get-tuple-element.40), calls=%async_computation.1 | async-start | bytes 3145728 | tf_op jit(solution)/shard_map/all_to_all | solution.py:622
  56.9 1.8 collective-permute-start.1
  59.3 14.0 %static_parts.1 = (f32[3,2048,128]{2,1,0:T(8,128)}, f32[3,2048,128]{2,1,0:T(8,128)}) custom-call(s32[3,256]{1,0:T(4,128)} %broadcast_add_fusion.slots_ref, bf16[3,64,128,128]{3,2,1,0:T(8,128)(2,1)} %tiles_ref.5, bf16[4,2048,128]{2,1,0:T(8,128)(2,1)} %all-to-all-done.hist_ref, bf16[3,2048,128]{2,1,0:T(8,128)(2,1)} %copy-done.28), custom_call_target="tpu_custom_call" | custom-call | flops 6442450944 | bytes 12582912 | tf_op jit(solution)/shard_map/static_parts/pallas_call | solution.py:358
  75.4 1.0 all-to-all-done.1.in_ref
  76.4 1.6 collect.4.sup_ref
  78.4 1.8 collective-permute-start.4
  80.2 1.3 collective-permute-start.5
  81.6 2.3 collective-permute-done.3
  84.5 7.3 %all-gather = bf16[8,384,128]{2,1,0:T(8,128)(2,1)S(1)} all-gather(bf16[4,384,128]{2,1,0:T(8,128)(2,1)S(1)} %pad_maximum_fusion), channel_id=2, replica_groups=mesh['section'=4,'vertex'=16,'feat'=2] {'feat'}, dimensions={0}, use_global_device_ids=true | all-gather | bytes 1179648 | tf_op jit(solution)/shard_map/all_gather | solution.py:631
  91.9 2.2 copy-done.13
  95.9 3.9 %layer_step.3 = bf16[16,3,128,128]{3,2,1,0:T(8,128)(2,1)S(1)} custom-call(s32[2]{0:T(128)S(1)} %pad_add_fusion.place_ref, bf16[2,4,384,128]{3,2,1,0:T(8,128)(2,1)S(1)} %bitcast.46, bf16[384,128]{1,0:T(8,128)(2,1)S(1)} %collect.4.sup_ref, f32[3,2048,128]{2,1,0:T(8,128)S(1)} %copy-done.13, bf16[1024,128]{1,0:T(8,128)(2,1)S(1)} %copy-done.12, ...), custom_call_target="tpu_custom_call" | custom-call | flops 704643072 | bytes 9437184 | tf_op jit(solution)/shard_map/layer_step/pallas_call | solution.py:467
  99.9 26.1 %all_to_all.25.in_ref = bf16[16,3,128,128]{3,2,1,0:T(8,128)(2,1)S(1)} all-to-all(bf16[16,3,128,128]{3,2,1,0:T(8,128)(2,1)S(1)} %layer_step.3), channel_id=1, replica_groups=mesh['section'=4,'vertex'=16,'feat'=2] {'vertex'}, dimensions={0} | all-to-all | bytes 3145728 | tf_op jit(solution)/shard_map/all_to_all | solution.py:622
  125.9 1.0 collect.5.sup_ref
  127.0 1.8 collective-permute-start.6
  128.8 2.8 %collective-permute-start.7 = (bf16[384,128]{1,0:T(8,128)(2,1)S(1)}, bf16[384,128]{1,0:T(8,128)(2,1)S(1)}, u32[]{:S(2)}, u32[]{:S(2)}) collective-permute-start(bf16[384,128]{1,0:T(8,128)(2,1)S(1)} %collect.5.sup_ref), channel_id=1, source_target_pairs={{0,64},{32,96},{64,0},{96,32},{1,65},{33,97},{65,1},{97,33},{2,66}... | collective-permute-start | bytes 294920 | tf_op jit(solution)/shard_map/ppermute | solution.py:22
  132.3 2.3 %collective-permute-done.7 = bf16[384,128]{1,0:T(8,128)(2,1)S(1)} collective-permute-done((bf16[384,128]{1,0:T(8,128)(2,1)S(1)}, bf16[384,128]{1,0:T(8,128)(2,1)S(1)}, u32[]{:S(2)}, u32[]{:S(2)}) %collective-permute-start.7) | collective-permute-done | bytes 98336 | tf_op jit(solution)/shard_map/ppermute | solution.py:22
  134.7 1.4 collective-permute-done.8
  136.1 4.4 %all-gather.1 = bf16[8,384,128]{2,1,0:T(8,128)(2,1)S(1)} all-gather(bf16[4,384,128]{2,1,0:T(8,128)(2,1)S(1)} %pad_maximum_fusion.1), channel_id=3, replica_groups=mesh['section'=4,'vertex'=16,'feat'=2] {'feat'}, dimensions={0}, use_global_device_ids=true | all-gather | bytes 1179648 | tf_op jit(solution)/shard_map/all_gather | solution.py:631
  140.5 3.9 %layer_step.4 = bf16[16,3,128,128]{3,2,1,0:T(8,128)(2,1)S(1)} custom-call(s32[2]{0:T(128)S(1)} %pad_add_fusion.place_ref, bf16[2,4,384,128]{3,2,1,0:T(8,128)(2,1)S(1)} %bitcast.48, bf16[384,128]{1,0:T(8,128)(2,1)S(1)} %collect.5.sup_ref, f32[3,2048,128]{2,1,0:T(8,128)S(1)} %copy-done.15, bf16[1024,128]{1,0:T(8,128)(2,1)S(1)} %copy-done.12, ...), custom_call_target="tpu_custom_call" | custom-call | flops 704643072 | bytes 9437184 | tf_op jit(solution)/shard_map/layer_step/pallas_call | solution.py:467
  144.5 25.0 %all_to_all.26.in_ref = bf16[16,3,128,128]{3,2,1,0:T(8,128)(2,1)S(1)} all-to-all(bf16[16,3,128,128]{3,2,1,0:T(8,128)(2,1)S(1)} %layer_step.4), channel_id=1, replica_groups=mesh['section'=4,'vertex'=16,'feat'=2] {'vertex'}, dimensions={0} | all-to-all | bytes 3145728 | tf_op jit(solution)/shard_map/all_to_all | solution.py:622
  169.4 1.0 collect.6.sup_ref
  170.5 3.1 %collective-permute-start.10 = (bf16[384,128]{1,0:T(8,128)(2,1)S(1)}, bf16[384,128]{1,0:T(8,128)(2,1)S(1)}, u32[]{:S(2)}, u32[]{:S(2)}) collective-permute-start(bf16[384,128]{1,0:T(8,128)(2,1)S(1)} %collect.6.sup_ref), channel_id=1, source_target_pairs={{0,64},{32,96},{64,0},{96,32},{1,65},{33,97},{65,1},{97,33},{2,66}... | collective-permute-start | bytes 294920 | tf_op jit(solution)/shard_map/ppermute | solution.py:22
  173.8 1.4 collective-permute-done.9
  175.2 1.6 collective-permute-done.10
  177.4 4.9 %all-gather.2 = bf16[8,384,128]{2,1,0:T(8,128)(2,1)S(1)} all-gather(bf16[4,384,128]{2,1,0:T(8,128)(2,1)S(1)} %pad_maximum_fusion.2), channel_id=4, replica_groups=mesh['section'=4,'vertex'=16,'feat'=2] {'feat'}, dimensions={0}, use_global_device_ids=true | all-gather | bytes 1179648 | tf_op jit(solution)/shard_map/all_gather | solution.py:631
  182.3 3.9 %layer_step.5 = bf16[16,3,128,128]{3,2,1,0:T(8,128)(2,1)S(1)} custom-call(s32[2]{0:T(128)S(1)} %pad_add_fusion.place_ref, bf16[2,4,384,128]{3,2,1,0:T(8,128)(2,1)S(1)} %bitcast.50, bf16[384,128]{1,0:T(8,128)(2,1)S(1)} %collect.6.sup_ref, f32[3,2048,128]{2,1,0:T(8,128)S(1)} %copy-done.14, bf16[1024,128]{1,0:T(8,128)(2,1)S(1)} %copy-done.12, ...), custom_call_target="tpu_custom_call" | custom-call | flops 704643072 | bytes 9437184 | tf_op jit(solution)/shard_map/layer_step/pallas_call | solution.py:467
  187.2 1.1 copy-done.10
  188.3 4.5 %all-to-all-start.4 = ((bf16[16,3,128,128]{3,2,1,0:T(8,128)(2,1)}), bf16[16,3,128,128]{3,2,1,0:T(8,128)(2,1)}, u32[]{:S(2)}, u32[]{:S(2)}) async-start(bf16[16,3,128,128]{3,2,1,0:T(8,128)(2,1)} %copy-done.10), calls=%async_computation.4 | async-start | bytes 3145728 | tf_op jit(solution)/shard_map/all_to_all | solution.py:622
  192.9 1.1 copy-done.5
  195.0 1.2 whole_rows.4.refs_0_
  199.0 10.1 %collective-permute-done.12.fresh_ref = bf16[384,512]{1,0:T(8,128)(2,1)S(1)} collective-permute-done((bf16[384,512]{1,0:T(8,128)(2,1)S(1)}, bf16[384,512]{1,0:T(8,128)(2,1)S(1)}, u32[]{:S(2)}, u32[]{:S(2)}) %collective-permute-start.12) | collective-permute-done | bytes 393248 | tf_op jit(solution)/shard_map/ppermute | solution.py:22
  209.8 4.7 %replace_rows.1 = bf16[2048,512]{1,0:T(8,128)(2,1)} custom-call(bf16[2048,512]{1,0:T(8,128)(2,1)} %bitcast.60, s32[1,384]{1,0:T(1,128)} %bitcast.58, bf16[384,512]{1,0:T(8,128)(2,1)} %copy-done.30), custom_call_target="tpu_custom_call" | custom-call | flops 805306368 | bytes 4194304 | tf_op jit(solution)/shard_map/replace_rows/pallas_call | solution.py:553
  214.5 3.5 %all-to-all-done.4.in_ref = bf16[16,3,128,128]{3,2,1,0:T(8,128)(2,1)} async-done(((bf16[16,3,128,128]{3,2,1,0:T(8,128)(2,1)}), bf16[16,3,128,128]{3,2,1,0:T(8,128)(2,1)}, u32[]{:S(2)}, u32[]{:S(2)}) %all-to-all-start.4) | async-done | bytes 1572896 | tf_op jit(solution)/shard_map/all_to_all | solution.py:622
  218.0 1.5 collect.7
  219.9 2.9 %collective-permute-start.14 = (bf16[384,128]{1,0:T(8,128)(2,1)S(1)}, bf16[384,128]{1,0:T(8,128)(2,1)S(1)}, u32[]{:S(2)}, u32[]{:S(2)}) collective-permute-start(bf16[384,128]{1,0:T(8,128)(2,1)S(1)} %collect.7), channel_id=1, source_target_pairs={{0,64},{32,96},{64,0},{96,32},{1,65},{33,97},{65,1},{97,33},{2,66}... | collective-permute-start | bytes 294920 | tf_op jit(solution)/shard_map/ppermute | solution.py:22
  222.9 1.4 collective-permute-done.13
  224.3 1.9 collective-permute-done.14
  227.1 4.1 %all-gather.3 = bf16[8,384,128]{2,1,0:T(8,128)(2,1)S(1)} all-gather(bf16[4,384,128]{2,1,0:T(8,128)(2,1)S(1)} %pad_maximum_fusion.3), channel_id=5, replica_groups=mesh['section'=4,'vertex'=16,'feat'=2] {'feat'}, dimensions={0}, use_global_device_ids=true | all-gather | bytes 1179648 | tf_op jit(solution)/shard_map/all_gather | solution.py:631
  231.2 1.3 whole_rows.7
  (101 shorter events, 17.5 us)
Async XLA Ops:
  0.6 11.1 %copy-start = (bf16[2048,512]{1,0:T(8,128)(2,1)S(1)}, bf16[2048,512]{1,0:T(8,128)(2,1)}, u32[]{:S(2)}) copy-start(bf16[2048,512]{1,0:T(8,128)(2,1)} %param.9) | copy-start | bytes 6291460
  3.2 4.9 %copy-start.31 = (s32[3,128]{1,0:T(4,128)S(1)}, s32[3,128]{1,0:T(4,128)}, u32[]{:S(2)}) copy-start(s32[3,128]{1,0:T(4,128)} %param.16) | copy-start | bytes 4612
  3.2 30.7 %all-to-all-start = ((bf16[4,2048,128]{2,1,0:T(8,128)(2,1)}), bf16[4,2048,128]{2,1,0:T(8,128)(2,1)}, u32[]{:S(2)}, u32[]{:S(2)}) async-start(bf16[4,2048,128]{2,1,0:T(8,128)(2,1)} %section_slices.1), calls=%async_computation | async-start | bytes 4194304 | tf_op jit(solution)/shard_map/all_to_all | solution.py:584
  8.1 5.8 %copy-start.27 = (s32[1,1,3,128]{3,1,2,0:T(1,128)}, s32[1,1,3,128]{3,1,2,0:T(1,128)S(1)}, u32[]{:S(2)}) copy-start(s32[1,1,3,128]{3,1,2,0:T(1,128)S(1)} %copy.15) | copy-start | bytes 4612
  9.4 1.1 copy-start.28
  10.5 1.2 copy-start.29
  11.7 2.3 copy-start.32
  11.7 2.3 copy-start.33
  11.7 2.3 copy-start.34
  13.9 15.7 %copy-start.22 = (bf16[384,512]{1,0:T(8,128)(2,1)}, bf16[384,512]{1,0:T(8,128)(2,1)S(1)}, u32[]{:S(2)}) copy-start(bf16[384,512]{1,0:T(8,128)(2,1)S(1)} %broadcast_select_fusion.refs_0_) | copy-start | bytes 1179652
  47.2 8.5 %copy-start.1 = (bf16[1,1024,512]{2,1,0:T(8,128)(2,1)S(1)}, bf16[1,1024,512]{2,1,0:T(8,128)(2,1)}, u32[]{:S(2)}) copy-start(bf16[1,1024,512]{2,1,0:T(8,128)(2,1)} %param.11) | copy-start | bytes 3145732
  47.2 29.2 %all-to-all-start.1 = ((bf16[16,3,128,128]{3,2,1,0:T(8,128)(2,1)}), bf16[16,3,128,128]{3,2,1,0:T(8,128)(2,1)}, u32[]{:S(2)}, u32[]{:S(2)}) async-start(bf16[16,3,128,128]{3,2,1,0:T(8,128)(2,1)} %get-tuple-element.40), calls=%async_computation.1 | async-start | bytes 3145728 | tf_op jit(solution)/shard_map/all_to_all | solution.py:622
  56.6 16.7 %collective-permute-start = (bf16[1024,128]{1,0:T(8,128)(2,1)S(1)}, bf16[1024,128]{1,0:T(8,128)(2,1)S(1)}, u32[]{:S(2)}, u32[]{:S(2)}) collective-permute-start(bf16[1024,128]{1,0:T(8,128)(2,1)S(1)} %get-tuple-element.62), channel_id=1, source_target_pairs={{0,32},{32,64},{64,96},{96,0},{1,33},{33,65},{65,97},{97,1},{2,34}... | collective-permute-start | bytes 786440 | tf_op jit(solution)/shard_map/ppermute | solution.py:22
  56.9 17.1 %collective-permute-start.1 = (bf16[1024,128]{1,0:T(8,128)(2,1)S(1)}, bf16[1024,128]{1,0:T(8,128)(2,1)S(1)}, u32[]{:S(2)}, u32[]{:S(2)}) collective-permute-start(bf16[1024,128]{1,0:T(8,128)(2,1)S(1)} %get-tuple-element.61), channel_id=1, source_target_pairs={{0,64},{32,96},{64,0},{96,32},{1,65},{33,97},{65,1},{97,33},{2,66}... | collective-permute-start | bytes 786440 | tf_op jit(solution)/shard_map/ppermute | solution.py:22
  58.6 16.0 %collective-permute-start.2 = (bf16[1024,128]{1,0:T(8,128)(2,1)S(1)}, bf16[1024,128]{1,0:T(8,128)(2,1)S(1)}, u32[]{:S(2)}, u32[]{:S(2)}) collective-permute-start(bf16[1024,128]{1,0:T(8,128)(2,1)S(1)} %get-tuple-element.60), channel_id=1, source_target_pairs={{0,96},{32,0},{64,32},{96,64},{1,97},{33,1},{65,33},{97,65},{2,98}... | collective-permute-start | bytes 786440 | tf_op jit(solution)/shard_map/ppermute | solution.py:22
  76.4 15.4 %copy-start.2 = (bf16[2048,384]{1,0:T(8,128)(2,1)S(1)}, bf16[2048,384]{1,0:T(8,128)(2,1)}, u32[]{:S(2)}) copy-start(bf16[2048,384]{1,0:T(8,128)(2,1)} %get-tuple-element.55.refs_6_) | copy-start | bytes 4718596
  76.4 15.4 %copy-start.3 = (bf16[2048,256]{1,0:T(8,128)(2,1)S(1)}, bf16[2048,256]{1,0:T(8,128)(2,1)}, u32[]{:S(2)}) copy-start(bf16[2048,256]{1,0:T(8,128)(2,1)} %get-tuple-element.54.refs_5_) | copy-start | bytes 3145732
  76.4 15.4 %copy-start.11 = (bf16[2048,128]{1,0:T(8,128)(2,1)S(1)}, bf16[2048,128]{1,0:T(8,128)(2,1)}, u32[]{:S(2)}) copy-start(bf16[2048,128]{1,0:T(8,128)(2,1)} %get-tuple-element.53.refs_4_) | copy-start | bytes 1572868
  76.4 15.4 %copy-start.12 = (bf16[1024,128]{1,0:T(8,128)(2,1)S(1)}, bf16[1024,128]{1,0:T(8,128)(2,1)}, u32[]{:S(2)}) copy-start(bf16[1024,128]{1,0:T(8,128)(2,1)} %get-tuple-element.49.refs_0_) | copy-start | bytes 786436
  76.4 15.4 %copy-start.17 = (bf16[1024,128]{1,0:T(8,128)(2,1)S(1)}, bf16[1024,128]{1,0:T(8,128)(2,1)}, u32[]{:S(2)}) copy-start(bf16[1024,128]{1,0:T(8,128)(2,1)} %copy-done.16) | copy-start | bytes 786436
  78.1 5.8 %collective-permute-start.3 = (bf16[384,128]{1,0:T(8,128)(2,1)S(1)}, bf16[384,128]{1,0:T(8,128)(2,1)S(1)}, u32[]{:S(2)}, u32[]{:S(2)}) collective-permute-start(bf16[384,128]{1,0:T(8,128)(2,1)S(1)} %collect.4.sup_ref), channel_id=1, source_target_pairs={{0,32},{32,64},{64,96},{96,0},{1,33},{33,65},{65,97},{97,1},{2,34}... | collective-permute-start | bytes 294920 | tf_op jit(solution)/shard_map/ppermute | solution.py:22
  78.4 5.5 %collective-permute-start.4 = (bf16[384,128]{1,0:T(8,128)(2,1)S(1)}, bf16[384,128]{1,0:T(8,128)(2,1)S(1)}, u32[]{:S(2)}, u32[]{:S(2)}) collective-permute-start(bf16[384,128]{1,0:T(8,128)(2,1)S(1)} %collect.4.sup_ref), channel_id=1, source_target_pairs={{0,64},{32,96},{64,0},{96,32},{1,65},{33,97},{65,1},{97,33},{2,66}... | collective-permute-start | bytes 294920 | tf_op jit(solution)/shard_map/ppermute | solution.py:22
  80.2 4.3 %collective-permute-start.5 = (bf16[384,128]{1,0:T(8,128)(2,1)S(1)}, bf16[384,128]{1,0:T(8,128)(2,1)S(1)}, u32[]{:S(2)}, u32[]{:S(2)}) collective-permute-start(bf16[384,128]{1,0:T(8,128)(2,1)S(1)} %collect.4.sup_ref), channel_id=1, source_target_pairs={{0,96},{32,0},{64,32},{96,64},{1,97},{33,1},{65,33},{97,65},{2,98}... | collective-permute-start | bytes 294920 | tf_op jit(solution)/shard_map/ppermute | solution.py:22
  91.8 8.0 %copy-start.4 = (bf16[8,384,128]{2,1,0:T(8,128)(2,1)}, bf16[8,384,128]{2,1,0:T(8,128)(2,1)S(1)}, u32[]{:S(2)}) copy-start(bf16[8,384,128]{2,1,0:T(8,128)(2,1)S(1)} %all-gather) | copy-start | bytes 2359300
  91.9 2.2 copy-start.13
  94.0 0.9 copy-start.19
  95.0 0.9 copy-start.21
  125.9 14.6 %copy-start.15 = (f32[3,2048,128]{2,1,0:T(8,128)S(1)}, f32[3,2048,128]{2,1,0:T(8,128)}, u32[]{:S(2)}) copy-start(f32[3,2048,128]{2,1,0:T(8,128)} %get-tuple-element.56.static_ref) | copy-start | bytes 9437188
  127.0 5.4 %collective-permute-start.6 = (bf16[384,128]{1,0:T(8,128)(2,1)S(1)}, bf16[384,128]{1,0:T(8,128)(2,1)S(1)}, u32[]{:S(2)}, u32[]{:S(2)}) collective-permute-start(bf16[384,128]{1,0:T(8,128)(2,1)S(1)} %collect.5.sup_ref), channel_id=1, source_target_pairs={{0,32},{32,64},{64,96},{96,0},{1,33},{33,65},{65,97},{97,1},{2,34}... | collective-permute-start | bytes 294920 | tf_op jit(solution)/shard_map/ppermute | solution.py:22
  128.8 5.9 %collective-permute-start.7 = (bf16[384,128]{1,0:T(8,128)(2,1)S(1)}, bf16[384,128]{1,0:T(8,128)(2,1)S(1)}, u32[]{:S(2)}, u32[]{:S(2)}) collective-permute-start(bf16[384,128]{1,0:T(8,128)(2,1)S(1)} %collect.5.sup_ref), channel_id=1, source_target_pairs={{0,64},{32,96},{64,0},{96,32},{1,65},{33,97},{65,1},{97,33},{2,66}... | collective-permute-start | bytes 294920 | tf_op jit(solution)/shard_map/ppermute | solution.py:22
  131.5 4.5 %collective-permute-start.8 = (bf16[384,128]{1,0:T(8,128)(2,1)S(1)}, bf16[384,128]{1,0:T(8,128)(2,1)S(1)}, u32[]{:S(2)}, u32[]{:S(2)}) collective-permute-start(bf16[384,128]{1,0:T(8,128)(2,1)S(1)} %collect.5.sup_ref), channel_id=1, source_target_pairs={{0,96},{32,0},{64,32},{96,64},{1,97},{33,1},{65,33},{97,65},{2,98}... | collective-permute-start | bytes 294920 | tf_op jit(solution)/shard_map/ppermute | solution.py:22
  140.5 3.9 %copy-start.6 = (bf16[8,384,128]{2,1,0:T(8,128)(2,1)}, bf16[8,384,128]{2,1,0:T(8,128)(2,1)S(1)}, u32[]{:S(2)}) copy-start(bf16[8,384,128]{2,1,0:T(8,128)(2,1)S(1)} %all-gather.1) | copy-start | bytes 2359300
  169.4 12.9 %copy-start.14 = (f32[3,2048,128]{2,1,0:T(8,128)S(1)}, f32[3,2048,128]{2,1,0:T(8,128)}, u32[]{:S(2)}) copy-start(f32[3,2048,128]{2,1,0:T(8,128)} %get-tuple-element.57.static_ref) | copy-start | bytes 9437188
  170.5 4.7 %collective-permute-start.9 = (bf16[384,128]{1,0:T(8,128)(2,1)S(1)}, bf16[384,128]{1,0:T(8,128)(2,1)S(1)}, u32[]{:S(2)}, u32[]{:S(2)}) collective-permute-start(bf16[384,128]{1,0:T(8,128)(2,1)S(1)} %collect.6.sup_ref), channel_id=1, source_target_pairs={{0,32},{32,64},{64,96},{96,0},{1,33},{33,65},{65,97},{97,1},{2,34}... | collective-permute-start | bytes 294920 | tf_op jit(solution)/shard_map/ppermute | solution.py:22
  170.5 6.2 %collective-permute-start.10 = (bf16[384,128]{1,0:T(8,128)(2,1)S(1)}, bf16[384,128]{1,0:T(8,128)(2,1)S(1)}, u32[]{:S(2)}, u32[]{:S(2)}) collective-permute-start(bf16[384,128]{1,0:T(8,128)(2,1)S(1)} %collect.6.sup_ref), channel_id=1, source_target_pairs={{0,64},{32,96},{64,0},{96,32},{1,65},{33,97},{65,1},{97,33},{2,66}... | collective-permute-start | bytes 294920 | tf_op jit(solution)/shard_map/ppermute | solution.py:22
  173.6 3.8 %collective-permute-start.11 = (bf16[384,128]{1,0:T(8,128)(2,1)S(1)}, bf16[384,128]{1,0:T(8,128)(2,1)S(1)}, u32[]{:S(2)}, u32[]{:S(2)}) collective-permute-start(bf16[384,128]{1,0:T(8,128)(2,1)S(1)} %collect.6.sup_ref), channel_id=1, source_target_pairs={{0,96},{32,0},{64,32},{96,64},{1,97},{33,1},{65,33},{97,65},{2,98}... | collective-permute-start | bytes 294920 | tf_op jit(solution)/shard_map/ppermute | solution.py:22
  187.2 1.1 copy-start.10
  188.3 4.6 %copy-start.26 = (f32[4]{0:T(128)S(1)}, f32[4]{0:T(128)}, u32[]{:S(2)}) copy-start(f32[4]{0:T(128)} %constant.71.clone.betas_ref) | copy-start | bytes 52
  188.3 29.7 %all-to-all-start.4 = ((bf16[16,3,128,128]{3,2,1,0:T(8,128)(2,1)}), bf16[16,3,128,128]{3,2,1,0:T(8,128)(2,1)}, u32[]{:S(2)}, u32[]{:S(2)}) async-start(bf16[16,3,128,128]{3,2,1,0:T(8,128)(2,1)} %copy-done.10), calls=%async_computation.4 | async-start | bytes 3145728 | tf_op jit(solution)/shard_map/all_to_all | solution.py:622
  192.9 1.1 copy-start.5
  194.0 1.0 copy-start.23
  195.0 1.2 copy-start.7
  195.0 1.8 copy-start.9
  197.4 11.7 %collective-permute-start.12 = (bf16[384,512]{1,0:T(8,128)(2,1)S(1)}, bf16[384,512]{1,0:T(8,128)(2,1)S(1)}, u32[]{:S(2)}, u32[]{:S(2)}) collective-permute-start(bf16[384,512]{1,0:T(8,128)(2,1)S(1)} %whole_rows.6.refs_0_), channel_id=1, source_target_pairs={{0,32},{32,64},{64,96},{96,0},{1,33},{33,65},{65,97},{97,1},{2,34}... | collective-permute-start | bytes 1179656 | tf_op jit(solution)/shard_map/ppermute | solution.py:22
  218.0 13.2 %copy-start.25 = (bf16[384,512]{1,0:T(8,128)(2,1)S(1)}, bf16[384,512]{1,0:T(8,128)(2,1)}, u32[]{:S(2)}) copy-start(bf16[384,512]{1,0:T(8,128)(2,1)} %copy-done.24) | copy-start | bytes 1179652
  219.5 4.7 %collective-permute-start.13 = (bf16[384,128]{1,0:T(8,128)(2,1)S(1)}, bf16[384,128]{1,0:T(8,128)(2,1)S(1)}, u32[]{:S(2)}, u32[]{:S(2)}) collective-permute-start(bf16[384,128]{1,0:T(8,128)(2,1)S(1)} %collect.7), channel_id=1, source_target_pairs={{0,32},{32,64},{64,96},{96,0},{1,33},{33,65},{65,97},{97,1},{2,34}... | collective-permute-start | bytes 294920 | tf_op jit(solution)/shard_map/ppermute | solution.py:22
  219.9 6.3 %collective-permute-start.14 = (bf16[384,128]{1,0:T(8,128)(2,1)S(1)}, bf16[384,128]{1,0:T(8,128)(2,1)S(1)}, u32[]{:S(2)}, u32[]{:S(2)}) collective-permute-start(bf16[384,128]{1,0:T(8,128)(2,1)S(1)} %collect.7), channel_id=1, source_target_pairs={{0,64},{32,96},{64,0},{96,32},{1,65},{33,97},{65,1},{97,33},{2,66}... | collective-permute-start | bytes 294920 | tf_op jit(solution)/shard_map/ppermute | solution.py:22
  222.8 4.3 %collective-permute-start.15 = (bf16[384,128]{1,0:T(8,128)(2,1)S(1)}, bf16[384,128]{1,0:T(8,128)(2,1)S(1)}, u32[]{:S(2)}, u32[]{:S(2)}) collective-permute-start(bf16[384,128]{1,0:T(8,128)(2,1)S(1)} %collect.7), channel_id=1, source_target_pairs={{0,96},{32,0},{64,32},{96,64},{1,97},{33,1},{65,33},{97,65},{2,98}... | collective-permute-start | bytes 294920 | tf_op jit(solution)/shard_map/ppermute | solution.py:22
  (6 other events, 4.5 us)
